TPU v7x, 32 devices: a whole 2x2x4 slice. The times are simulated.
32 devices in a mesh: grp: 2 (over y), section: 2 (over core), seq: 4 (over z), fsdp: 2 (over x).
Axes of the slice: x: 2, y: 2, z: 4, core: 2. Of those that a mesh axis runs over, the one named last changes fastest.
Arguments:
- head_inputs: bfloat16 [2, 4, 256, 7680], P('section', ('grp', 'fsdp'), 'seq'), parts along dimension 1, may hold values from -8 to 8
- hidden: bfloat16 [2, 4, 256, 2560], P('section', ('grp', 'fsdp'), 'seq'), parts along dimension 1, may hold values from -3 to 3
- out_weight: bfloat16 [2, 2560, 2560], P('section', 'fsdp'), may hold values from -0.125 to 0.125
- time_weight: bfloat16 [2, 256, 7680], P('section', None, ('seq', 'fsdp')), may hold values from -0.375 to 0.375
- head_weight: bfloat16 [2, 2560, 64], P('section', ('seq', 'fsdp')), may hold values from -0.125 to 0.125
- latent: float32 [2, 4, 128, 128], P('section', ('grp', 'fsdp'), 'seq'), parts along dimension 1, may hold values from -6 to 6
- timesteps: int32 [2, 4, 2], P('section', ('grp', 'fsdp')), parts along dimension 1, may hold values from 41 to 999, as said below
Outputs:
- velocity: float32 [2, 4, 128, 128], P('section', ('grp', 'fsdp'), 'seq'), parts along dimension 1
- carried: float32 [2, 4, 128, 128], P('section', ('grp', 'fsdp'), 'seq'), parts along dimension 1
There are 2 independent parts, one for each index of `grp`. A program takes and returns all parts, laid end to end along the dimension named above; an argument that names none is the same for every part. Nothing has to cross between parts.
Inputs may be any that keep to these rules, and one draw needn't show every extreme that they name: timesteps[0] lie in 875 to 999 and timesteps[1] in 100 to 874 for the current entry; the next entry is the current one minus 10 to 59.
All inputs are finite; a program needn't handle non-finite values.
Results may differ from a plain program's by a relative error of at most 0.0049.
Values may be sent and summed in bfloat16 or wider, within the bound.
No kernel may reach another device: no remote copies, remote signals or barrier semaphores. Data moves between devices by JAX's collectives and lax.ppermute only.
A program may use at most 128 MiB of HBM per device.

v0:
```python
import math

import jax
import jax.numpy as jnp
from jax import lax
from jax.sharding import PartitionSpec as P

DIM = 2560
HEADS = 32
HEAD = 80
PATCH = 64
FREQ = 256


def partner(block, axis, apart):
    count = lax.axis_size(axis)
    route = []
    for low in range(count):
        high = low | 1 << apart
        if high != low and high < count:
            route += [(low, high), (high, low)]
    return lax.ppermute(block, axis, route)


def time_embed(steps_now):
    half = FREQ // 2
    freqs = jnp.exp(-math.log(10000.0) * jnp.arange(half, dtype=jnp.float32) / half)
    angle = steps_now.astype(jnp.float32)[..., None] * freqs
    return jnp.concatenate([jnp.cos(angle), jnp.sin(angle)], axis=-1)


def sigma_of(steps_now):
    unit_time = steps_now.astype(jnp.float32) / 1000.0
    return 5.0 * unit_time / (1.0 + 4.0 * unit_time)


def attend(exchanged):
    items = exchanged.shape[0]
    length = exchanged.shape[1]
    local_heads = exchanged.shape[2]
    query_all = exchanged[..., :HEAD]
    key_rows = exchanged[..., HEAD : 2 * HEAD]
    value_rows = exchanged[..., 2 * HEAD :]
    block_rows = min(512, length)
    block_count = length // block_rows

    def one_block(block_index):
        query_block = lax.dynamic_slice_in_dim(query_all, block_index * block_rows, block_rows, 1)
        scores = jnp.einsum(
            "nqhe,nkhe->nhqk", query_block, key_rows, preferred_element_type=jnp.float32
        ) * HEAD ** (-0.5)
        row_max = jnp.max(scores, axis=-1, keepdims=True)
        exp_scores = jnp.exp(scores - row_max)
        row_sum = jnp.sum(exp_scores, axis=-1, keepdims=True)
        weights = (exp_scores / row_sum).astype(jnp.bfloat16)
        return jnp.einsum(
            "nhqk,nkhe->nqhe", weights, value_rows, preferred_element_type=jnp.float32
        ).astype(jnp.bfloat16)

    blocks = lax.map(one_block, jnp.arange(block_count, dtype=jnp.int32))
    return blocks.transpose(1, 0, 2, 3, 4).reshape(items, length, local_heads * HEAD)


def body(head_inputs, hidden, out_weight, time_weight, head_weight, latent, timesteps):
    samples = head_inputs.shape[1]
    row_count = head_inputs.shape[2]
    flat_count = samples * row_count
    local = head_inputs.reshape(samples, row_count, HEADS, 3 * HEAD)
    attended = lax.all_to_all(
        attend(lax.all_to_all(local, "seq", split_axis=2, concat_axis=1, tiled=True)),
        "seq",
        split_axis=1,
        concat_axis=2,
        tiled=True,
    )
    flattened = attended.reshape(flat_count, HEADS * HEAD)
    time_full, head_full = (
        lax.all_gather(time_weight, ("seq", "fsdp"), axis=2, tiled=True),
        lax.all_gather(head_weight, ("seq", "fsdp"), axis=1, tiled=True),
    )
    embedding = time_embed(timesteps[0, :, 0]).astype(jnp.bfloat16)
    modulation = jnp.dot(embedding, time_full[0], preferred_element_type=jnp.float32)
    gate_term = modulation[:, None, :DIM]
    shift_term = modulation[:, None, DIM : 2 * DIM]
    scale_term = modulation[:, None, 2 * DIM :]
    own_columns = lax.all_to_all(flattened, "fsdp", split_axis=1, concat_axis=0, tiled=True)
    projected = lax.psum_scatter(
        jnp.dot(own_columns, out_weight[0], preferred_element_type=jnp.float32).astype(
            jnp.bfloat16
        ),
        "fsdp",
        scatter_dimension=0,
        tiled=True,
    ).astype(jnp.float32)
    updated = hidden.reshape(samples, row_count, DIM).astype(
        jnp.float32
    ) + gate_term * projected.reshape(samples, row_count, DIM)
    average = jnp.mean(updated, axis=-1, keepdims=True)
    centred = updated - average
    variance = jnp.mean(centred * centred, axis=-1, keepdims=True)
    normed = (centred * lax.rsqrt(variance + 1e-06) * (1.0 + scale_term) + shift_term).astype(
        jnp.bfloat16
    )
    velocity = jnp.dot(
        normed.reshape(flat_count, DIM), head_full[0], preferred_element_type=jnp.float32
    )
    velocity = velocity.reshape(1, samples, row_count // 2, 2 * PATCH)
    step_size = sigma_of(timesteps[0, :, 1]) - sigma_of(timesteps[0, :, 0])
    stepped = latent + step_size[None, :, None, None] * velocity
    carried = partner(stepped, "section", 0)
    return (velocity, carried)


def solution(mesh):
    return jax.shard_map(
        body,
        mesh=mesh,
        in_specs=(
            P("section", ("grp", "fsdp"), "seq", None),
            P("section", ("grp", "fsdp"), "seq", None),
            P("section", "fsdp", None),
            P("section", None, ("seq", "fsdp")),
            P("section", ("seq", "fsdp"), None),
            P("section", ("grp", "fsdp"), "seq", None),
            P("section", ("grp", "fsdp"), None),
        ),
        out_specs=(
            P("section", ("grp", "fsdp"), "seq", None),
            P("section", ("grp", "fsdp"), "seq", None),
        ),
        check_vma=False,
    )
```

profile of v0, /device:TPU:0, one launch (start us, length us, event | category | flops | bytes accessed | tf_op | source)
XLA Modules:
  0.0 163.8 jit_solution(13938546322388415020)
XLA Ops:
  8.0 0.7 all-gather.2.cloned.1.call-update
  8.8 3.5 %reshape.152 = bf16[1,64,32,240]{3,2,1,0:T(8,128)(2,1)S(1)} reshape(bf16[1,1,64,7680]{3,2,1,0:T(8,128)(2,1)} %param.7) | data formatting | bytes 1966080 | tf_op jit(solution)/shard_map/reshape | solution.py:68
  12.3 0.6 copy.28
  12.9 47.7 %all_to_all.52 = bf16[1,64,32,240]{3,1,0,2:T(8,128)(2,1)S(1)} all-to-all(bf16[1,64,32,240]{3,1,0,2:T(8,128)(2,1)S(1)} %copy.28), channel_id=1, replica_groups=mesh['grp'=2,'section'=2,'seq'=4,'fsdp'=2] {'seq'}, dimensions={2} | all-to-all | bytes 1966080 | tf_op jit(solution)/shard_map/all_to_all | solution.py:70
  60.6 0.6 copy.46
  61.2 0.4 fusion.35
  61.7 0.3 copy.42
  62.0 0.3 copy.43
  62.3 0.3 copy.44
  62.7 2.2 %fusion.37 = (f32[8,256]{1,0:T(8,128)S(1)}, f32[8,256,256]{1,2,0:T(8,128)}) fusion(bf16[1,256,8,80]{1,3,2,0:T(8,128)(2,1)S(1)} %copy.44, bf16[1,256,8,80]{1,3,2,0:T(8,128)(2,1)S(1)} %copy.43), kind=kOutput, calls=%fused_computation.41 | convolution fusion | flops 85459200 | bytes 2760704 | tf_op jit(solution)/shard_map/while/body/eval_jaxpr/sub | solution.py:53
  64.8 1.9 %convolution_convert_fusion = bf16[8,256,80]{1,2,0:T(8,128)(2,1)S(1)} fusion(f32[8,256,256]{1,2,0:T(8,128)} %get-tuple-element.26, f32[8,256]{1,0:T(8,128)S(1)} %get-tuple-element.25, bf16[1,256,8,80]{1,3,2,0:T(8,128)(2,1)S(1)} %copy.42), kind=kOutput, calls=%fused_computation.10 | convolution fusion | flops 85098496 | bytes 2760704 | tf_op jit(solution)/shard_map/while/body/eval_jaxpr/nhqk,nkhe->nqhe/dot_general | solution.py:56
  66.7 0.6 copy.35
  67.3 0.5 broadcast.88
  67.9 2.6 %reduce.14 = bf16[256,640]{1,0:T(8,128)(2,1)S(1)} reduce(bf16[256,1,640]{2,1,0:T(2,128)(2,1)S(1)} %bitcast.71, bf16[]{:T(256)} %broadcast.88), dimensions={1}, to_apply=%bitcast.60.reduce_sub_computation | reduce | bytes 655362
  70.5 0.1 reshape.166
  70.6 22.7 %all_to_all.53 = bf16[4,2,20480]{2,1,0:T(2,128)(2,1)S(1)} all-to-all(bf16[4,2,20480]{2,1,0:T(2,128)(2,1)S(1)} %reshape.166), channel_id=1, replica_groups=mesh['grp'=2,'section'=2,'seq'=4,'fsdp'=2] {'seq'}, dimensions={0} | all-to-all | bytes 655360 | tf_op jit(solution)/shard_map/all_to_all | solution.py:69
  93.2 0.3 reshape.167
  93.6 0.3 copy.36
  93.9 0.2 all_to_all.45
  94.1 8.1 %all_to_all.54 = bf16[64,2,1280]{2,0,1:T(8,128)(2,1)S(1)} all-to-all(bf16[64,2,1280]{2,0,1:T(8,128)(2,1)S(1)} %copy.37), channel_id=1, replica_groups=mesh['grp'=2,'section'=2,'seq'=4,'fsdp'=2] {'fsdp'}, dimensions={1} | all-to-all | bytes 655360 | tf_op jit(solution)/shard_map/all_to_all | solution.py:86
  102.2 4.7 %fusion.5 = bf16[128,2560]{1,0:T(8,128)(2,1)} fusion(bf16[128,1280]{1,0:T(8,128)(2,1)S(1)} %bitcast.73, bf16[1,1280,2560]{2,1,0:T(8,128)(2,1)} %param.9), kind=kOutput, calls=%fused_computation.5 | convolution fusion | flops 839188480 | bytes 7536640 | tf_op jit(solution)/shard_map/dot_general | solution.py:88
  107.0 0.6 fusion.36
  108.9 0.2 copy.38
  109.1 37.3 %all_gather.7 = bf16[1,2560,64]{2,0,1:T(2,128)(2,1)S(1)} all-gather(bf16[1,320,64]{2,0,1:T(2,128)(2,1)S(1)} %copy.38), channel_id=1, replica_groups=mesh['grp'=2,'section'=2,'seq'=4,'fsdp'=2] {'seq','fsdp'}, dimensions={1}, use_global_device_ids=true | all-gather | bytes 368640 | tf_op jit(solution)/shard_map/all_gather | solution.py:79
  146.4 0.8 copy.39
  147.3 3.2 %fusion.3 = f32[1,7680]{1,0:T(1,128)S(1)} fusion(bf16[256,1]{0,1:T(2,128)(2,1)S(1)} %reshape.160, bf16[1,256,7680]{1,2,0:T(8,128)(2,1)} %all-gather.2.cloned.1.call-done), kind=kOutput, calls=%fused_computation.3 | convolution fusion | flops 3932160 | bytes 3963392 | tf_op jit(solution)/shard_map/dot_general | solution.py:82
  150.5 0.1 slice_reduce_fusion.1
  150.6 1.2 fusion.10
  151.8 1.2 multiply_reduce_fusion.1
  153.1 1.3 fusion.11
  154.6 1.2 collective-permute-done
  155.7 0.6 copy.48
  (26 shorter events, 0.5 us)
Async XLA Ops:
  8.0 139.3 %all-gather.2.cloned.1.call-start = ((), (), s32[]{:S(2)}) async-start(), calls=%async_computation.4 | async-start | bytes 4423680 | tf_op jit(solution)/shard_map/all_gather | solution.py:78
  8.7 141.9 %reduce-scatter.2.cloned.1.call-start = ((), (), s32[]{:S(2)}) async-start(), calls=%async_computation.5 | async-start | bytes 983040 | tf_op jit(solution)/shard_map/reduce_scatter | solution.py:87
  102.2 4.8 %copy-start.4 = (s32[1,1,2]{2,1,0:T(1,128)S(1)}, s32[1,1,2]{2,1,0:T(1,128)}, u32[]{:S(2)}) copy-start(s32[1,1,2]{2,1,0:T(1,128)} %param.13) | copy-start | bytes 28
  102.2 6.7 %copy-start.2 = (bf16[1,320,64]{1,2,0:T(8,128)(2,1)S(1)}, bf16[1,320,64]{1,2,0:T(8,128)(2,1)}, u32[]{:S(2)}) copy-start(bf16[1,320,64]{1,2,0:T(8,128)(2,1)} %param.11) | copy-start | bytes 122884
  147.1 3.5 %copy-start = (bf16[1,1,64,2560]{3,2,1,0:T(8,128)(2,1)S(1)}, bf16[1,1,64,2560]{3,2,1,0:T(8,128)(2,1)}, u32[]{:S(2)}) copy-start(bf16[1,1,64,2560]{3,2,1,0:T(8,128)(2,1)} %param.8) | copy-start | bytes 983044
  150.5 4.0 %copy-start.3 = (f32[1,1,32,128]{3,2,1,0:T(8,128)S(1)}, f32[1,1,32,128]{3,2,1,0:T(8,128)}, u32[]{:S(2)}) copy-start(f32[1,1,32,128]{3,2,1,0:T(8,128)} %param.12) | copy-start | bytes 49156
  154.5 1.9 %copy-start.1 = (f32[1,1,32,128]{3,2,1,0:T(8,128)}, f32[1,1,32,128]{3,2,1,0:T(8,128)S(1)}, u32[]{:S(2)}) copy-start(f32[1,1,32,128]{3,2,1,0:T(8,128)S(1)} %reshape.156) | copy-start | bytes 49156
  154.5 1.2 collective-permute-start
Sparse Core Ops, SparseCore 0:
  11.0 94.3 all-gather.1
Sparse Core Ops, SparseCore 1:
  107.0 29.8 reduce-scatter.1
where the time goes:
time: 164 us
  blocking collectives  116 us (71%)
  between operations  17.1 us (10%)
  matrix products  13.4 us (8%)
  local copies, waits for them, and re-layouts  10.4 us (6%)
  other arithmetic  5.18 us (3%)
  waiting for transfers between devices  1.92 us (1%)
    all_to_all x1, blocking collectives, body(): lax.all_to_all(local, 'seq', split_axis=2, concat_axis=1, tiled=True)  47.7 us
    all_gather x1, blocking collectives, body(): lax.all_gather(head_weight, ('seq', 'fsdp'), axis=1, tiled=True)  37.3 us
    all_to_all x1, blocking collectives, body(): lax.all_to_all(attend(lax.all_to_all(local, 'seq', split_axis=2, concat_a...  22.7 us
    all_to_all x1, blocking collectives, body(): lax.all_to_all(flattened, 'fsdp', split_axis=1, concat_axis=0, tiled=True)  8.07 us
    dot_general x1, matrix products, body(): jnp.dot(own_columns, out_weight[0], preferred_element_type=jnp.float32)  4.74 us
    reshape x2, local copies, waits for them, and re-layouts, body(): local = head_inputs.reshape(samples, row_count, HEADS, 3 * HEAD)  4.12 us
  transfers between devices with their start and end apart: 3, of which 1 were waited for; matrix products, arithmetic and copies ran while one was open for 15% of the time, Pallas kernels for 0%

commit v1 on v0

--- a/solution.py
+++ b/solution.py
@@ -1,15 +1,20 @@
+import functools
 import math
 
 import jax
 import jax.numpy as jnp
 from jax import lax
+from jax.experimental import pallas as pl
+from jax.experimental.pallas import tpu as pltpu
 from jax.sharding import PartitionSpec as P
+
 
 DIM = 2560
 HEADS = 32
 HEAD = 80
 PATCH = 64
 FREQ = 256
+LANES = 128
 
 
 def partner(block, axis, apart):
@@ -61,7 +66,7 @@
     return blocks.transpose(1, 0, 2, 3, 4).reshape(items, length, local_heads * HEAD)
 
 
-def body(head_inputs, hidden, out_weight, time_weight, head_weight, latent, timesteps):
+def general_body(head_inputs, hidden, out_weight, time_weight, head_weight, latent, timesteps):
     samples = head_inputs.shape[1]
     row_count = head_inputs.shape[2]
     flat_count = samples * row_count
@@ -111,7 +116,546 @@
     return (velocity, carried)
 
 
-def solution(mesh):
+def turn(half):
+    return pltpu.roll(half.astype(jnp.float32), LANES // 2, 1)
+
+
+def pack_half(tile):
+    rows = tile.shape[0]
+    wide = tile.astype(jnp.float32)
+    lane = lax.broadcasted_iota(jnp.int32, (rows // 2, LANES), 1)
+    return jnp.where(
+        lane < LANES // 2, wide[: rows // 2], pltpu.roll(wide[rows // 2 :], LANES // 2, 1)
+    ).astype(jnp.bfloat16)
+
+
+def unpack_tiles(ref, rows, width):
+    whole = width // LANES
+    tiles = [ref[t * rows : (t + 1) * rows, :] for t in range(whole)]
+    last = ref[whole * rows : whole * rows + rows // 2, :]
+    tiles.append(jnp.concatenate([last, turn(last).astype(jnp.bfloat16)], axis=0))
+    return tiles
+
+
+def head_tiles(width):
+    return -(-width // LANES)
+
+
+MOD_ROWS = 32
+
+
+def put_head(out, at, head_ref, group_ref):
+    patch, width = head_ref.shape
+    cut = patch // 2
+    mine = pl.ds(pl.multiple_of(group_ref[0] * cut, cut), cut)
+    for t in range(head_tiles(width)):
+        lanes = min(LANES, width - t * LANES)
+        out[at + t * cut : at + (t + 1) * cut, :lanes] = head_ref[
+            mine, t * LANES : t * LANES + lanes
+        ]
+
+
+def put_modulation(out, at, row):
+    width = row.shape[1]
+    tiles = -(-width // LANES)
+    left = jnp.concatenate([row, jnp.zeros((1, tiles * LANES - width), jnp.float32)], axis=1)
+    left = jnp.concatenate(
+        [left[:, t * LANES : (t + 1) * LANES] for t in range(tiles)]
+        + [jnp.zeros((8 - tiles, LANES), jnp.float32)][: 8 - tiles],
+        axis=0,
+    )
+    terms = []
+    for _ in range(3):
+        term = left.astype(jnp.bfloat16).astype(jnp.float32)
+        terms.append(term)
+        left = left - term
+    terms.append(jnp.zeros_like(left))
+    out[at : at + MOD_ROWS, :] = jnp.concatenate(terms, axis=0).astype(jnp.bfloat16)
+
+
+def get_modulation(ref, at, width):
+    terms = ref[at : at + MOD_ROWS, :].astype(jnp.float32)
+    total = terms[0:8] + terms[8:16] + terms[16:24]
+    tiles = -(-width // LANES)
+    return jnp.concatenate([total[t : t + 1] for t in range(tiles)], axis=1)[:, :width]
+
+
+def near_extra(count):
+    return [(r not in (0, count // 2), r != 0) for r in range(count)]
+
+
+def far_extra(count):
+    return [(r == count // 2, False) for r in range(count)]
+
+
+def split_kernel(width, flip, extra, place_ref, half_ref, group_ref, x_ref, *refs):
+    count = len(extra)
+    head_ref, refs = refs[0], refs[1:]
+    if not flip:
+        mod_ref, refs = refs[0], refs[1:]
+    outs, held, sems = refs[:count], refs[count], refs[count + 1]
+    rows = x_ref.shape[0]
+    whole = width // LANES
+    me = place_ref[0]
+    half = 1 - half_ref[0] if flip else half_ref[0]
+    base = half * (count * width)
+
+    def window(r):
+        to = me ^ r
+        start = pl.multiple_of(base + lax.div(to * width, LANES) * LANES, LANES)
+        return pltpu.make_async_copy(
+            x_ref.at[:, pl.ds(start, (whole + 1) * LANES)], held.at[r], sems.at[r]
+        )
+
+    order = [r for r in range(count) if r != 0] + [0]
+    for r in order:
+        window(r).start()
+    packed = rows * width // LANES
+    for r in order:
+        at = packed
+        if extra[r][0]:
+            put_head(outs[r], at, head_ref, group_ref)
+            at += head_ref.shape[0] // 2 * head_tiles(head_ref.shape[1])
+        if extra[r][1]:
+            put_modulation(outs[r], at, mod_ref[0:1, :])
+    for r in order:
+        window(r).wait()
+        odd = lax.rem(me ^ r, 2) == 1
+        last = slice(whole * rows, packed)
+
+        @pl.when(jnp.logical_not(odd))
+        def _():
+            for t in range(whole):
+                outs[r][t * rows : (t + 1) * rows, :] = held[r, :, t * LANES : (t + 1) * LANES]
+            outs[r][last, :] = pack_half(held[r, :, whole * LANES :])
+
+        @pl.when(odd)
+        def _():
+            lane = lax.broadcasted_iota(jnp.int32, (rows, LANES), 1)
+            turned = [turn(held[r, :, t * LANES : (t + 1) * LANES]) for t in range(whole + 1)]
+            for t in range(whole):
+                outs[r][t * rows : (t + 1) * rows, :] = jnp.where(
+                    lane < LANES // 2, turned[t], turned[t + 1]
+                ).astype(jnp.bfloat16)
+            outs[r][last, :] = pack_half(turned[whole])
+
+
+def split_heads(x, flip, extra, scalars, riders, halves):
+    rows, columns = x.shape
+    count = len(extra)
+    width = columns // halves // count
+    head = riders[0]
+    pieces = []
+    for with_head, with_mod in extra:
+        length = rows * width // LANES
+        length += head.shape[0] // 2 * head_tiles(head.shape[1]) * with_head
+        length += MOD_ROWS * with_mod
+        pieces.append(jax.ShapeDtypeStruct((length, LANES), jnp.bfloat16))
+    return pl.pallas_call(
+        functools.partial(split_kernel, width, flip, extra),
+        in_specs=[pl.BlockSpec(memory_space=pltpu.SMEM)] * 3
+        + [pl.BlockSpec(memory_space=pltpu.HBM)]
+        + [pl.BlockSpec(memory_space=pltpu.VMEM)] * len(riders),
+        out_shape=pieces,
+        scratch_shapes=[
+            pltpu.VMEM((count, rows, (width // LANES + 1) * LANES), jnp.bfloat16),
+            pltpu.SemaphoreType.DMA((count,)),
+        ],
+        compiler_params=pltpu.CompilerParams(vmem_limit_bytes=4 << 20),
+        cost_estimate=pl.CostEstimate(
+            flops=0, transcendentals=0, bytes_accessed=4 * rows * columns // halves
+        ),
+        name="split_heads",
+    )(*scalars, pltpu.with_memory_space_constraint(x, pltpu.HBM), *riders)
+
+
+def load_kernel(count, place_ref, w_ref, out_ref, sems):
+    depth = w_ref.shape[0] // count
+
+    def block(r):
+        owner = place_ref[0] ^ r
+        return pltpu.make_async_copy(
+            w_ref.at[pl.ds(pl.multiple_of(owner * depth, depth), depth), :],
+            out_ref.at[r * depth : (r + 1) * depth, :],
+            sems.at[r],
+        )
+
+    for r in range(count):
+        block(r).start()
+    for r in range(count):
+        block(r).wait()
+
+
+def load_rows(weight, place, count):
+    return pl.pallas_call(
+        functools.partial(load_kernel, count),
+        in_specs=[
+            pl.BlockSpec(memory_space=pltpu.SMEM),
+            pl.BlockSpec(memory_space=pltpu.HBM),
+        ],
+        out_specs=pl.BlockSpec(memory_space=pltpu.VMEM),
+        out_shape=pltpu.VMEM(weight.shape, weight.dtype),
+        scratch_shapes=[pltpu.SemaphoreType.DMA((count,))],
+        compiler_params=pltpu.CompilerParams(vmem_limit_bytes=2 << 20),
+        cost_estimate=pl.CostEstimate(
+            flops=0, transcendentals=0, bytes_accessed=2 * weight.size * 2
+        ),
+        name="load_rows",
+    )(place, pltpu.with_memory_space_constraint(weight, pltpu.HBM))
+
+
+def attend_kernel(heads, rows, count, *refs):
+    riders, ins, outs = refs[: -2 * count], refs[-2 * count : -count], refs[-count:]
+    width = heads * 3 * HEAD
+    blocks = [unpack_tiles(ref, rows, width) for ref in ins]
+
+    def columns(start):
+        first, offset = divmod(start, LANES)
+        parts = []
+        for tiles in blocks:
+            if offset + HEAD <= LANES:
+                parts.append(tiles[first][:, offset : offset + HEAD])
+            else:
+                wide = jnp.concatenate([tiles[first], tiles[first + 1]], axis=1)
+                parts.append(wide[:, offset : offset + HEAD])
+        return jnp.concatenate(parts, axis=0)
+
+    results = []
+    for h in range(heads):
+        start = h * 3 * HEAD
+        query, key, value = (columns(start + i * HEAD) for i in range(3))
+        scores = lax.dot_general(
+            query, key, (((1,), (1,)), ((), ())), preferred_element_type=jnp.float32
+        ) * HEAD ** (-0.5)
+        row_max = jnp.max(scores, axis=-1, keepdims=True)
+        exp_scores = jnp.exp(scores - row_max)
+        row_sum = jnp.sum(exp_scores, axis=-1, keepdims=True)
+        weights = (exp_scores / row_sum).astype(jnp.bfloat16)
+        results.append(jnp.dot(weights, value, preferred_element_type=jnp.float32))
+    attended = jnp.concatenate(results, axis=1).astype(jnp.bfloat16)
+    whole = heads * HEAD // LANES
+    for b in range(count):
+        mine = attended[b * rows : (b + 1) * rows]
+        for t in range(whole):
+            outs[b][t * rows : (t + 1) * rows, :] = mine[:, t * LANES : (t + 1) * LANES]
+        rest = mine[:, whole * LANES :].astype(jnp.float32)
+        packed = rows * heads * HEAD // LANES
+        outs[b][whole * rows : packed, :] = jnp.concatenate(
+            [rest[: rows // 2], rest[rows // 2 :]], axis=1
+        ).astype(jnp.bfloat16)
+        if riders:
+            group_ref, head_ref, mod_ref = riders
+            put_head(outs[b], packed, head_ref, group_ref)
+            packed += head_ref.shape[0] // 2 * head_tiles(head_ref.shape[1])
+            put_modulation(outs[b], packed, mod_ref[1:2, :])
+
+
+def attend_packed(pieces, heads, rows, riders=()):
+    count = len(pieces)
+    total = count * rows
+    length = rows * heads * HEAD // LANES
+    specs = [pl.BlockSpec(memory_space=pltpu.VMEM)] * count
+    if riders:
+        head = riders[1]
+        length += head.shape[0] // 2 * head_tiles(head.shape[1]) + MOD_ROWS
+        specs = [pl.BlockSpec(memory_space=pltpu.SMEM)] + specs + specs[:2]
+    out = jax.ShapeDtypeStruct((length, LANES), jnp.bfloat16)
+    return pl.pallas_call(
+        functools.partial(attend_kernel, heads, rows, count),
+        in_specs=specs,
+        out_shape=[out] * count,
+        compiler_params=pltpu.CompilerParams(vmem_limit_bytes=12 << 20),
+        cost_estimate=pl.CostEstimate(
+            flops=4 * heads * total * total * HEAD,
+            transcendentals=heads * total * total,
+            bytes_accessed=8 * total * heads * HEAD,
+        ),
+        name="attend_packed",
+    )(*riders, *pieces)
+
+
+def gather_left(refs, left_ref, rows):
+    depth = left_ref.shape[1] // len(refs)
+    left_ref[...] = jnp.concatenate(
+        [jnp.concatenate(unpack_tiles(ref, rows, depth), axis=1)[:, :depth] for ref in refs],
+        axis=1,
+    )
+
+
+def project_kernel(rows, w_ref, *refs):
+    pieces, out_ref, left_ref = refs[:-2], refs[-2], refs[-1]
+    gather_left(pieces, left_ref, rows)
+    for start in range(0, w_ref.shape[1], 512):
+        cut = slice(start, start + 512)
+        out_ref[:, cut] = jnp.dot(
+            left_ref[...], w_ref[:, cut], preferred_element_type=jnp.float32
+        ).astype(jnp.bfloat16)
+
+
+def project_packed(pieces, weight, rows):
+    depth, dim = weight.shape
+    return pl.pallas_call(
+        functools.partial(project_kernel, rows),
+        out_shape=jax.ShapeDtypeStruct((rows, dim), jnp.bfloat16),
+        scratch_shapes=[pltpu.VMEM((rows, depth), jnp.bfloat16)],
+        compiler_params=pltpu.CompilerParams(vmem_limit_bytes=16 << 20),
+        cost_estimate=pl.CostEstimate(
+            flops=2 * rows * depth * dim, transcendentals=0, bytes_accessed=2 * depth * dim
+        ),
+        name="project_packed",
+    )(pltpu.with_memory_space_constraint(weight, pltpu.VMEM), *pieces)
+
+
+def finish_kernel(rows, count, size_ref, w_ref, *refs):
+    pieces, refs = refs[:count], refs[count:]
+    mod_ref, far_ref, hidden_ref, head_ref, latent_ref, out_ref, step_ref = refs[:7]
+    acc_ref, left_ref, turn_ref = refs[7:]
+    steps, _, tile = acc_ref.shape
+    dim = steps * tile
+
+    def modulation(which, i):
+        start = which * dim + i * tile
+        line, offset = divmod(start, mod_ref.shape[2])
+        return mod_ref[line, :, offset : offset + tile]
+
+    gather_left(pieces, left_ref, rows)
+    total = jnp.zeros((rows, 1), jnp.float32)
+    for i in range(steps):
+        cut = slice(i * tile, (i + 1) * tile)
+        projected = jnp.dot(left_ref[...], w_ref[:, cut], preferred_element_type=jnp.float32)
+        projected = projected + far_ref[:, cut].astype(jnp.float32)
+        part = hidden_ref[:, cut].astype(jnp.float32) + modulation(0, i) * projected
+        acc_ref[i] = part
+        total += jnp.sum(part, axis=-1, keepdims=True)
+    average = total / dim
+    square = jnp.zeros((rows, 1), jnp.float32)
+    for i in range(steps):
+        centred = acc_ref[i] - average
+        square += jnp.sum(centred * centred, axis=-1, keepdims=True)
+    rate = lax.rsqrt(square / dim + 1e-06)
+    velocity = jnp.zeros(turn_ref.shape, jnp.float32)
+    for i in range(steps):
+        cut = slice(i * tile, (i + 1) * tile)
+        normed = (
+            (acc_ref[i] - average) * rate * (1.0 + modulation(2, i)) + modulation(1, i)
+        ).astype(jnp.bfloat16)
+        velocity += lax.dot_general(
+            normed,
+            head_ref[:, cut],
+            (((1,), (1,)), ((), ())),
+            preferred_element_type=jnp.float32,
+        )
+    turn_ref[...] = velocity
+    paired = jnp.concatenate(
+        [turn_ref[pl.ds(0, rows // 2, stride=2), :], turn_ref[pl.ds(1, rows // 2, stride=2), :]],
+        axis=1,
+    )
+    out_ref[...] = paired
+    step_ref[...] = latent_ref[...] + size_ref[0] * paired
+
+
+def finish(pieces, weight, far, hidden, lines, head_rows, latent, size, rows):
+    depth, dim = weight.shape
+    count = len(pieces)
+    tile = math.gcd(dim, lines.shape[2])
+    patch = head_rows.shape[0]
+    inputs = (pltpu.with_memory_space_constraint(weight, pltpu.VMEM), *pieces, lines)
+    inputs += (far, hidden, head_rows, latent)
+    result = jax.ShapeDtypeStruct((rows // 2, 2 * patch), jnp.float32)
+    return pl.pallas_call(
+        functools.partial(finish_kernel, rows, count),
+        in_specs=[pl.BlockSpec(memory_space=pltpu.SMEM)]
+        + [pl.BlockSpec(memory_space=pltpu.VMEM)] * len(inputs),
+        out_shape=[result] * 2,
+        scratch_shapes=[
+            pltpu.VMEM((dim // tile, rows, tile), jnp.float32),
+            pltpu.VMEM((rows, depth), jnp.bfloat16),
+            pltpu.VMEM((rows, patch), jnp.float32),
+        ],
+        compiler_params=pltpu.CompilerParams(vmem_limit_bytes=16 << 20),
+        cost_estimate=pl.CostEstimate(
+            flops=2 * rows * depth * dim, transcendentals=0, bytes_accessed=2 * depth * dim
+        ),
+        name="finish",
+    )(size, *inputs)
+
+
+def collect_kernel(count, packed, done, group_ref, head_ref, *refs):
+    queries, far, out_ref = refs[:count], refs[count:-1], refs[-1]
+    span = out_ref.shape[0] // (2 * count)
+    put_head(out_ref, 0, head_ref, group_ref)
+    for r in range(1, count):
+        out_ref[r * span : (r + 1) * span, :] = queries[r][packed : packed + span, :]
+    for r in range(count):
+        out_ref[(count + r) * span : (count + r + 1) * span, :] = far[r][done : done + span, :]
+
+
+def collect_head(queries, far, head, group, packed, done):
+    count = len(far)
+    span = head.shape[0] // 2 * head_tiles(head.shape[1])
+    return pl.pallas_call(
+        functools.partial(collect_kernel, count, packed, done),
+        in_specs=[pl.BlockSpec(memory_space=pltpu.SMEM)]
+        + [pl.BlockSpec(memory_space=pltpu.VMEM)] * (1 + 2 * count),
+        out_shape=jax.ShapeDtypeStruct((2 * count * span, LANES), jnp.bfloat16),
+        compiler_params=pltpu.CompilerParams(vmem_limit_bytes=4 << 20),
+        cost_estimate=pl.CostEstimate(
+            flops=0, transcendentals=0, bytes_accessed=8 * count * span * LANES
+        ),
+        name="collect_head",
+    )(group, head, *queries, *far)
+
+
+def arrange_kernel(count, width, near_at, done, place_ref, half_ref, group_ref, *refs):
+    mine_ref, up_ref, mod_ref = refs[:3]
+    near, far = refs[3 : 3 + count], refs[3 + count : -2]
+    head_out, mod_out = refs[-2:]
+    span = mine_ref.shape[0] // (2 * count)
+    cut = head_out.shape[0] // 2
+    tiles = span // cut
+    first = half_ref[0] == 0
+    lower = group_ref[0] == 0
+    columns = mod_ref.shape[1]
+
+    def block(ref, k):
+        parts = [ref[k * span + t * cut : k * span + (t + 1) * cut, :] for t in range(tiles)]
+        return jnp.concatenate(parts, axis=1)[:, :width]
+
+    def whole(k):
+        mine, up = block(mine_ref, k), block(up_ref, k)
+        return jnp.concatenate(
+            [jnp.where(lower, mine, up), jnp.where(lower, up, mine)], axis=0
+        )
+
+    for r in range(count):
+        owner = place_ref[0] ^ r
+        own, other = whole(r), whole(count + r)
+        start = pl.multiple_of(owner * 2 * width, LANES)
+        head_out[:, pl.ds(start, 2 * width)] = jnp.concatenate(
+            [jnp.where(first, own, other), jnp.where(first, other, own)], axis=1
+        )
+        own = mod_ref[0:1, :] if r == 0 else get_modulation(near[r], near_at[r], columns)
+        other = get_modulation(far[r], done + span, columns)
+        mod_out[owner] = jnp.concatenate(
+            [jnp.where(first, own, other), jnp.where(first, other, own)], axis=1
+        )
+
+
+def arrange(mine, up, modulation, near, far, head, scalars, near_at, done):
+    count = len(far)
+    patch, width = head.shape
+    columns = modulation.shape[1]
+    return pl.pallas_call(
+        functools.partial(arrange_kernel, count, width, near_at, done),
+        in_specs=[pl.BlockSpec(memory_space=pltpu.SMEM)] * 3
+        + [pl.BlockSpec(memory_space=pltpu.VMEM)] * (3 + 2 * count),
+        out_shape=[
+            jax.ShapeDtypeStruct((patch, 2 * count * width), jnp.bfloat16),
+            jax.ShapeDtypeStruct((count, 1, 2 * columns), jnp.float32),
+        ],
+        compiler_params=pltpu.CompilerParams(vmem_limit_bytes=4 << 20),
+        cost_estimate=pl.CostEstimate(
+            flops=0, transcendentals=0, bytes_accessed=8 * count * patch * width
+        ),
+        name="arrange",
+    )(*scalars, mine, up, modulation, *near, *far)
+
+
+def packed_body(head_inputs, hidden, out_weight, time_weight, head_weight, latent, timesteps):
+    count = lax.axis_size("seq")
+    halves = lax.axis_size("fsdp")
+    rows = head_inputs.shape[2]
+    place = lax.axis_index("seq")
+    half = lax.axis_index("fsdp")
+    group = lax.axis_index("grp")
+    heads = HEADS // halves // count
+
+    def along(block, r):
+        return lax.ppermute(block, "seq", [(i, i ^ r) for i in range(count)])
+
+    def swap(block, axis):
+        return lax.ppermute(block, axis, [(0, 1), (1, 0)])
+
+    def slanted(block, r):
+        route = []
+        for i in range(count):
+            for j in range(halves):
+                route.append((i * halves + j, (i ^ r) * halves + 1 - j))
+        return lax.ppermute(block, ("seq", "fsdp"), route)
+
+    x = head_inputs.reshape(rows, head_inputs.shape[3])
+    head = jnp.swapaxes(head_weight[0], 0, 1)
+    span = head.shape[0] // 2 * head_tiles(head.shape[1])
+    here = place[None].astype(jnp.int32)
+    side = half[None].astype(jnp.int32)
+    level = group[None].astype(jnp.int32)
+    scalars = (here, side, level)
+    far_rides, near_rides = far_extra(count), near_extra(count)
+
+    far_sent = split_heads(x, True, far_rides, scalars, (head,), halves)
+    far_pieces = [far_sent[0]] + [along(far_sent[r], r) for r in range(1, count)]
+
+    other_steps = swap(timesteps, "fsdp")
+    steps_both = jnp.concatenate([timesteps[0, :, 0], other_steps[0, :, 0]])
+    embedding = time_embed(steps_both).astype(jnp.bfloat16)
+    modulation = jnp.dot(embedding, time_weight[0], preferred_element_type=jnp.float32)
+    step_size = sigma_of(timesteps[0, :, 1]) - sigma_of(timesteps[0, :, 0])
+
+    near_sent = split_heads(x, False, near_rides, scalars, (head, modulation), halves)
+    near_pieces = [near_sent[0]] + [along(near_sent[r], r) for r in range(1, count)]
+
+    weight = load_rows(out_weight[0], here, count)
+    far_attended = attend_packed(far_pieces, heads, rows, (level, head, modulation))
+    far_home = [slanted(far_attended[r], r) for r in range(count)]
+    partial = project_packed(far_home, weight, rows)
+    partial = swap(partial, "fsdp")
+
+    packed = far_sent[0].shape[0]
+    done = far_home[0].shape[0] - span - MOD_ROWS
+    queries = [far_pieces[r] if far_rides[r][0] else near_pieces[r] for r in range(count)]
+    near_at = [packed + span * with_head for with_head, _ in near_rides]
+    mine = collect_head(queries, far_home, head, level, packed, done)
+    up = swap(mine, "grp")
+    head_rows, lines = arrange(
+        mine, up, modulation, near_pieces, far_home, head, scalars, near_at, done
+    )
+
+    near_attended = attend_packed(near_pieces, heads, rows)
+    near_home = [near_attended[0]]
+    near_home += [along(near_attended[r], r) for r in range(1, count)]
+    velocity, stepped = finish(
+        near_home,
+        weight,
+        partial,
+        hidden.reshape(rows, DIM),
+        lines,
+        head_rows,
+        latent.reshape(rows // 2, 2 * PATCH),
+        step_size,
+        rows,
+    )
+    carried = partner(stepped, "section", 0)
+    return (velocity.reshape(latent.shape), carried.reshape(latent.shape))
+
+
+def packed_fits(mesh, head_shape):
+    count, halves = mesh.shape["seq"], mesh.shape["fsdp"]
+    rows = head_shape[2]
+    return (
+        head_shape[1] == 1
+        and halves == 2
+        and mesh.shape["grp"] == 2
+        and count & (count - 1) == 0
+        and HEADS % (halves * count) == 0
+        and 3 * DIM // (halves * count) <= 8 * LANES
+        and DIM % (halves * count) == 0
+        and HEADS // (halves * count) * HEAD % LANES == LANES // 2
+        and rows % 32 == 0
+        and rows * count <= 512
+    )
+
+
+def step(mesh, body):
     return jax.shard_map(
         body,
         mesh=mesh,
@@ -130,3 +674,17 @@
         ),
         check_vma=False,
     )
+
+
+def solution(mesh):
+    def choose(head_inputs, *rest):
+        local = (
+            head_inputs.shape[0] // mesh.shape["section"],
+            head_inputs.shape[1] // mesh.shape["grp"] // mesh.shape["fsdp"],
+            head_inputs.shape[2] // mesh.shape["seq"],
+        )
+        if not packed_fits(mesh, local):
+            return step(mesh, general_body)(head_inputs, *rest)
+        return step(mesh, packed_body)(head_inputs, *rest)
+
+    return choose

time: 164 us -> 67.5 us (0.41)
  blocking collectives: 116 us -> 0 us
  starting transfers between devices: 0.15 us -> 25.6 us
  waiting for transfers between devices: 1.92 us -> 21.7 us
  between operations: 17.1 us -> 2.18 us
  matrix products: 13.4 us -> 0.23 us
  Pallas kernels: 0 us -> 13 us
  local copies, waits for them, and re-layouts: 10.4 us -> 3.55 us
  other arithmetic: 5.18 us -> 0.88 us
    all_to_all x3 -> x0, blocking collectives: 78.4 us -> none  [the longest x1 47.7 us: body(): lax.all_to_all(local, 'seq', split_axis=2, concat_axis=1, tiled=True)]
    all_gather x1 -> x0, blocking collectives: 37.3 us -> none  [body(): lax.all_gather(head_weight, ('seq', 'fsdp'), axis=1, tiled=True)]
    ppermute x0 -> x16, starting transfers between devices: none -> 25.6 us  [the longest x9 13.5 us: along(): return lax.ppermute(block, 'seq', [(i, i ^ r) for i in range(count)])]
    ppermute x0 -> x16, waiting for transfers between devices: none -> 20.6 us  [the longest x9 20.5 us: along(): return lax.ppermute(block, 'seq', [(i, i ^ r) for i in range(count)])]
    pallas_call x0 -> x9, Pallas kernels: none -> 13 us  [the longest x2 3.45 us: attend_packed(): pl.pallas_call(functools.partial(attend_kernel, heads, rows, count), in_s...]
    dot_general x4 -> x1, matrix products: 11.2 us -> 0.23 us  [packed_body(): jnp.dot(embedding, time_weight[0], preferred_element_type=jnp.float32)]
    reshape x3 -> x0, local copies, waits for them, and re-layouts: 4.19 us -> none  [the longest x2 4.12 us: body(): local = head_inputs.reshape(samples, row_count, HEADS, 3 * HEAD)]
    unnamed x1 -> x0, other arithmetic: 2.61 us -> none
  transfers between devices with their start and end apart: 3 -> 17, of which waited for: 1 -> 7; matrix products, arithmetic and copies ran while one was open for 15% -> 4% of each run, Pallas kernels for 0% -> 13%
where the time goes in v1:
time: 67.5 us; the launch traced here: 67.1 us
  starting transfers between devices  25.6 us (38%)
  waiting for transfers between devices  21.7 us (32%)
  Pallas kernels  13 us (19%)
  local copies, waits for them, and re-layouts  3.55 us (5%)
  between operations  2.18 us (3%)
  other arithmetic  0.88 us (1%)
    ppermute x9, waiting for transfers between devices, along(): return lax.ppermute(block, 'seq', [(i, i ^ r) for i in range(count)])  20.5 us
    ppermute x9, starting transfers between devices, along(): return lax.ppermute(block, 'seq', [(i, i ^ r) for i in range(count)])  13.5 us
    ppermute x4, starting transfers between devices, slanted(): return lax.ppermute(block, ('seq', 'fsdp'), route)  6.81 us
    ppermute x3, starting transfers between devices, swap(): return lax.ppermute(block, axis, [(0, 1), (1, 0)])  5.22 us
    pallas_call x2, Pallas kernels, attend_packed(): pl.pallas_call(functools.partial(attend_kernel, heads, rows, count), in_s...  3.45 us
    pallas_call x1, Pallas kernels, load_rows(): pl.pallas_call(functools.partial(load_kernel, count), in_specs=[pl.BlockS...  2.95 us
    pallas_call x2, Pallas kernels, split_heads(): pl.pallas_call(functools.partial(split_kernel, width, flip, extra), in_sp...  2.82 us
    pallas_call x1, Pallas kernels, finish(): pl.pallas_call(functools.partial(finish_kernel, rows, count), in_specs=[p...  2.34 us
  transfers between devices with their start and end apart: 17, of which 7 were waited for; matrix products, arithmetic and copies ran while one was open for 4% of the time, Pallas kernels for 13%

profile of v1, /device:TPU:0, one launch (start us, length us, event | category | flops | bytes accessed | tf_op | source)
XLA Modules:
  0.0 67.1 jit_solution(6958053034412661068)
XLA Ops:
  0.6 3.0 %collective-permute-start = (s32[1,1,2]{2,1,0:T(1,128)}, s32[1,1,2]{2,1,0:T(1,128)S(1)}, u32[]{:S(2)}, u32[]{:S(2)}) collective-permute-start(s32[1,1,2]{2,1,0:T(1,128)} %param.13), channel_id=1, source_target_pairs={{0,1},{1,0},{2,3},{3,2},{4,5},{5,4},{6,7},{7,6},{8,9},{9,8},{10,11... | collective-permute-start | bytes 32 | tf_op jit(solution)/shard_map/ppermute | solution.py:577
  3.7 0.8 %copy-done.1 = bf16[1,320,64]{1,2,0:T(8,128)(2,1)S(1)} copy-done((bf16[1,320,64]{1,2,0:T(8,128)(2,1)S(1)}, bf16[1,320,64]{1,2,0:T(8,128)(2,1)}, u32[]{:S(2)}) %copy-start.1) | copy-done | bytes 40984
  4.5 1.4 %split_heads.3 = (bf16[480,128]{1,0:T(8,128)(2,1)S(1)}, bf16[480,128]{1,0:T(8,128)(2,1)S(1)}, bf16[576,128]{1,0:T(8,128)(2,1)S(1)}, bf16[480,128]{1,0:T(8,128)(2,1)S(1)}) custom-call(s32[1]{0:T(128)} %bitcast.2.place_ref, s32[1]{0:T(128)} %bitcast.4.half_ref, s32[1]{0:T(128)} %bitcast.5.group_ref.refs_0_, bf16[64,7680]{1,0:T(8,128)(2,1)} %bitcast.26, ...), custom_call_target="tpu_custom_call" | custom-call | bytes 983040 | tf_op jit(solution)/shard_map/split_heads/pallas_call | solution.py:254
  5.9 1.6 %collective-permute-start.8 = (bf16[480,128]{1,0:T(8,128)(2,1)S(1)}, bf16[480,128]{1,0:T(8,128)(2,1)S(1)}, u32[]{:S(2)}, u32[]{:S(2)}) collective-permute-start(bf16[480,128]{1,0:T(8,128)(2,1)S(1)} %get-tuple-element.32), channel_id=1, source_target_pairs={{0,2},{2,0},{4,6},{6,4},{1,3},{3,1},{5,7},{7,5},{8,10},{10,8},{12,... | collective-permute-start | bytes 368648 | tf_op jit(solution)/shard_map/ppermute | solution.py:574
  7.5 2.5 %collective-permute-start.9 = (bf16[480,128]{1,0:T(8,128)(2,1)S(1)}, bf16[480,128]{1,0:T(8,128)(2,1)S(1)}, u32[]{:S(2)}, u32[]{:S(2)}) collective-permute-start(bf16[480,128]{1,0:T(8,128)(2,1)S(1)} %get-tuple-element.33), channel_id=1, source_target_pairs={{0,6},{2,4},{4,2},{6,0},{1,7},{3,5},{5,3},{7,1},{8,14},{10,12},{12... | collective-permute-start | bytes 368648 | tf_op jit(solution)/shard_map/ppermute | solution.py:574
  10.1 1.3 %fusion.8 = (s32[1,1,1]{2,1,0:T(1,128)}, s32[1,1,1]{2,1,0:T(1,128)}) fusion(s32[1,1,2]{2,1,0:T(1,128)} %param.13), kind=kLoop, calls=%fused_computation.12 | loop fusion | bytes 16 | tf_op jit(solution)/shard_map/slice | solution.py:602
  11.4 0.8 %add_convert_fusion = f32[2]{0:T(128)S(1)} fusion(s32[1]{0:T(128)S(1)} %bitcast.30, s32[1]{0:T(128)} %bitcast.1), kind=kLoop, calls=%fused_computation.9 | loop fusion | flops 4 | bytes 16 | tf_op jit(solution)/shard_map/convert_element_type | solution.py:33
  12.5 4.2 %collective-permute-done.9.refs_6_ = bf16[480,128]{1,0:T(8,128)(2,1)S(1)} collective-permute-done((bf16[480,128]{1,0:T(8,128)(2,1)S(1)}, bf16[480,128]{1,0:T(8,128)(2,1)S(1)}, u32[]{:S(2)}, u32[]{:S(2)}) %collective-permute-start.9) | collective-permute-done | bytes 122912 | tf_op jit(solution)/shard_map/ppermute | solution.py:574
  16.8 5.0 %collective-permute-done.7.refs_5_.refs_2_ = bf16[576,128]{1,0:T(8,128)(2,1)S(1)} collective-permute-done((bf16[576,128]{1,0:T(8,128)(2,1)S(1)}, bf16[576,128]{1,0:T(8,128)(2,1)S(1)}, u32[]{:S(2)}, u32[]{:S(2)}) %collective-permute-start.7) | collective-permute-done | bytes 147488 | tf_op jit(solution)/shard_map/ppermute | solution.py:574
  21.8 0.8 %copy-done.2 = bf16[1,320,64]{1,2,0:T(8,128)(2,1)S(1)} copy-done((bf16[1,320,64]{1,2,0:T(8,128)(2,1)S(1)}, bf16[1,320,64]{1,2,0:T(8,128)(2,1)}, u32[]{:S(2)}) %copy-start.2) | copy-done | bytes 40984
  22.6 1.7 %attend_packed.3 = (bf16[288,128]{1,0:T(8,128)(2,1)S(1)}, bf16[288,128]{1,0:T(8,128)(2,1)S(1)}, bf16[288,128]{1,0:T(8,128)(2,1)S(1)}, bf16[288,128]{1,0:T(8,128)(2,1)S(1)}) custom-call(s32[1]{0:T(128)} %bitcast.5.group_ref.refs_0_, bf16[64,320]{1,0:T(8,128)(2,1)S(1)} %bitcast.20, f32[2,960]{1,0:T(2,128)S(1)} %fusion.refs_1_.refs_2_, ...), custom_call_target="tpu_custom_call" | custom-call | flops 83886080 | bytes 655360 | tf_op jit(solution)/shard_map/attend_packed/pallas_call | solution.py:363
  24.3 0.6 collective-permute-start.10
  24.9 0.8 %collective-permute-start.11 = (bf16[288,128]{1,0:T(8,128)(2,1)S(1)}, bf16[288,128]{1,0:T(8,128)(2,1)S(1)}, u32[]{:S(2)}, u32[]{:S(2)}) collective-permute-start(bf16[288,128]{1,0:T(8,128)(2,1)S(1)} %get-tuple-element.35), channel_id=1, source_target_pairs={{0,3},{1,2},{2,1},{3,0},{4,7},{5,6},{6,5},{7,4},{8,11},{9,10},{10,... | collective-permute-start | bytes 221192 | tf_op jit(solution)/shard_map/ppermute | solution.py:584
  25.7 3.4 %collective-permute-start.12 = (bf16[288,128]{1,0:T(8,128)(2,1)S(1)}, bf16[288,128]{1,0:T(8,128)(2,1)S(1)}, u32[]{:S(2)}, u32[]{:S(2)}) collective-permute-start(bf16[288,128]{1,0:T(8,128)(2,1)S(1)} %get-tuple-element.36), channel_id=1, source_target_pairs={{0,5},{1,4},{2,7},{3,6},{4,1},{5,0},{6,3},{7,2},{8,13},{9,12},{10,... | collective-permute-start | bytes 221192 | tf_op jit(solution)/shard_map/ppermute | solution.py:584
  29.0 2.1 %collective-permute-start.13 = (bf16[288,128]{1,0:T(8,128)(2,1)S(1)}, bf16[288,128]{1,0:T(8,128)(2,1)S(1)}, u32[]{:S(2)}, u32[]{:S(2)}) collective-permute-start(bf16[288,128]{1,0:T(8,128)(2,1)S(1)} %get-tuple-element.37), channel_id=1, source_target_pairs={{0,7},{1,6},{2,5},{3,4},{4,3},{5,2},{6,1},{7,0},{8,15},{9,14},{10,... | collective-permute-start | bytes 221192 | tf_op jit(solution)/shard_map/ppermute | solution.py:584
  31.2 2.9 %load_rows.1.w_ref = bf16[1280,2560]{1,0:T(8,128)(2,1)S(1)} custom-call(s32[1]{0:T(128)} %bitcast.2.place_ref, bf16[1280,2560]{1,0:T(8,128)(2,1)} %bitcast.25), custom_call_target="tpu_custom_call" | custom-call | bytes 13107200 | tf_op jit(solution)/shard_map/load_rows/pallas_call | solution.py:290
  34.1 1.4 %split_heads.2 = (bf16[480,128]{1,0:T(8,128)(2,1)S(1)}, bf16[608,128]{1,0:T(8,128)(2,1)S(1)}, bf16[512,128]{1,0:T(8,128)(2,1)S(1)}, bf16[608,128]{1,0:T(8,128)(2,1)S(1)}) custom-call(s32[1]{0:T(128)} %bitcast.2.place_ref, s32[1]{0:T(128)} %bitcast.4.half_ref, s32[1]{0:T(128)} %bitcast.5.group_ref.refs_0_, bf16[64,7680]{1,0:T(8,128)(2,1)} %bitcast.27, ...), custom_call_target="tpu_custom_call" | custom-call | bytes 983040 | tf_op jit(solution)/shard_map/split_heads/pallas_call | solution.py:254
  35.7 2.7 %collective-permute-start.3 = (bf16[608,128]{1,0:T(8,128)(2,1)S(1)}, bf16[608,128]{1,0:T(8,128)(2,1)S(1)}, u32[]{:S(2)}, u32[]{:S(2)}) collective-permute-start(bf16[608,128]{1,0:T(8,128)(2,1)S(1)} %get-tuple-element.25), channel_id=1, source_target_pairs={{0,6},{2,4},{4,2},{6,0},{1,7},{3,5},{5,3},{7,1},{8,14},{10,12},{12... | collective-permute-start | bytes 466952 | tf_op jit(solution)/shard_map/ppermute | solution.py:574
  38.4 1.3 %project_packed.1 = bf16[64,2560]{1,0:T(8,128)(2,1)S(1)} custom-call(bf16[1280,2560]{1,0:T(8,128)(2,1)S(1)} %load_rows.1.w_ref, bf16[288,128]{1,0:T(8,128)(2,1)S(1)} %collective-permute-done.10.refs_4_.refs_7_.refs_0_, bf16[288,128]{1,0:T(8,128)(2,1)S(1)} %collective-permute-done.11.refs_5_.refs_8_.refs_1_, ...), custom_call_target="tpu_custom_call" | custom-call | flops 419430400 | bytes 6553600 | tf_op jit(solution)/shard_map/project_packed/pallas_call | solution.py:397
  39.7 0.6 collective-permute-start.15
  40.3 1.7 %collective-permute-done.1.refs_1_.refs_4_ = bf16[608,128]{1,0:T(8,128)(2,1)S(1)} collective-permute-done((bf16[608,128]{1,0:T(8,128)(2,1)S(1)}, bf16[608,128]{1,0:T(8,128)(2,1)S(1)}, u32[]{:S(2)}, u32[]{:S(2)}) %collective-permute-start.1) | collective-permute-done | bytes 155680 | tf_op jit(solution)/shard_map/ppermute | solution.py:574
  42.0 1.7 %collective-permute-done.3.refs_3_.refs_6_ = bf16[608,128]{1,0:T(8,128)(2,1)S(1)} collective-permute-done((bf16[608,128]{1,0:T(8,128)(2,1)S(1)}, bf16[608,128]{1,0:T(8,128)(2,1)S(1)}, u32[]{:S(2)}, u32[]{:S(2)}) %collective-permute-start.3) | collective-permute-done | bytes 155680 | tf_op jit(solution)/shard_map/ppermute | solution.py:574
  43.7 1.6 %collective-permute-start.14 = (bf16[768,128]{1,0:T(8,128)(2,1)S(1)}, bf16[768,128]{1,0:T(8,128)(2,1)S(1)}, u32[]{:S(2)}, u32[]{:S(2)}) collective-permute-start(bf16[768,128]{1,0:T(8,128)(2,1)S(1)} %collect_head.1.refs_0_), channel_id=1, source_target_pairs={{0,16},{16,0},{1,17},{17,1},{2,18},{18,2},{3,19},{19,3},{4,20},{20... | collective-permute-start | bytes 589832 | tf_op jit(solution)/shard_map/ppermute | solution.py:577
  45.3 2.1 %collective-permute-start.2 = (bf16[512,128]{1,0:T(8,128)(2,1)S(1)}, bf16[512,128]{1,0:T(8,128)(2,1)S(1)}, u32[]{:S(2)}, u32[]{:S(2)}) collective-permute-start(bf16[512,128]{1,0:T(8,128)(2,1)S(1)} %get-tuple-element.24), channel_id=1, source_target_pairs={{0,4},{2,6},{4,0},{6,2},{1,5},{3,7},{5,1},{7,3},{8,12},{10,14},{12... | collective-permute-start | bytes 393224 | tf_op jit(solution)/shard_map/ppermute | solution.py:574
  47.4 5.2 %collective-permute-done.2.refs_2_.refs_5_ = bf16[512,128]{1,0:T(8,128)(2,1)S(1)} collective-permute-done((bf16[512,128]{1,0:T(8,128)(2,1)S(1)}, bf16[512,128]{1,0:T(8,128)(2,1)S(1)}, u32[]{:S(2)}, u32[]{:S(2)}) %collective-permute-start.2) | collective-permute-done | bytes 131104 | tf_op jit(solution)/shard_map/ppermute | solution.py:574
  52.6 1.7 %attend_packed.2 = (bf16[160,128]{1,0:T(8,128)(2,1)S(1)}, bf16[160,128]{1,0:T(8,128)(2,1)S(1)}, bf16[160,128]{1,0:T(8,128)(2,1)S(1)}, bf16[160,128]{1,0:T(8,128)(2,1)S(1)}) custom-call(bf16[480,128]{1,0:T(8,128)(2,1)S(1)} %get-tuple-element.22.refs_0_.refs_3_, bf16[608,128]{1,0:T(8,128)(2,1)S(1)} %collective-permute-done.1.refs_1_.refs_4_, ...), custom_call_target="tpu_custom_call" | custom-call | flops 83886080 | bytes 655360 | tf_op jit(solution)/shard_map/attend_packed/pallas_call | solution.py:363
  54.4 2.8 %collective-permute-start.5 = (bf16[160,128]{1,0:T(8,128)(2,1)S(1)}, bf16[160,128]{1,0:T(8,128)(2,1)S(1)}, u32[]{:S(2)}, u32[]{:S(2)}) collective-permute-start(bf16[160,128]{1,0:T(8,128)(2,1)S(1)} %get-tuple-element.28), channel_id=1, source_target_pairs={{0,4},{2,6},{4,0},{6,2},{1,5},{3,7},{5,1},{7,3},{8,12},{10,14},{12... | collective-permute-start | bytes 122888 | tf_op jit(solution)/shard_map/ppermute | solution.py:574
  57.2 1.6 %collective-permute-start.6 = (bf16[160,128]{1,0:T(8,128)(2,1)S(1)}, bf16[160,128]{1,0:T(8,128)(2,1)S(1)}, u32[]{:S(2)}, u32[]{:S(2)}) collective-permute-start(bf16[160,128]{1,0:T(8,128)(2,1)S(1)} %get-tuple-element.29), channel_id=1, source_target_pairs={{0,6},{2,4},{4,2},{6,0},{1,7},{3,5},{5,3},{7,1},{8,14},{10,12},{12... | collective-permute-start | bytes 122888 | tf_op jit(solution)/shard_map/ppermute | solution.py:574
  60.4 2.6 %collective-permute-done.6.refs_3_ = bf16[160,128]{1,0:T(8,128)(2,1)S(1)} collective-permute-done((bf16[160,128]{1,0:T(8,128)(2,1)S(1)}, bf16[160,128]{1,0:T(8,128)(2,1)S(1)}, u32[]{:S(2)}, u32[]{:S(2)}) %collective-permute-start.6) | collective-permute-done | bytes 40992 | tf_op jit(solution)/shard_map/ppermute | solution.py:574
  63.0 2.3 %finish.1 = (f32[32,128]{1,0:T(8,128)}, f32[32,128]{1,0:T(8,128)S(1)}) custom-call(f32[1]{0:T(128)S(6)} %sub.3.size_ref, bf16[1280,2560]{1,0:T(8,128)(2,1)S(1)} %load_rows.1.w_ref, bf16[160,128]{1,0:T(8,128)(2,1)S(1)} %get-tuple-element.26.refs_0_, bf16[160,128]{1,0:T(8,128)(2,1)S(1)} %collective-permute-done.4.refs_1_, ...), custom_call_target="tpu_custom_call" | custom-call | flops 419430400 | bytes 6553600 | tf_op jit(solution)/shard_map/finish/pallas_call | solution.py:465
  65.4 1.2 %collective-permute-done.16 = f32[32,128]{1,0:T(8,128)S(1)} collective-permute-done((f32[32,128]{1,0:T(8,128)S(1)}, f32[32,128]{1,0:T(8,128)S(1)}, u32[]{:S(2)}, u32[]{:S(2)}) %collective-permute-start.16) | collective-permute-done | bytes 16416 | tf_op jit(solution)/shard_map/ppermute | solution.py:27
  66.5 0.6 copy.10
  (29 shorter events, 0.8 us)
Async XLA Ops:
  0.6 11.7 %copy-start = (bf16[1,256,960]{1,2,0:T(8,128)(2,1)S(1)}, bf16[1,256,960]{1,2,0:T(8,128)(2,1)}, u32[]{:S(2)}) copy-start(bf16[1,256,960]{1,2,0:T(8,128)(2,1)} %param.10) | copy-start | bytes 1474564
  0.6 10.8 %collective-permute-start = (s32[1,1,2]{2,1,0:T(1,128)}, s32[1,1,2]{2,1,0:T(1,128)S(1)}, u32[]{:S(2)}, u32[]{:S(2)}) collective-permute-start(s32[1,1,2]{2,1,0:T(1,128)} %param.13), channel_id=1, source_target_pairs={{0,1},{1,0},{2,3},{3,2},{4,5},{5,4},{6,7},{7,6},{8,9},{9,8},{10,11... | collective-permute-start | bytes 32 | tf_op jit(solution)/shard_map/ppermute | solution.py:577
  3.7 0.8 %copy-start.1 = (bf16[1,320,64]{1,2,0:T(8,128)(2,1)S(1)}, bf16[1,320,64]{1,2,0:T(8,128)(2,1)}, u32[]{:S(2)}) copy-start(bf16[1,320,64]{1,2,0:T(8,128)(2,1)} %param.11) | copy-start | bytes 122884
  5.9 6.7 %collective-permute-start.8 = (bf16[480,128]{1,0:T(8,128)(2,1)S(1)}, bf16[480,128]{1,0:T(8,128)(2,1)S(1)}, u32[]{:S(2)}, u32[]{:S(2)}) collective-permute-start(bf16[480,128]{1,0:T(8,128)(2,1)S(1)} %get-tuple-element.32), channel_id=1, source_target_pairs={{0,2},{2,0},{4,6},{6,4},{1,3},{3,1},{5,7},{7,5},{8,10},{10,8},{12,... | collective-permute-start | bytes 368648 | tf_op jit(solution)/shard_map/ppermute | solution.py:574
  7.5 9.3 %collective-permute-start.9 = (bf16[480,128]{1,0:T(8,128)(2,1)S(1)}, bf16[480,128]{1,0:T(8,128)(2,1)S(1)}, u32[]{:S(2)}, u32[]{:S(2)}) collective-permute-start(bf16[480,128]{1,0:T(8,128)(2,1)S(1)} %get-tuple-element.33), channel_id=1, source_target_pairs={{0,6},{2,4},{4,2},{6,0},{1,7},{3,5},{5,3},{7,1},{8,14},{10,12},{12... | collective-permute-start | bytes 368648 | tf_op jit(solution)/shard_map/ppermute | solution.py:574
  10.0 11.8 %collective-permute-start.7 = (bf16[576,128]{1,0:T(8,128)(2,1)S(1)}, bf16[576,128]{1,0:T(8,128)(2,1)S(1)}, u32[]{:S(2)}, u32[]{:S(2)}) collective-permute-start(bf16[576,128]{1,0:T(8,128)(2,1)S(1)} %get-tuple-element.30), channel_id=1, source_target_pairs={{0,4},{2,6},{4,0},{6,2},{1,5},{3,7},{5,1},{7,3},{8,12},{10,14},{12... | collective-permute-start | bytes 442376 | tf_op jit(solution)/shard_map/ppermute | solution.py:574
  21.8 0.8 %copy-start.2 = (bf16[1,320,64]{1,2,0:T(8,128)(2,1)S(1)}, bf16[1,320,64]{1,2,0:T(8,128)(2,1)}, u32[]{:S(2)}) copy-start(bf16[1,320,64]{1,2,0:T(8,128)(2,1)} %param.11) | copy-start | bytes 122884
  24.3 11.3 %collective-permute-start.10 = (bf16[288,128]{1,0:T(8,128)(2,1)S(1)}, bf16[288,128]{1,0:T(8,128)(2,1)S(1)}, u32[]{:S(2)}, u32[]{:S(2)}) collective-permute-start(bf16[288,128]{1,0:T(8,128)(2,1)S(1)} %get-tuple-element.34), channel_id=1, source_target_pairs={{0,1},{1,0},{2,3},{3,2},{4,5},{5,4},{6,7},{7,6},{8,9},{9,8},{10,11... | collective-permute-start | bytes 221192 | tf_op jit(solution)/shard_map/ppermute | solution.py:584
  24.9 13.5 %collective-permute-start.11 = (bf16[288,128]{1,0:T(8,128)(2,1)S(1)}, bf16[288,128]{1,0:T(8,128)(2,1)S(1)}, u32[]{:S(2)}, u32[]{:S(2)}) collective-permute-start(bf16[288,128]{1,0:T(8,128)(2,1)S(1)} %get-tuple-element.35), channel_id=1, source_target_pairs={{0,3},{1,2},{2,1},{3,0},{4,7},{5,6},{6,5},{7,4},{8,11},{9,10},{10,... | collective-permute-start | bytes 221192 | tf_op jit(solution)/shard_map/ppermute | solution.py:584
  25.7 12.7 %collective-permute-start.12 = (bf16[288,128]{1,0:T(8,128)(2,1)S(1)}, bf16[288,128]{1,0:T(8,128)(2,1)S(1)}, u32[]{:S(2)}, u32[]{:S(2)}) collective-permute-start(bf16[288,128]{1,0:T(8,128)(2,1)S(1)} %get-tuple-element.36), channel_id=1, source_target_pairs={{0,5},{1,4},{2,7},{3,6},{4,1},{5,0},{6,3},{7,2},{8,13},{9,12},{10,... | collective-permute-start | bytes 221192 | tf_op jit(solution)/shard_map/ppermute | solution.py:584
  29.0 9.4 %collective-permute-start.13 = (bf16[288,128]{1,0:T(8,128)(2,1)S(1)}, bf16[288,128]{1,0:T(8,128)(2,1)S(1)}, u32[]{:S(2)}, u32[]{:S(2)}) collective-permute-start(bf16[288,128]{1,0:T(8,128)(2,1)S(1)} %get-tuple-element.37), channel_id=1, source_target_pairs={{0,7},{1,6},{2,5},{3,4},{4,3},{5,2},{6,1},{7,0},{8,15},{9,14},{10,... | collective-permute-start | bytes 221192 | tf_op jit(solution)/shard_map/ppermute | solution.py:584
  34.1 9.6 %copy-start.3 = (bf16[1,320,64]{1,2,0:T(8,128)(2,1)S(1)}, bf16[1,320,64]{1,2,0:T(8,128)(2,1)}, u32[]{:S(2)}) copy-start(bf16[1,320,64]{1,2,0:T(8,128)(2,1)} %param.11) | copy-start | bytes 122884
  34.1 28.9 %copy-start.4 = (bf16[1,1,64,2560]{3,2,1,0:T(8,128)(2,1)S(1)}, bf16[1,1,64,2560]{3,2,1,0:T(8,128)(2,1)}, u32[]{:S(2)}) copy-start(bf16[1,1,64,2560]{3,2,1,0:T(8,128)(2,1)} %param.8) | copy-start | bytes 983044
  34.1 28.9 %copy-start.5 = (f32[1,1,32,128]{3,2,1,0:T(8,128)S(1)}, f32[1,1,32,128]{3,2,1,0:T(8,128)}, u32[]{:S(2)}) copy-start(f32[1,1,32,128]{3,2,1,0:T(8,128)} %param.12) | copy-start | bytes 49156
  35.6 6.4 %collective-permute-start.1 = (bf16[608,128]{1,0:T(8,128)(2,1)S(1)}, bf16[608,128]{1,0:T(8,128)(2,1)S(1)}, u32[]{:S(2)}, u32[]{:S(2)}) collective-permute-start(bf16[608,128]{1,0:T(8,128)(2,1)S(1)} %get-tuple-element.23), channel_id=1, source_target_pairs={{0,2},{2,0},{4,6},{6,4},{1,3},{3,1},{5,7},{7,5},{8,10},{10,8},{12,... | collective-permute-start | bytes 466952 | tf_op jit(solution)/shard_map/ppermute | solution.py:574
  35.7 8.0 %collective-permute-start.3 = (bf16[608,128]{1,0:T(8,128)(2,1)S(1)}, bf16[608,128]{1,0:T(8,128)(2,1)S(1)}, u32[]{:S(2)}, u32[]{:S(2)}) collective-permute-start(bf16[608,128]{1,0:T(8,128)(2,1)S(1)} %get-tuple-element.25), channel_id=1, source_target_pairs={{0,6},{2,4},{4,2},{6,0},{1,7},{3,5},{5,3},{7,1},{8,14},{10,12},{12... | collective-permute-start | bytes 466952 | tf_op jit(solution)/shard_map/ppermute | solution.py:574
  39.7 23.3 %collective-permute-start.15 = (bf16[64,2560]{1,0:T(8,128)(2,1)S(1)}, bf16[64,2560]{1,0:T(8,128)(2,1)S(1)}, u32[]{:S(2)}, u32[]{:S(2)}) collective-permute-start(bf16[64,2560]{1,0:T(8,128)(2,1)S(1)} %project_packed.1), channel_id=1, source_target_pairs={{0,1},{1,0},{2,3},{3,2},{4,5},{5,4},{6,7},{7,6},{8,9},{9,8},{10,11... | collective-permute-start | bytes 983048 | tf_op jit(solution)/shard_map/ppermute | solution.py:577
  43.7 16.4 %collective-permute-start.14 = (bf16[768,128]{1,0:T(8,128)(2,1)S(1)}, bf16[768,128]{1,0:T(8,128)(2,1)S(1)}, u32[]{:S(2)}, u32[]{:S(2)}) collective-permute-start(bf16[768,128]{1,0:T(8,128)(2,1)S(1)} %collect_head.1.refs_0_), channel_id=1, source_target_pairs={{0,16},{16,0},{1,17},{17,1},{2,18},{18,2},{3,19},{19,3},{4,20},{20... | collective-permute-start | bytes 589832 | tf_op jit(solution)/shard_map/ppermute | solution.py:577
  45.3 7.3 %collective-permute-start.2 = (bf16[512,128]{1,0:T(8,128)(2,1)S(1)}, bf16[512,128]{1,0:T(8,128)(2,1)S(1)}, u32[]{:S(2)}, u32[]{:S(2)}) collective-permute-start(bf16[512,128]{1,0:T(8,128)(2,1)S(1)} %get-tuple-element.24), channel_id=1, source_target_pairs={{0,4},{2,6},{4,0},{6,2},{1,5},{3,7},{5,1},{7,3},{8,12},{10,14},{12... | collective-permute-start | bytes 393224 | tf_op jit(solution)/shard_map/ppermute | solution.py:574
  54.4 6.0 %collective-permute-start.4 = (bf16[160,128]{1,0:T(8,128)(2,1)S(1)}, bf16[160,128]{1,0:T(8,128)(2,1)S(1)}, u32[]{:S(2)}, u32[]{:S(2)}) collective-permute-start(bf16[160,128]{1,0:T(8,128)(2,1)S(1)} %get-tuple-element.27), channel_id=1, source_target_pairs={{0,2},{2,0},{4,6},{6,4},{1,3},{3,1},{5,7},{7,5},{8,10},{10,8},{12,... | collective-permute-start | bytes 122888 | tf_op jit(solution)/shard_map/ppermute | solution.py:574
  54.4 6.0 %collective-permute-start.5 = (bf16[160,128]{1,0:T(8,128)(2,1)S(1)}, bf16[160,128]{1,0:T(8,128)(2,1)S(1)}, u32[]{:S(2)}, u32[]{:S(2)}) collective-permute-start(bf16[160,128]{1,0:T(8,128)(2,1)S(1)} %get-tuple-element.28), channel_id=1, source_target_pairs={{0,4},{2,6},{4,0},{6,2},{1,5},{3,7},{5,1},{7,3},{8,12},{10,14},{12... | collective-permute-start | bytes 122888 | tf_op jit(solution)/shard_map/ppermute | solution.py:574
  57.2 5.8 %collective-permute-start.6 = (bf16[160,128]{1,0:T(8,128)(2,1)S(1)}, bf16[160,128]{1,0:T(8,128)(2,1)S(1)}, u32[]{:S(2)}, u32[]{:S(2)}) collective-permute-start(bf16[160,128]{1,0:T(8,128)(2,1)S(1)} %get-tuple-element.29), channel_id=1, source_target_pairs={{0,6},{2,4},{4,2},{6,0},{1,7},{3,5},{5,3},{7,1},{8,14},{10,12},{12... | collective-permute-start | bytes 122888 | tf_op jit(solution)/shard_map/ppermute | solution.py:574
  65.4 1.2 %collective-permute-start.16 = (f32[32,128]{1,0:T(8,128)S(1)}, f32[32,128]{1,0:T(8,128)S(1)}, u32[]{:S(2)}, u32[]{:S(2)}) collective-permute-start(f32[32,128]{1,0:T(8,128)S(1)} %get-tuple-element.41), channel_id=1, source_target_pairs={{0,8},{8,0},{1,9},{9,1},{2,10},{10,2},{3,11},{11,3},{4,12},{12,4},... | collective-permute-start | bytes 49160 | tf_op jit(solution)/shard_map/ppermute | solution.py:27

commit v2 on v1

--- a/solution.py
+++ b/solution.py
@@ -141,18 +141,7 @@
     return -(-width // LANES)
 
 
-MOD_ROWS = 32
-
-
-def put_head(out, at, head_ref, group_ref):
-    patch, width = head_ref.shape
-    cut = patch // 2
-    mine = pl.ds(pl.multiple_of(group_ref[0] * cut, cut), cut)
-    for t in range(head_tiles(width)):
-        lanes = min(LANES, width - t * LANES)
-        out[at + t * cut : at + (t + 1) * cut, :lanes] = head_ref[
-            mine, t * LANES : t * LANES + lanes
-        ]
+MOD_ROWS = 16
 
 
 def put_modulation(out, at, row):
@@ -164,99 +153,158 @@
         + [jnp.zeros((8 - tiles, LANES), jnp.float32)][: 8 - tiles],
         axis=0,
     )
-    terms = []
-    for _ in range(3):
-        term = left.astype(jnp.bfloat16).astype(jnp.float32)
-        terms.append(term)
-        left = left - term
-    terms.append(jnp.zeros_like(left))
-    out[at : at + MOD_ROWS, :] = jnp.concatenate(terms, axis=0).astype(jnp.bfloat16)
+    high = left.astype(jnp.bfloat16)
+    low = (left - high.astype(jnp.float32)).astype(jnp.bfloat16)
+    out[at : at + MOD_ROWS, :] = jnp.concatenate([high, low], axis=0)
 
 
 def get_modulation(ref, at, width):
     terms = ref[at : at + MOD_ROWS, :].astype(jnp.float32)
-    total = terms[0:8] + terms[8:16] + terms[16:24]
+    total = terms[0:8] + terms[8:16]
     tiles = -(-width // LANES)
     return jnp.concatenate([total[t : t + 1] for t in range(tiles)], axis=1)[:, :width]
 
 
-def near_extra(count):
-    return [(r not in (0, count // 2), r != 0) for r in range(count)]
-
-
-def far_extra(count):
-    return [(r == count // 2, False) for r in range(count)]
-
-
-def split_kernel(width, flip, extra, place_ref, half_ref, group_ref, x_ref, *refs):
-    count = len(extra)
-    head_ref, refs = refs[0], refs[1:]
-    if not flip:
-        mod_ref, refs = refs[0], refs[1:]
+def cut_window(width, held, out, r, odd):
+    rows = held.shape[1]
+    whole = width // LANES
+    last = slice(whole * rows, rows * width // LANES)
+
+    @pl.when(jnp.logical_not(odd))
+    def _():
+        for t in range(whole):
+            out[t * rows : (t + 1) * rows, :] = held[r, :, t * LANES : (t + 1) * LANES]
+        out[last, :] = pack_half(held[r, :, whole * LANES :])
+
+    @pl.when(odd)
+    def _():
+        lane = lax.broadcasted_iota(jnp.int32, (rows, LANES), 1)
+        turned = [turn(held[r, :, t * LANES : (t + 1) * LANES]) for t in range(whole + 1)]
+        for t in range(whole):
+            out[t * rows : (t + 1) * rows, :] = jnp.where(
+                lane < LANES // 2, turned[t], turned[t + 1]
+            ).astype(jnp.bfloat16)
+        out[last, :] = pack_half(turned[whole])
+
+
+def windows(x_ref, held, sems, me, half, count, width):
+    span = held.shape[2]
+
+    def window(r):
+        start = half * (count * width) + lax.div((me ^ r) * width, LANES) * LANES
+        return pltpu.make_async_copy(
+            x_ref.at[:, pl.ds(pl.multiple_of(start, LANES), span)], held.at[r], sems.at[r]
+        )
+
+    return [window(r) for r in range(count)]
+
+
+def sigma_row(step):
+    unit_time = jnp.full((1, LANES), step, jnp.int32).astype(jnp.float32) / 1000.0
+    return 5.0 * unit_time / (1.0 + 4.0 * unit_time)
+
+
+def far_kernel(width, count, place_ref, half_ref, group_ref, when_ref, x_ref, head_ref, *refs):
+    outs, refs = refs[:count], refs[count:]
+    pack_ref, clock_ref, held, head_held, steps_ref, sems, head_sem, steps_sem = refs
+    me = place_ref[0]
+    cut, columns = head_held.shape
+    order = [count // 2] + [r for r in range(count - 1, -1, -1) if r != count // 2]
+    copies = windows(x_ref, held, sems, me, 1 - half_ref[0], count, width)
+    head_copy = pltpu.make_async_copy(
+        head_ref.at[pl.ds(pl.multiple_of(group_ref[0] * cut, cut), cut), :], head_held, head_sem
+    )
+    steps_copy = pltpu.make_async_copy(when_ref, steps_ref, steps_sem)
+    copies[order[0]].start()
+    steps_copy.start()
+    head_copy.start()
+    for r in order[1:]:
+        copies[r].start()
+    packed = outs[0].shape[0]
+    for r in order:
+        copies[r].wait()
+        cut_window(width, held, outs[r], r, lax.rem(me ^ r, 2) == 1)
+    head_copy.wait()
+    for t in range(head_tiles(columns)):
+        tile = head_held[:, t * LANES : min((t + 1) * LANES, columns)]
+        if tile.shape[1] < LANES:
+            fill = jnp.zeros((cut, LANES - tile.shape[1]), tile.dtype)
+            tile = jnp.concatenate([tile, fill], axis=1)
+        pack_ref[t * cut : (t + 1) * cut, :] = tile
+        for r in range(1, count):
+            outs[r][packed + t * cut : packed + (t + 1) * cut, :] = tile
+    steps_copy.wait()
+    now = jnp.full((1, LANES), steps_ref[0, 0], jnp.int32).astype(jnp.float32)
+    change = sigma_row(steps_ref[0, 1]) - sigma_row(steps_ref[0, 0])
+    clock_ref[...] = jnp.concatenate([now, change])
+
+
+def split_far(x, head, steps, scalars, count, halves):
+    rows, columns = x.shape
+    width = columns // halves // count
+    cut = head.shape[0] // 2
+    span = cut * head_tiles(head.shape[1])
+    length = rows * width // LANES
+    pieces = [
+        jax.ShapeDtypeStruct((length + span * (r != 0), LANES), jnp.bfloat16)
+        for r in range(count)
+    ]
+    results = pl.pallas_call(
+        functools.partial(far_kernel, width, count),
+        in_specs=[pl.BlockSpec(memory_space=pltpu.SMEM)] * 3
+        + [pl.BlockSpec(memory_space=pltpu.HBM)] * 3,
+        out_shape=pieces
+        + [
+            jax.ShapeDtypeStruct((span, LANES), jnp.bfloat16),
+            jax.ShapeDtypeStruct((2, LANES), jnp.float32),
+        ],
+        scratch_shapes=[
+            pltpu.VMEM((count, rows, (width // LANES + 1) * LANES), jnp.bfloat16),
+            pltpu.VMEM((cut, head.shape[1]), jnp.bfloat16),
+            pltpu.SMEM((1, 2), jnp.int32),
+            pltpu.SemaphoreType.DMA((count,)),
+            pltpu.SemaphoreType.DMA,
+            pltpu.SemaphoreType.DMA,
+        ],
+        compiler_params=pltpu.CompilerParams(vmem_limit_bytes=4 << 20),
+        cost_estimate=pl.CostEstimate(
+            flops=0, transcendentals=0, bytes_accessed=4 * rows * columns // halves
+        ),
+        name="split_far",
+    )(
+        *scalars,
+        pltpu.with_memory_space_constraint(steps, pltpu.HBM),
+        pltpu.with_memory_space_constraint(x, pltpu.HBM),
+        pltpu.with_memory_space_constraint(head, pltpu.HBM),
+    )
+    return results[:count], results[count], results[count + 1]
+
+
+def near_kernel(width, count, place_ref, half_ref, x_ref, mod_ref, *refs):
     outs, held, sems = refs[:count], refs[count], refs[count + 1]
-    rows = x_ref.shape[0]
-    whole = width // LANES
     me = place_ref[0]
-    half = 1 - half_ref[0] if flip else half_ref[0]
-    base = half * (count * width)
-
-    def window(r):
-        to = me ^ r
-        start = pl.multiple_of(base + lax.div(to * width, LANES) * LANES, LANES)
-        return pltpu.make_async_copy(
-            x_ref.at[:, pl.ds(start, (whole + 1) * LANES)], held.at[r], sems.at[r]
-        )
-
-    order = [r for r in range(count) if r != 0] + [0]
-    for r in order:
-        window(r).start()
-    packed = rows * width // LANES
-    for r in order:
-        at = packed
-        if extra[r][0]:
-            put_head(outs[r], at, head_ref, group_ref)
-            at += head_ref.shape[0] // 2 * head_tiles(head_ref.shape[1])
-        if extra[r][1]:
-            put_modulation(outs[r], at, mod_ref[0:1, :])
-    for r in order:
-        window(r).wait()
-        odd = lax.rem(me ^ r, 2) == 1
-        last = slice(whole * rows, packed)
-
-        @pl.when(jnp.logical_not(odd))
-        def _():
-            for t in range(whole):
-                outs[r][t * rows : (t + 1) * rows, :] = held[r, :, t * LANES : (t + 1) * LANES]
-            outs[r][last, :] = pack_half(held[r, :, whole * LANES :])
-
-        @pl.when(odd)
-        def _():
-            lane = lax.broadcasted_iota(jnp.int32, (rows, LANES), 1)
-            turned = [turn(held[r, :, t * LANES : (t + 1) * LANES]) for t in range(whole + 1)]
-            for t in range(whole):
-                outs[r][t * rows : (t + 1) * rows, :] = jnp.where(
-                    lane < LANES // 2, turned[t], turned[t + 1]
-                ).astype(jnp.bfloat16)
-            outs[r][last, :] = pack_half(turned[whole])
-
-
-def split_heads(x, flip, extra, scalars, riders, halves):
+    copies = windows(x_ref, held, sems, me, half_ref[0], count, width)
+    for r in range(count - 1, -1, -1):
+        copies[r].start()
+    for r in range(1, count):
+        put_modulation(outs[r], outs[0].shape[0], mod_ref[0:1, :])
+    for r in range(count - 1, -1, -1):
+        copies[r].wait()
+        cut_window(width, held, outs[r], r, lax.rem(me ^ r, 2) == 1)
+
+
+def split_near(x, modulation, scalars, count, halves):
     rows, columns = x.shape
-    count = len(extra)
     width = columns // halves // count
-    head = riders[0]
-    pieces = []
-    for with_head, with_mod in extra:
-        length = rows * width // LANES
-        length += head.shape[0] // 2 * head_tiles(head.shape[1]) * with_head
-        length += MOD_ROWS * with_mod
-        pieces.append(jax.ShapeDtypeStruct((length, LANES), jnp.bfloat16))
+    length = rows * width // LANES
     return pl.pallas_call(
-        functools.partial(split_kernel, width, flip, extra),
-        in_specs=[pl.BlockSpec(memory_space=pltpu.SMEM)] * 3
-        + [pl.BlockSpec(memory_space=pltpu.HBM)]
-        + [pl.BlockSpec(memory_space=pltpu.VMEM)] * len(riders),
-        out_shape=pieces,
+        functools.partial(near_kernel, width, count),
+        in_specs=[pl.BlockSpec(memory_space=pltpu.SMEM)] * 2
+        + [pl.BlockSpec(memory_space=pltpu.HBM), pl.BlockSpec(memory_space=pltpu.VMEM)],
+        out_shape=[
+            jax.ShapeDtypeStruct((length + MOD_ROWS * (r != 0), LANES), jnp.bfloat16)
+            for r in range(count)
+        ],
         scratch_shapes=[
             pltpu.VMEM((count, rows, (width // LANES + 1) * LANES), jnp.bfloat16),
             pltpu.SemaphoreType.DMA((count,)),
@@ -265,8 +313,8 @@
         cost_estimate=pl.CostEstimate(
             flops=0, transcendentals=0, bytes_accessed=4 * rows * columns // halves
         ),
-        name="split_heads",
-    )(*scalars, pltpu.with_memory_space_constraint(x, pltpu.HBM), *riders)
+        name="split_near",
+    )(*scalars[:2], pltpu.with_memory_space_constraint(x, pltpu.HBM), modulation)
 
 
 def load_kernel(count, place_ref, w_ref, out_ref, sems):
@@ -326,12 +374,14 @@
         query, key, value = (columns(start + i * HEAD) for i in range(3))
         scores = lax.dot_general(
             query, key, (((1,), (1,)), ((), ())), preferred_element_type=jnp.float32
-        ) * HEAD ** (-0.5)
+        )
         row_max = jnp.max(scores, axis=-1, keepdims=True)
-        exp_scores = jnp.exp(scores - row_max)
+        exp_scores = jnp.exp2((scores - row_max) * (HEAD ** (-0.5) / math.log(2.0)))
         row_sum = jnp.sum(exp_scores, axis=-1, keepdims=True)
-        weights = (exp_scores / row_sum).astype(jnp.bfloat16)
-        results.append(jnp.dot(weights, value, preferred_element_type=jnp.float32))
+        summed = jnp.dot(
+            exp_scores.astype(jnp.bfloat16), value, preferred_element_type=jnp.float32
+        )
+        results.append(summed / row_sum)
     attended = jnp.concatenate(results, axis=1).astype(jnp.bfloat16)
     whole = heads * HEAD // LANES
     for b in range(count):
@@ -344,21 +394,16 @@
             [rest[: rows // 2], rest[rows // 2 :]], axis=1
         ).astype(jnp.bfloat16)
         if riders:
-            group_ref, head_ref, mod_ref = riders
-            put_head(outs[b], packed, head_ref, group_ref)
-            packed += head_ref.shape[0] // 2 * head_tiles(head_ref.shape[1])
-            put_modulation(outs[b], packed, mod_ref[1:2, :])
+            put_modulation(outs[b], packed, riders[0][1:2, :])
 
 
 def attend_packed(pieces, heads, rows, riders=()):
     count = len(pieces)
     total = count * rows
     length = rows * heads * HEAD // LANES
-    specs = [pl.BlockSpec(memory_space=pltpu.VMEM)] * count
+    specs = [pl.BlockSpec(memory_space=pltpu.VMEM)] * (count + len(riders))
     if riders:
-        head = riders[1]
-        length += head.shape[0] // 2 * head_tiles(head.shape[1]) + MOD_ROWS
-        specs = [pl.BlockSpec(memory_space=pltpu.SMEM)] + specs + specs[:2]
+        length += MOD_ROWS
     out = jax.ShapeDtypeStruct((length, LANES), jnp.bfloat16)
     return pl.pallas_call(
         functools.partial(attend_kernel, heads, rows, count),
@@ -406,10 +451,10 @@
     )(pltpu.with_memory_space_constraint(weight, pltpu.VMEM), *pieces)
 
 
-def finish_kernel(rows, count, size_ref, w_ref, *refs):
+def finish_kernel(rows, count, w_ref, *refs):
     pieces, refs = refs[:count], refs[count:]
-    mod_ref, far_ref, hidden_ref, head_ref, latent_ref, out_ref, step_ref = refs[:7]
-    acc_ref, left_ref, turn_ref = refs[7:]
+    mod_ref, far_ref, hidden_ref, head_ref, latent_ref, clock_ref = refs[:6]
+    out_ref, step_ref, acc_ref, left_ref, turn_ref = refs[6:]
     steps, _, tile = acc_ref.shape
     dim = steps * tile
 
@@ -451,21 +496,20 @@
         axis=1,
     )
     out_ref[...] = paired
-    step_ref[...] = latent_ref[...] + size_ref[0] * paired
-
-
-def finish(pieces, weight, far, hidden, lines, head_rows, latent, size, rows):
+    step_ref[...] = latent_ref[...] + clock_ref[1:2, :] * paired
+
+
+def finish(pieces, weight, far, hidden, lines, head_rows, latent, clock, rows):
     depth, dim = weight.shape
     count = len(pieces)
     tile = math.gcd(dim, lines.shape[2])
     patch = head_rows.shape[0]
     inputs = (pltpu.with_memory_space_constraint(weight, pltpu.VMEM), *pieces, lines)
-    inputs += (far, hidden, head_rows, latent)
+    inputs += (far, hidden, head_rows, latent, clock)
     result = jax.ShapeDtypeStruct((rows // 2, 2 * patch), jnp.float32)
     return pl.pallas_call(
         functools.partial(finish_kernel, rows, count),
-        in_specs=[pl.BlockSpec(memory_space=pltpu.SMEM)]
-        + [pl.BlockSpec(memory_space=pltpu.VMEM)] * len(inputs),
+        in_specs=[pl.BlockSpec(memory_space=pltpu.VMEM)] * len(inputs),
         out_shape=[result] * 2,
         scratch_shapes=[
             pltpu.VMEM((dim // tile, rows, tile), jnp.float32),
@@ -477,36 +521,31 @@
             flops=2 * rows * depth * dim, transcendentals=0, bytes_accessed=2 * depth * dim
         ),
         name="finish",
-    )(size, *inputs)
-
-
-def collect_kernel(count, packed, done, group_ref, head_ref, *refs):
-    queries, far, out_ref = refs[:count], refs[count:-1], refs[-1]
-    span = out_ref.shape[0] // (2 * count)
-    put_head(out_ref, 0, head_ref, group_ref)
-    for r in range(1, count):
-        out_ref[r * span : (r + 1) * span, :] = queries[r][packed : packed + span, :]
-    for r in range(count):
-        out_ref[(count + r) * span : (count + r + 1) * span, :] = far[r][done : done + span, :]
-
-
-def collect_head(queries, far, head, group, packed, done):
-    count = len(far)
-    span = head.shape[0] // 2 * head_tiles(head.shape[1])
+    )(*inputs)
+
+
+def collect_kernel(start, *refs):
+    out_ref = refs[-1]
+    span = out_ref.shape[0] // (len(refs) - 1)
+    for r, ref in enumerate(refs[:-1]):
+        at = ref.shape[0] - span if start is None or r == 0 else start
+        out_ref[r * span : (r + 1) * span, :] = ref[at : at + span, :]
+
+
+def collect(pieces, span, start=None):
     return pl.pallas_call(
-        functools.partial(collect_kernel, count, packed, done),
-        in_specs=[pl.BlockSpec(memory_space=pltpu.SMEM)]
-        + [pl.BlockSpec(memory_space=pltpu.VMEM)] * (1 + 2 * count),
-        out_shape=jax.ShapeDtypeStruct((2 * count * span, LANES), jnp.bfloat16),
+        functools.partial(collect_kernel, start),
+        in_specs=[pl.BlockSpec(memory_space=pltpu.VMEM)] * len(pieces),
+        out_shape=jax.ShapeDtypeStruct((len(pieces) * span, LANES), jnp.bfloat16),
         compiler_params=pltpu.CompilerParams(vmem_limit_bytes=4 << 20),
         cost_estimate=pl.CostEstimate(
-            flops=0, transcendentals=0, bytes_accessed=8 * count * span * LANES
-        ),
-        name="collect_head",
-    )(group, head, *queries, *far)
-
-
-def arrange_kernel(count, width, near_at, done, place_ref, half_ref, group_ref, *refs):
+            flops=0, transcendentals=0, bytes_accessed=4 * len(pieces) * span * LANES
+        ),
+        name="collect",
+    )(*pieces)
+
+
+def arrange_kernel(count, width, packed, done, place_ref, half_ref, group_ref, *refs):
     mine_ref, up_ref, mod_ref = refs[:3]
     near, far = refs[3 : 3 + count], refs[3 + count : -2]
     head_out, mod_out = refs[-2:]
@@ -534,19 +573,19 @@
         head_out[:, pl.ds(start, 2 * width)] = jnp.concatenate(
             [jnp.where(first, own, other), jnp.where(first, other, own)], axis=1
         )
-        own = mod_ref[0:1, :] if r == 0 else get_modulation(near[r], near_at[r], columns)
-        other = get_modulation(far[r], done + span, columns)
+        own = mod_ref[0:1, :] if r == 0 else get_modulation(near[r], packed, columns)
+        other = get_modulation(far[r], done, columns)
         mod_out[owner] = jnp.concatenate(
             [jnp.where(first, own, other), jnp.where(first, other, own)], axis=1
         )
 
 
-def arrange(mine, up, modulation, near, far, head, scalars, near_at, done):
+def arrange(mine, up, modulation, near, far, head, scalars, packed, done):
     count = len(far)
     patch, width = head.shape
     columns = modulation.shape[1]
     return pl.pallas_call(
-        functools.partial(arrange_kernel, count, width, near_at, done),
+        functools.partial(arrange_kernel, count, width, packed, done),
         in_specs=[pl.BlockSpec(memory_space=pltpu.SMEM)] * 3
         + [pl.BlockSpec(memory_space=pltpu.VMEM)] * (3 + 2 * count),
         out_shape=[
@@ -590,34 +629,35 @@
     side = half[None].astype(jnp.int32)
     level = group[None].astype(jnp.int32)
     scalars = (here, side, level)
-    far_rides, near_rides = far_extra(count), near_extra(count)
-
-    far_sent = split_heads(x, True, far_rides, scalars, (head,), halves)
+    far_sent, pack, clock = split_far(x, head, timesteps.reshape(1, 2), scalars, count, halves)
     far_pieces = [far_sent[0]] + [along(far_sent[r], r) for r in range(1, count)]
 
     other_steps = swap(timesteps, "fsdp")
-    steps_both = jnp.concatenate([timesteps[0, :, 0], other_steps[0, :, 0]])
-    embedding = time_embed(steps_both).astype(jnp.bfloat16)
+    freqs = jnp.exp(
+        -math.log(10000.0) * jnp.arange(FREQ // 2, dtype=jnp.float32) / (FREQ // 2)
+    )
+    angle = jnp.concatenate([clock[:1], jnp.full((1, LANES), other_steps[0, 0, 0], jnp.float32)])
+    angle = angle * freqs
+    embedding = jnp.concatenate([jnp.cos(angle), jnp.sin(angle)], axis=-1).astype(jnp.bfloat16)
     modulation = jnp.dot(embedding, time_weight[0], preferred_element_type=jnp.float32)
-    step_size = sigma_of(timesteps[0, :, 1]) - sigma_of(timesteps[0, :, 0])
-
-    near_sent = split_heads(x, False, near_rides, scalars, (head, modulation), halves)
+
+    near_sent = split_near(x, modulation, scalars, count, halves)
     near_pieces = [near_sent[0]] + [along(near_sent[r], r) for r in range(1, count)]
 
     weight = load_rows(out_weight[0], here, count)
-    far_attended = attend_packed(far_pieces, heads, rows, (level, head, modulation))
+    far_attended = attend_packed(far_pieces, heads, rows, (modulation,))
     far_home = [slanted(far_attended[r], r) for r in range(count)]
     partial = project_packed(far_home, weight, rows)
     partial = swap(partial, "fsdp")
 
     packed = far_sent[0].shape[0]
-    done = far_home[0].shape[0] - span - MOD_ROWS
-    queries = [far_pieces[r] if far_rides[r][0] else near_pieces[r] for r in range(count)]
-    near_at = [packed + span * with_head for with_head, _ in near_rides]
-    mine = collect_head(queries, far_home, head, level, packed, done)
+    done = far_home[0].shape[0] - MOD_ROWS
+    line = collect([pack] + far_pieces[1:], span, packed)
+    other = swap(line, "fsdp")
+    mine = collect([line, other], line.shape[0])
     up = swap(mine, "grp")
     head_rows, lines = arrange(
-        mine, up, modulation, near_pieces, far_home, head, scalars, near_at, done
+        mine, up, modulation, near_pieces, far_home, head, scalars, packed, done
     )
 
     near_attended = attend_packed(near_pieces, heads, rows)
@@ -631,7 +671,7 @@
         lines,
         head_rows,
         latent.reshape(rows // 2, 2 * PATCH),
-        step_size,
+        clock,
         rows,
     )
     carried = partner(stepped, "section", 0)
@@ -644,6 +684,8 @@
     return (
         head_shape[1] == 1
         and halves == 2
+        and FREQ == 2 * LANES
+        and 2 * PATCH == LANES
         and mesh.shape["grp"] == 2
         and count & (count - 1) == 0
         and HEADS % (halves * count) == 0

time: 67.5 us -> 70.7 us (1.047)
  waiting for transfers between devices: 21.7 us -> 28.9 us
  local copies, waits for them, and re-layouts: 3.55 us -> 0.63 us
  between operations: 2.18 us -> 0.82 us
  starting transfers between devices: 25.6 us -> 26.9 us
  Pallas kernels: 13 us -> 12.2 us
    ppermute x3 -> x4, waiting for transfers between devices: 0.01 us -> 6.97 us  [swap(): return lax.ppermute(block, axis, [(0, 1), (1, 0)])]
    ppermute x4, waiting for transfers between devices: 0.01 us -> 1.71 us  [slanted(): return lax.ppermute(block, ('seq', 'fsdp'), route)]
    unnamed x13 -> x7, local copies, waits for them, and re-layouts: 2.23 us -> 0.63 us
    ppermute x3 -> x4, starting transfers between devices: 5.22 us -> 6.76 us  [swap(): return lax.ppermute(block, axis, [(0, 1), (1, 0)])]
    ppermute x9, waiting for transfers between devices: 20.5 us -> 19 us  [along(): return lax.ppermute(block, 'seq', [(i, i ^ r) for i in range(count)])]
    slice x1 -> x0, local copies, waits for them, and re-layouts: 1.32 us -> none  [packed_body(): step_size = sigma_of(timesteps[0, :, 1]) - sigma_of(timesteps[0, :, 0])]
    pallas_call x2, Pallas kernels: 3.45 us -> 2.67 us  [attend_packed(): pl.pallas_call(functools.partial(attend_kernel, heads, rows, count), in_s...]
    convert_element_type x1 -> x0, other arithmetic: 0.76 us -> none  [time_embed(): angle = steps_now.astype(jnp.float32)[..., None] * freqs]
  transfers between devices with their start and end apart: 17 -> 18, of which waited for: 7 -> 9; matrix products, arithmetic and copies ran while one was open for 4% -> 1% of each run, Pallas kernels for 13% -> 10%
where the time goes in v2:
time: 70.7 us; the launch traced here: 70.5 us
  waiting for transfers between devices  28.9 us (41%)
  starting transfers between devices  26.9 us (38%)
  Pallas kernels  12.2 us (17%)
  other arithmetic  0.82 us (1%)
  between operations  0.82 us (1%)
    ppermute x9, waiting for transfers between devices, along(): return lax.ppermute(block, 'seq', [(i, i ^ r) for i in range(count)])  19 us
    ppermute x9, starting transfers between devices, along(): return lax.ppermute(block, 'seq', [(i, i ^ r) for i in range(count)])  13.4 us
    ppermute x4, waiting for transfers between devices, swap(): return lax.ppermute(block, axis, [(0, 1), (1, 0)])  6.97 us
    ppermute x4, starting transfers between devices, slanted(): return lax.ppermute(block, ('seq', 'fsdp'), route)  6.81 us
    ppermute x4, starting transfers between devices, swap(): return lax.ppermute(block, axis, [(0, 1), (1, 0)])  6.76 us
    pallas_call x1, Pallas kernels, load_rows(): pl.pallas_call(functools.partial(load_kernel, count), in_specs=[pl.BlockS...  2.95 us
    pallas_call x2, Pallas kernels, attend_packed(): pl.pallas_call(functools.partial(attend_kernel, heads, rows, count), in_s...  2.67 us
    pallas_call x1, Pallas kernels, finish(): pl.pallas_call(functools.partial(finish_kernel, rows, count), in_specs=[p...  2.34 us
  transfers between devices with their start and end apart: 18, of which 9 were waited for; matrix products, arithmetic and copies ran while one was open for 1% of the time, Pallas kernels for 10%

profile of v2, /device:TPU:0, one launch (start us, length us, event | category | flops | bytes accessed | tf_op | source)
XLA Modules:
  0.0 70.5 jit_solution(3702382201785516604)
XLA Ops:
  0.6 3.0 %collective-permute-start = (s32[1,1,2]{2,1,0:T(1,128)}, s32[1,1,2]{2,1,0:T(1,128)S(1)}, u32[]{:S(2)}, u32[]{:S(2)}) collective-permute-start(s32[1,1,2]{2,1,0:T(1,128)} %param.13), channel_id=1, source_target_pairs={{0,1},{1,0},{2,3},{3,2},{4,5},{5,4},{6,7},{7,6},{8,9},{9,8},{10,11... | collective-permute-start | bytes 32 | tf_op jit(solution)/shard_map/ppermute | solution.py:616
  3.7 1.4 %split_far.1 = (bf16[480,128]{1,0:T(8,128)(2,1)S(1)}, bf16[576,128]{1,0:T(8,128)(2,1)S(1)}, bf16[576,128]{1,0:T(8,128)(2,1)S(1)}, bf16[576,128]{1,0:T(8,128)(2,1...) custom-call(s32[1]{0:T(128)} %bitcast.place_ref, s32[1]{0:T(128)} %bitcast.2.half_ref, s32[1]{0:T(128)} %bitcast.4.group_ref, ...), custom_call_target="tpu_custom_call" | custom-call | bytes 983040 | tf_op jit(solution)/shard_map/split_far/pallas_call | solution.py:252
  5.1 1.6 %collective-permute-start.7 = (bf16[576,128]{1,0:T(8,128)(2,1)S(1)}, bf16[576,128]{1,0:T(8,128)(2,1)S(1)}, u32[]{:S(2)}, u32[]{:S(2)}) collective-permute-start(bf16[576,128]{1,0:T(8,128)(2,1)S(1)} %get-tuple-element.34), channel_id=1, source_target_pairs={{0,2},{2,0},{4,6},{6,4},{1,3},{3,1},{5,7},{7,5},{8,10},{10,8},{12,... | collective-permute-start | bytes 442376 | tf_op jit(solution)/shard_map/ppermute | solution.py:613
  6.8 2.6 %collective-permute-start.8 = (bf16[576,128]{1,0:T(8,128)(2,1)S(1)}, bf16[576,128]{1,0:T(8,128)(2,1)S(1)}, u32[]{:S(2)}, u32[]{:S(2)}) collective-permute-start(bf16[576,128]{1,0:T(8,128)(2,1)S(1)} %get-tuple-element.35), channel_id=1, source_target_pairs={{0,4},{2,6},{4,0},{6,2},{1,5},{3,7},{5,1},{7,3},{8,12},{10,14},{12... | collective-permute-start | bytes 442376 | tf_op jit(solution)/shard_map/ppermute | solution.py:613
  9.6 0.8 %cosine_convert_fusion = (bf16[2,128]{1,0:T(2,128)(2,1)S(1)}, f32[2,128]{1,0:T(2,128)S(1)}) fusion(f32[128]{0:T(128)S(1)} %multiply_exponential_fusion, f32[2,128]{1,0:T(2,128)S(1)} %get-tuple-element.24.refs_9_, f32[]{:T(128)} %bitcast.8, pred[2]{0:T(512)(128)(4,1)} %constant.16.clone.1), kind=kLoop, calls=%fused_computation.6 | loop fusion | flops 768 | bytes 3078 | tf_op jit(solution)/shard_map/convert | solution.py:730
  10.7 1.7 %collective-permute-done.7.refs_1_.refs_2_ = bf16[576,128]{1,0:T(8,128)(2,1)S(1)} collective-permute-done((bf16[576,128]{1,0:T(8,128)(2,1)S(1)}, bf16[576,128]{1,0:T(8,128)(2,1)S(1)}, u32[]{:S(2)}, u32[]{:S(2)}) %collective-permute-start.7) | collective-permute-done | bytes 147488 | tf_op jit(solution)/shard_map/ppermute | solution.py:613
  12.4 8.3 %collective-permute-done.8.refs_2_.refs_3_ = bf16[576,128]{1,0:T(8,128)(2,1)S(1)} collective-permute-done((bf16[576,128]{1,0:T(8,128)(2,1)S(1)}, bf16[576,128]{1,0:T(8,128)(2,1)S(1)}, u32[]{:S(2)}, u32[]{:S(2)}) %collective-permute-start.8) | collective-permute-done | bytes 147488 | tf_op jit(solution)/shard_map/ppermute | solution.py:613
  20.6 1.3 %attend_packed.3 = (bf16[176,128]{1,0:T(8,128)(2,1)S(1)}, bf16[176,128]{1,0:T(8,128)(2,1)S(1)}, bf16[176,128]{1,0:T(8,128)(2,1)S(1)}, bf16[176,128]{1,0:T(8,128)(2,1)S(1)}) custom-call(f32[2,960]{1,0:T(2,128)S(1)} %fusion.mod_ref.refs_0_.refs_2_, bf16[480,128]{1,0:T(8,128)(2,1)S(1)} %get-tuple-element.37.refs_1_, ...), custom_call_target="tpu_custom_call" | custom-call | flops 83886080 | bytes 655360 | tf_op jit(solution)/shard_map/attend_packed/pallas_call | solution.py:408
  22.6 3.1 %collective-permute-start.13 = (bf16[176,128]{1,0:T(8,128)(2,1)S(1)}, bf16[176,128]{1,0:T(8,128)(2,1)S(1)}, u32[]{:S(2)}, u32[]{:S(2)}) collective-permute-start(bf16[176,128]{1,0:T(8,128)(2,1)S(1)} %get-tuple-element.39), channel_id=1, source_target_pairs={{0,3},{1,2},{2,1},{3,0},{4,7},{5,6},{6,5},{7,4},{8,11},{9,10},{10,... | collective-permute-start | bytes 135176 | tf_op jit(solution)/shard_map/ppermute | solution.py:623
  25.7 1.0 %collective-permute-start.14 = (bf16[176,128]{1,0:T(8,128)(2,1)S(1)}, bf16[176,128]{1,0:T(8,128)(2,1)S(1)}, u32[]{:S(2)}, u32[]{:S(2)}) collective-permute-start(bf16[176,128]{1,0:T(8,128)(2,1)S(1)} %get-tuple-element.40), channel_id=1, source_target_pairs={{0,5},{1,4},{2,7},{3,6},{4,1},{5,0},{6,3},{7,2},{8,13},{9,12},{10,... | collective-permute-start | bytes 135176 | tf_op jit(solution)/shard_map/ppermute | solution.py:623
  26.7 2.1 %collective-permute-start.15 = (bf16[176,128]{1,0:T(8,128)(2,1)S(1)}, bf16[176,128]{1,0:T(8,128)(2,1)S(1)}, u32[]{:S(2)}, u32[]{:S(2)}) collective-permute-start(bf16[176,128]{1,0:T(8,128)(2,1)S(1)} %get-tuple-element.41), channel_id=1, source_target_pairs={{0,7},{1,6},{2,5},{3,4},{4,3},{5,2},{6,1},{7,0},{8,15},{9,14},{10,... | collective-permute-start | bytes 135176 | tf_op jit(solution)/shard_map/ppermute | solution.py:623
  28.8 2.9 %load_rows.1.w_ref = bf16[1280,2560]{1,0:T(8,128)(2,1)S(1)} custom-call(s32[1]{0:T(128)} %bitcast.place_ref, bf16[1280,2560]{1,0:T(8,128)(2,1)} %bitcast.20), custom_call_target="tpu_custom_call" | custom-call | bytes 13107200 | tf_op jit(solution)/shard_map/load_rows/pallas_call | solution.py:338
  31.8 1.7 %collective-permute-done.15.refs_10_.refs_3_ = bf16[176,128]{1,0:T(8,128)(2,1)S(1)} collective-permute-done((bf16[176,128]{1,0:T(8,128)(2,1)S(1)}, bf16[176,128]{1,0:T(8,128)(2,1)S(1)}, u32[]{:S(2)}, u32[]{:S(2)}) %collective-permute-start.15) | collective-permute-done | bytes 45088 | tf_op jit(solution)/shard_map/ppermute | solution.py:623
  33.5 1.3 %project_packed.1 = bf16[64,2560]{1,0:T(8,128)(2,1)S(1)} custom-call(bf16[1280,2560]{1,0:T(8,128)(2,1)S(1)} %load_rows.1.w_ref, bf16[176,128]{1,0:T(8,128)(2,1)S(1)} %collective-permute-done.12.refs_7_.refs_0_, bf16[176,128]{1,0:T(8,128)(2,1)S(1)} %collective-permute-done.13.refs_8_.refs_1_, bf16[176,128]{1,0:T(8,128)(2,1)S(1)} %collective-permute-done.14.refs_9_.refs_2_, ...), custom_call_target="tpu_custom_call" | custom-call | flops 419430400 | bytes 6553600 | tf_op jit(solution)/shard_map/project_packed/pallas_call | solution.py:442
  34.8 1.1 %collective-permute-start.16 = (bf16[64,2560]{1,0:T(8,128)(2,1)S(1)}, bf16[64,2560]{1,0:T(8,128)(2,1)S(1)}, u32[]{:S(2)}, u32[]{:S(2)}) collective-permute-start(bf16[64,2560]{1,0:T(8,128)(2,1)S(1)} %project_packed.1), channel_id=1, source_target_pairs={{0,1},{1,0},{2,3},{3,2},{4,5},{5,4},{6,7},{7,6},{8,9},{9,8},{10,11... | collective-permute-start | bytes 983048 | tf_op jit(solution)/shard_map/ppermute | solution.py:616
  35.9 1.1 %collective-permute-start.10 = (bf16[384,128]{1,0:T(8,128)(2,1)S(1)}, bf16[384,128]{1,0:T(8,128)(2,1)S(1)}, u32[]{:S(2)}, u32[]{:S(2)}) collective-permute-start(bf16[384,128]{1,0:T(8,128)(2,1)S(1)} %collect.2.refs_0_), channel_id=1, source_target_pairs={{0,1},{1,0},{2,3},{3,2},{4,5},{5,4},{6,7},{7,6},{8,9},{9,8},{10,11... | collective-permute-start | bytes 294920 | tf_op jit(solution)/shard_map/ppermute | solution.py:616
  37.0 7.0 %collective-permute-done.10.refs_1_ = bf16[384,128]{1,0:T(8,128)(2,1)S(1)} collective-permute-done((bf16[384,128]{1,0:T(8,128)(2,1)S(1)}, bf16[384,128]{1,0:T(8,128)(2,1)S(1)}, u32[]{:S(2)}, u32[]{:S(2)}) %collective-permute-start.10) | collective-permute-done | bytes 98336 | tf_op jit(solution)/shard_map/ppermute | solution.py:616
  43.9 1.6 %collective-permute-start.11 = (bf16[768,128]{1,0:T(8,128)(2,1)S(1)}, bf16[768,128]{1,0:T(8,128)(2,1)S(1)}, u32[]{:S(2)}, u32[]{:S(2)}) collective-permute-start(bf16[768,128]{1,0:T(8,128)(2,1)S(1)} %collect.3.refs_0_), channel_id=1, source_target_pairs={{0,16},{16,0},{1,17},{17,1},{2,18},{18,2},{3,19},{19,3},{4,20},{20... | collective-permute-start | bytes 589832 | tf_op jit(solution)/shard_map/ppermute | solution.py:616
  45.5 1.4 %split_near.1 = (bf16[480,128]{1,0:T(8,128)(2,1)S(1)}, bf16[496,128]{1,0:T(8,128)(2,1)S(1)}, bf16[496,128]{1,0:T(8,128)(2,1)S(1)}, bf16[496,128]{1,0:T(8,128)(2,1)S(1)}) custom-call(s32[1]{0:T(128)} %bitcast.place_ref, s32[1]{0:T(128)} %bitcast.2.half_ref, bf16[64,7680]{1,0:T(8,128)(2,1)} %bitcast.22, f32[2,960]{1,0:T(2,128)S(1)} %fusion.mod_ref.refs_0_.refs_2_), custom_call_target="tpu_custom_call" | custom-call | bytes 983040 | tf_op jit(solution)/shard_map/split_near/pallas_call | solution.py:300
  47.3 1.5 %collective-permute-start.2 = (bf16[496,128]{1,0:T(8,128)(2,1)S(1)}, bf16[496,128]{1,0:T(8,128)(2,1)S(1)}, u32[]{:S(2)}, u32[]{:S(2)}) collective-permute-start(bf16[496,128]{1,0:T(8,128)(2,1)S(1)} %get-tuple-element.27), channel_id=1, source_target_pairs={{0,4},{2,6},{4,0},{6,2},{1,5},{3,7},{5,1},{7,3},{8,12},{10,14},{12... | collective-permute-start | bytes 380936 | tf_op jit(solution)/shard_map/ppermute | solution.py:613
  48.7 2.6 %collective-permute-start.3 = (bf16[496,128]{1,0:T(8,128)(2,1)S(1)}, bf16[496,128]{1,0:T(8,128)(2,1)S(1)}, u32[]{:S(2)}, u32[]{:S(2)}) collective-permute-start(bf16[496,128]{1,0:T(8,128)(2,1)S(1)} %get-tuple-element.28), channel_id=1, source_target_pairs={{0,6},{2,4},{4,2},{6,0},{1,7},{3,5},{5,3},{7,1},{8,14},{10,12},{12... | collective-permute-start | bytes 380936 | tf_op jit(solution)/shard_map/ppermute | solution.py:613
  51.4 1.4 %collective-permute-done.1.refs_1_.refs_4_ = bf16[496,128]{1,0:T(8,128)(2,1)S(1)} collective-permute-done((bf16[496,128]{1,0:T(8,128)(2,1)S(1)}, bf16[496,128]{1,0:T(8,128)(2,1)S(1)}, u32[]{:S(2)}, u32[]{:S(2)}) %collective-permute-start.1) | collective-permute-done | bytes 127008 | tf_op jit(solution)/shard_map/ppermute | solution.py:613
  52.8 3.6 %collective-permute-done.2.refs_2_.refs_5_ = bf16[496,128]{1,0:T(8,128)(2,1)S(1)} collective-permute-done((bf16[496,128]{1,0:T(8,128)(2,1)S(1)}, bf16[496,128]{1,0:T(8,128)(2,1)S(1)}, u32[]{:S(2)}, u32[]{:S(2)}) %collective-permute-start.2) | collective-permute-done | bytes 127008 | tf_op jit(solution)/shard_map/ppermute | solution.py:613
  56.3 1.3 %attend_packed.2 = (bf16[160,128]{1,0:T(8,128)(2,1)S(1)}, bf16[160,128]{1,0:T(8,128)(2,1)S(1)}, bf16[160,128]{1,0:T(8,128)(2,1)S(1)}, bf16[160,128]{1,0:T(8,128)(2,1)S(1)}) custom-call(bf16[480,128]{1,0:T(8,128)(2,1)S(1)} %get-tuple-element.25.refs_0_.refs_3_, bf16[496,128]{1,0:T(8,128)(2,1)S(1)} %collective-permute-done.1.refs_1_.refs_4_, ...), custom_call_target="tpu_custom_call" | custom-call | flops 83886080 | bytes 655360 | tf_op jit(solution)/shard_map/attend_packed/pallas_call | solution.py:408
  57.7 2.0 %collective-permute-start.4 = (bf16[160,128]{1,0:T(8,128)(2,1)S(1)}, bf16[160,128]{1,0:T(8,128)(2,1)S(1)}, u32[]{:S(2)}, u32[]{:S(2)}) collective-permute-start(bf16[160,128]{1,0:T(8,128)(2,1)S(1)} %get-tuple-element.30), channel_id=1, source_target_pairs={{0,2},{2,0},{4,6},{6,4},{1,3},{3,1},{5,7},{7,5},{8,10},{10,8},{12,... | collective-permute-start | bytes 122888 | tf_op jit(solution)/shard_map/ppermute | solution.py:613
  59.7 1.0 %collective-permute-start.5 = (bf16[160,128]{1,0:T(8,128)(2,1)S(1)}, bf16[160,128]{1,0:T(8,128)(2,1)S(1)}, u32[]{:S(2)}, u32[]{:S(2)}) collective-permute-start(bf16[160,128]{1,0:T(8,128)(2,1)S(1)} %get-tuple-element.31), channel_id=1, source_target_pairs={{0,4},{2,6},{4,0},{6,2},{1,5},{3,7},{5,1},{7,3},{8,12},{10,14},{12... | collective-permute-start | bytes 122888 | tf_op jit(solution)/shard_map/ppermute | solution.py:613
  60.6 1.5 %collective-permute-start.6 = (bf16[160,128]{1,0:T(8,128)(2,1)S(1)}, bf16[160,128]{1,0:T(8,128)(2,1)S(1)}, u32[]{:S(2)}, u32[]{:S(2)}) collective-permute-start(bf16[160,128]{1,0:T(8,128)(2,1)S(1)} %get-tuple-element.32), channel_id=1, source_target_pairs={{0,6},{2,4},{4,2},{6,0},{1,7},{3,5},{5,3},{7,1},{8,14},{10,12},{12... | collective-permute-start | bytes 122888 | tf_op jit(solution)/shard_map/ppermute | solution.py:613
  62.3 2.5 %collective-permute-done.5.refs_2_ = bf16[160,128]{1,0:T(8,128)(2,1)S(1)} collective-permute-done((bf16[160,128]{1,0:T(8,128)(2,1)S(1)}, bf16[160,128]{1,0:T(8,128)(2,1)S(1)}, u32[]{:S(2)}, u32[]{:S(2)}) %collective-permute-start.5) | collective-permute-done | bytes 40992 | tf_op jit(solution)/shard_map/ppermute | solution.py:613
  64.8 1.6 %collective-permute-done.6.refs_3_ = bf16[160,128]{1,0:T(8,128)(2,1)S(1)} collective-permute-done((bf16[160,128]{1,0:T(8,128)(2,1)S(1)}, bf16[160,128]{1,0:T(8,128)(2,1)S(1)}, u32[]{:S(2)}, u32[]{:S(2)}) %collective-permute-start.6) | collective-permute-done | bytes 40992 | tf_op jit(solution)/shard_map/ppermute | solution.py:613
  66.4 2.3 %finish.1 = (f32[32,128]{1,0:T(8,128)}, f32[32,128]{1,0:T(8,128)S(1)}) custom-call(bf16[1280,2560]{1,0:T(8,128)(2,1)S(1)} %load_rows.1.w_ref, bf16[160,128]{1,0:T(8,128)(2,1)S(1)} %get-tuple-element.29.refs_0_, bf16[160,128]{1,0:T(8,128)(2,1)S(1)} %collective-permute-done.4.refs_1_, bf16[160,128]{1,0:T(8,128)(2,1)S(1)} %collective-permute-done.5.refs_2_, ...), custom_call_target="tpu_custom_call" | custom-call | flops 419430400 | bytes 6553600 | tf_op jit(solution)/shard_map/finish/pallas_call | solution.py:510
  68.8 1.2 %collective-permute-done.17 = f32[32,128]{1,0:T(8,128)S(1)} collective-permute-done((f32[32,128]{1,0:T(8,128)S(1)}, f32[32,128]{1,0:T(8,128)S(1)}, u32[]{:S(2)}, u32[]{:S(2)}) %collective-permute-start.17) | collective-permute-done | bytes 16416 | tf_op jit(solution)/shard_map/ppermute | solution.py:27
  69.9 0.6 copy.10
  (25 shorter events, 1.7 us)
Async XLA Ops:
  0.6 9.8 %copy-start = (bf16[1,256,960]{1,2,0:T(8,128)(2,1)S(1)}, bf16[1,256,960]{1,2,0:T(8,128)(2,1)}, u32[]{:S(2)}) copy-start(bf16[1,256,960]{1,2,0:T(8,128)(2,1)} %param.10) | copy-start | bytes 1474564
  0.6 8.9 %collective-permute-start = (s32[1,1,2]{2,1,0:T(1,128)}, s32[1,1,2]{2,1,0:T(1,128)S(1)}, u32[]{:S(2)}, u32[]{:S(2)}) collective-permute-start(s32[1,1,2]{2,1,0:T(1,128)} %param.13), channel_id=1, source_target_pairs={{0,1},{1,0},{2,3},{3,2},{4,5},{5,4},{6,7},{7,6},{8,9},{9,8},{10,11... | collective-permute-start | bytes 32 | tf_op jit(solution)/shard_map/ppermute | solution.py:616
  5.1 7.2 %collective-permute-start.7 = (bf16[576,128]{1,0:T(8,128)(2,1)S(1)}, bf16[576,128]{1,0:T(8,128)(2,1)S(1)}, u32[]{:S(2)}, u32[]{:S(2)}) collective-permute-start(bf16[576,128]{1,0:T(8,128)(2,1)S(1)} %get-tuple-element.34), channel_id=1, source_target_pairs={{0,2},{2,0},{4,6},{6,4},{1,3},{3,1},{5,7},{7,5},{8,10},{10,8},{12,... | collective-permute-start | bytes 442376 | tf_op jit(solution)/shard_map/ppermute | solution.py:613
  6.8 13.9 %collective-permute-start.8 = (bf16[576,128]{1,0:T(8,128)(2,1)S(1)}, bf16[576,128]{1,0:T(8,128)(2,1)S(1)}, u32[]{:S(2)}, u32[]{:S(2)}) collective-permute-start(bf16[576,128]{1,0:T(8,128)(2,1)S(1)} %get-tuple-element.35), channel_id=1, source_target_pairs={{0,4},{2,6},{4,0},{6,2},{1,5},{3,7},{5,1},{7,3},{8,12},{10,14},{12... | collective-permute-start | bytes 442376 | tf_op jit(solution)/shard_map/ppermute | solution.py:613
  9.4 11.3 %collective-permute-start.9 = (bf16[576,128]{1,0:T(8,128)(2,1)S(1)}, bf16[576,128]{1,0:T(8,128)(2,1)S(1)}, u32[]{:S(2)}, u32[]{:S(2)}) collective-permute-start(bf16[576,128]{1,0:T(8,128)(2,1)S(1)} %get-tuple-element.36), channel_id=1, source_target_pairs={{0,6},{2,4},{4,2},{6,0},{1,7},{3,5},{5,3},{7,1},{8,14},{10,12},{12... | collective-permute-start | bytes 442376 | tf_op jit(solution)/shard_map/ppermute | solution.py:613
  22.0 9.8 %collective-permute-start.12 = (bf16[176,128]{1,0:T(8,128)(2,1)S(1)}, bf16[176,128]{1,0:T(8,128)(2,1)S(1)}, u32[]{:S(2)}, u32[]{:S(2)}) collective-permute-start(bf16[176,128]{1,0:T(8,128)(2,1)S(1)} %get-tuple-element.38), channel_id=1, source_target_pairs={{0,1},{1,0},{2,3},{3,2},{4,5},{5,4},{6,7},{7,6},{8,9},{9,8},{10,11... | collective-permute-start | bytes 135176 | tf_op jit(solution)/shard_map/ppermute | solution.py:623
  22.6 9.2 %collective-permute-start.13 = (bf16[176,128]{1,0:T(8,128)(2,1)S(1)}, bf16[176,128]{1,0:T(8,128)(2,1)S(1)}, u32[]{:S(2)}, u32[]{:S(2)}) collective-permute-start(bf16[176,128]{1,0:T(8,128)(2,1)S(1)} %get-tuple-element.39), channel_id=1, source_target_pairs={{0,3},{1,2},{2,1},{3,0},{4,7},{5,6},{6,5},{7,4},{8,11},{9,10},{10,... | collective-permute-start | bytes 135176 | tf_op jit(solution)/shard_map/ppermute | solution.py:623
  25.7 6.1 %collective-permute-start.14 = (bf16[176,128]{1,0:T(8,128)(2,1)S(1)}, bf16[176,128]{1,0:T(8,128)(2,1)S(1)}, u32[]{:S(2)}, u32[]{:S(2)}) collective-permute-start(bf16[176,128]{1,0:T(8,128)(2,1)S(1)} %get-tuple-element.40), channel_id=1, source_target_pairs={{0,5},{1,4},{2,7},{3,6},{4,1},{5,0},{6,3},{7,2},{8,13},{9,12},{10,... | collective-permute-start | bytes 135176 | tf_op jit(solution)/shard_map/ppermute | solution.py:623
  26.7 6.8 %collective-permute-start.15 = (bf16[176,128]{1,0:T(8,128)(2,1)S(1)}, bf16[176,128]{1,0:T(8,128)(2,1)S(1)}, u32[]{:S(2)}, u32[]{:S(2)}) collective-permute-start(bf16[176,128]{1,0:T(8,128)(2,1)S(1)} %get-tuple-element.41), channel_id=1, source_target_pairs={{0,7},{1,6},{2,5},{3,4},{4,3},{5,2},{6,1},{7,0},{8,15},{9,14},{10,... | collective-permute-start | bytes 135176 | tf_op jit(solution)/shard_map/ppermute | solution.py:623
  31.8 34.7 %copy-start.1 = (bf16[1,1,64,2560]{3,2,1,0:T(8,128)(2,1)S(1)}, bf16[1,1,64,2560]{3,2,1,0:T(8,128)(2,1)}, u32[]{:S(2)}) copy-start(bf16[1,1,64,2560]{3,2,1,0:T(8,128)(2,1)} %param.8) | copy-start | bytes 983044
  31.8 34.7 %copy-start.2 = (f32[1,1,32,128]{3,2,1,0:T(8,128)S(1)}, f32[1,1,32,128]{3,2,1,0:T(8,128)}, u32[]{:S(2)}) copy-start(f32[1,1,32,128]{3,2,1,0:T(8,128)} %param.12) | copy-start | bytes 49156
  34.8 31.6 %collective-permute-start.16 = (bf16[64,2560]{1,0:T(8,128)(2,1)S(1)}, bf16[64,2560]{1,0:T(8,128)(2,1)S(1)}, u32[]{:S(2)}, u32[]{:S(2)}) collective-permute-start(bf16[64,2560]{1,0:T(8,128)(2,1)S(1)} %project_packed.1), channel_id=1, source_target_pairs={{0,1},{1,0},{2,3},{3,2},{4,5},{5,4},{6,7},{7,6},{8,9},{9,8},{10,11... | collective-permute-start | bytes 983048 | tf_op jit(solution)/shard_map/ppermute | solution.py:616
  35.9 8.0 %collective-permute-start.10 = (bf16[384,128]{1,0:T(8,128)(2,1)S(1)}, bf16[384,128]{1,0:T(8,128)(2,1)S(1)}, u32[]{:S(2)}, u32[]{:S(2)}) collective-permute-start(bf16[384,128]{1,0:T(8,128)(2,1)S(1)} %collect.2.refs_0_), channel_id=1, source_target_pairs={{0,1},{1,0},{2,3},{3,2},{4,5},{5,4},{6,7},{7,6},{8,9},{9,8},{10,11... | collective-permute-start | bytes 294920 | tf_op jit(solution)/shard_map/ppermute | solution.py:616
  43.9 18.2 %collective-permute-start.11 = (bf16[768,128]{1,0:T(8,128)(2,1)S(1)}, bf16[768,128]{1,0:T(8,128)(2,1)S(1)}, u32[]{:S(2)}, u32[]{:S(2)}) collective-permute-start(bf16[768,128]{1,0:T(8,128)(2,1)S(1)} %collect.3.refs_0_), channel_id=1, source_target_pairs={{0,16},{16,0},{1,17},{17,1},{2,18},{18,2},{3,19},{19,3},{4,20},{20... | collective-permute-start | bytes 589832 | tf_op jit(solution)/shard_map/ppermute | solution.py:616
  46.9 5.8 %collective-permute-start.1 = (bf16[496,128]{1,0:T(8,128)(2,1)S(1)}, bf16[496,128]{1,0:T(8,128)(2,1)S(1)}, u32[]{:S(2)}, u32[]{:S(2)}) collective-permute-start(bf16[496,128]{1,0:T(8,128)(2,1)S(1)} %get-tuple-element.26), channel_id=1, source_target_pairs={{0,2},{2,0},{4,6},{6,4},{1,3},{3,1},{5,7},{7,5},{8,10},{10,8},{12,... | collective-permute-start | bytes 380936 | tf_op jit(solution)/shard_map/ppermute | solution.py:613
  47.3 9.1 %collective-permute-start.2 = (bf16[496,128]{1,0:T(8,128)(2,1)S(1)}, bf16[496,128]{1,0:T(8,128)(2,1)S(1)}, u32[]{:S(2)}, u32[]{:S(2)}) collective-permute-start(bf16[496,128]{1,0:T(8,128)(2,1)S(1)} %get-tuple-element.27), channel_id=1, source_target_pairs={{0,4},{2,6},{4,0},{6,2},{1,5},{3,7},{5,1},{7,3},{8,12},{10,14},{12... | collective-permute-start | bytes 380936 | tf_op jit(solution)/shard_map/ppermute | solution.py:613
  48.7 7.6 %collective-permute-start.3 = (bf16[496,128]{1,0:T(8,128)(2,1)S(1)}, bf16[496,128]{1,0:T(8,128)(2,1)S(1)}, u32[]{:S(2)}, u32[]{:S(2)}) collective-permute-start(bf16[496,128]{1,0:T(8,128)(2,1)S(1)} %get-tuple-element.28), channel_id=1, source_target_pairs={{0,6},{2,4},{4,2},{6,0},{1,7},{3,5},{5,3},{7,1},{8,14},{10,12},{12... | collective-permute-start | bytes 380936 | tf_op jit(solution)/shard_map/ppermute | solution.py:613
  57.7 4.6 %collective-permute-start.4 = (bf16[160,128]{1,0:T(8,128)(2,1)S(1)}, bf16[160,128]{1,0:T(8,128)(2,1)S(1)}, u32[]{:S(2)}, u32[]{:S(2)}) collective-permute-start(bf16[160,128]{1,0:T(8,128)(2,1)S(1)} %get-tuple-element.30), channel_id=1, source_target_pairs={{0,2},{2,0},{4,6},{6,4},{1,3},{3,1},{5,7},{7,5},{8,10},{10,8},{12,... | collective-permute-start | bytes 122888 | tf_op jit(solution)/shard_map/ppermute | solution.py:613
  59.7 5.2 %collective-permute-start.5 = (bf16[160,128]{1,0:T(8,128)(2,1)S(1)}, bf16[160,128]{1,0:T(8,128)(2,1)S(1)}, u32[]{:S(2)}, u32[]{:S(2)}) collective-permute-start(bf16[160,128]{1,0:T(8,128)(2,1)S(1)} %get-tuple-element.31), channel_id=1, source_target_pairs={{0,4},{2,6},{4,0},{6,2},{1,5},{3,7},{5,1},{7,3},{8,12},{10,14},{12... | collective-permute-start | bytes 122888 | tf_op jit(solution)/shard_map/ppermute | solution.py:613
  60.6 5.8 %collective-permute-start.6 = (bf16[160,128]{1,0:T(8,128)(2,1)S(1)}, bf16[160,128]{1,0:T(8,128)(2,1)S(1)}, u32[]{:S(2)}, u32[]{:S(2)}) collective-permute-start(bf16[160,128]{1,0:T(8,128)(2,1)S(1)} %get-tuple-element.32), channel_id=1, source_target_pairs={{0,6},{2,4},{4,2},{6,0},{1,7},{3,5},{5,3},{7,1},{8,14},{10,12},{12... | collective-permute-start | bytes 122888 | tf_op jit(solution)/shard_map/ppermute | solution.py:613
  68.8 1.2 %collective-permute-start.17 = (f32[32,128]{1,0:T(8,128)S(1)}, f32[32,128]{1,0:T(8,128)S(1)}, u32[]{:S(2)}, u32[]{:S(2)}) collective-permute-start(f32[32,128]{1,0:T(8,128)S(1)} %get-tuple-element.45), channel_id=1, source_target_pairs={{0,8},{8,0},{1,9},{9,1},{2,10},{10,2},{3,11},{11,3},{4,12},{12,4},... | collective-permute-start | bytes 49160 | tf_op jit(solution)/shard_map/ppermute | solution.py:27

commit v3 on v2

--- a/solution.py
+++ b/solution.py
@@ -187,16 +187,16 @@
         out[last, :] = pack_half(turned[whole])
 
 
-def windows(x_ref, held, sems, me, half, count, width):
+def windows(x_ref, held, sems, me, half, count, width, slots):
     span = held.shape[2]
 
-    def window(r):
+    def window(k, r):
         start = half * (count * width) + lax.div((me ^ r) * width, LANES) * LANES
         return pltpu.make_async_copy(
-            x_ref.at[:, pl.ds(pl.multiple_of(start, LANES), span)], held.at[r], sems.at[r]
-        )
-
-    return [window(r) for r in range(count)]
+            x_ref.at[:, pl.ds(pl.multiple_of(start, LANES), span)], held.at[k], sems.at[k]
+        )
+
+    return [window(k, r) for k, r in enumerate(slots)]
 
 
 def sigma_row(step):
@@ -204,107 +204,135 @@
     return 5.0 * unit_time / (1.0 + 4.0 * unit_time)
 
 
-def far_kernel(width, count, place_ref, half_ref, group_ref, when_ref, x_ref, head_ref, *refs):
-    outs, refs = refs[:count], refs[count:]
-    pack_ref, clock_ref, held, head_held, steps_ref, sems, head_sem, steps_sem = refs
+def first_kernel(width, count, slot, place_ref, half_ref, group_ref, x_ref, head_ref, *refs):
+    out_ref, pack_ref, held, head_held, sems, head_sem = refs
     me = place_ref[0]
     cut, columns = head_held.shape
-    order = [count // 2] + [r for r in range(count - 1, -1, -1) if r != count // 2]
-    copies = windows(x_ref, held, sems, me, 1 - half_ref[0], count, width)
+    copy = windows(x_ref, held, sems, me, 1 - half_ref[0], count, width, [slot])[0]
     head_copy = pltpu.make_async_copy(
         head_ref.at[pl.ds(pl.multiple_of(group_ref[0] * cut, cut), cut), :], head_held, head_sem
     )
-    steps_copy = pltpu.make_async_copy(when_ref, steps_ref, steps_sem)
-    copies[order[0]].start()
-    steps_copy.start()
     head_copy.start()
-    for r in order[1:]:
-        copies[r].start()
-    packed = outs[0].shape[0]
-    for r in order:
-        copies[r].wait()
-        cut_window(width, held, outs[r], r, lax.rem(me ^ r, 2) == 1)
+    copy.start()
     head_copy.wait()
+    packed = out_ref.shape[0] - pack_ref.shape[0]
     for t in range(head_tiles(columns)):
         tile = head_held[:, t * LANES : min((t + 1) * LANES, columns)]
         if tile.shape[1] < LANES:
             fill = jnp.zeros((cut, LANES - tile.shape[1]), tile.dtype)
             tile = jnp.concatenate([tile, fill], axis=1)
         pack_ref[t * cut : (t + 1) * cut, :] = tile
-        for r in range(1, count):
-            outs[r][packed + t * cut : packed + (t + 1) * cut, :] = tile
-    steps_copy.wait()
-    now = jnp.full((1, LANES), steps_ref[0, 0], jnp.int32).astype(jnp.float32)
-    change = sigma_row(steps_ref[0, 1]) - sigma_row(steps_ref[0, 0])
-    clock_ref[...] = jnp.concatenate([now, change])
-
-
-def split_far(x, head, steps, scalars, count, halves):
+        out_ref[packed + t * cut : packed + (t + 1) * cut, :] = tile
+    copy.wait()
+    cut_window(width, held, out_ref, 0, lax.rem(me ^ slot, 2) == 1)
+
+
+def split_first(x, head, scalars, slot, count, halves):
     rows, columns = x.shape
     width = columns // halves // count
     cut = head.shape[0] // 2
     span = cut * head_tiles(head.shape[1])
     length = rows * width // LANES
-    pieces = [
-        jax.ShapeDtypeStruct((length + span * (r != 0), LANES), jnp.bfloat16)
-        for r in range(count)
-    ]
-    results = pl.pallas_call(
-        functools.partial(far_kernel, width, count),
+    return pl.pallas_call(
+        functools.partial(first_kernel, width, count, slot),
         in_specs=[pl.BlockSpec(memory_space=pltpu.SMEM)] * 3
-        + [pl.BlockSpec(memory_space=pltpu.HBM)] * 3,
-        out_shape=pieces
-        + [
+        + [pl.BlockSpec(memory_space=pltpu.HBM)] * 2,
+        out_shape=[
+            jax.ShapeDtypeStruct((length + span, LANES), jnp.bfloat16),
             jax.ShapeDtypeStruct((span, LANES), jnp.bfloat16),
-            jax.ShapeDtypeStruct((2, LANES), jnp.float32),
         ],
         scratch_shapes=[
-            pltpu.VMEM((count, rows, (width // LANES + 1) * LANES), jnp.bfloat16),
+            pltpu.VMEM((1, rows, (width // LANES + 1) * LANES), jnp.bfloat16),
             pltpu.VMEM((cut, head.shape[1]), jnp.bfloat16),
-            pltpu.SMEM((1, 2), jnp.int32),
-            pltpu.SemaphoreType.DMA((count,)),
-            pltpu.SemaphoreType.DMA,
+            pltpu.SemaphoreType.DMA((1,)),
             pltpu.SemaphoreType.DMA,
         ],
         compiler_params=pltpu.CompilerParams(vmem_limit_bytes=4 << 20),
         cost_estimate=pl.CostEstimate(
+            flops=0, transcendentals=0, bytes_accessed=4 * rows * width
+        ),
+        name="split_first",
+    )(
+        *scalars,
+        pltpu.with_memory_space_constraint(x, pltpu.HBM),
+        pltpu.with_memory_space_constraint(head, pltpu.HBM),
+    )
+
+
+def far_kernel(width, count, slots, place_ref, half_ref, when_ref, x_ref, pack_ref, *refs):
+    outs, (clock_ref, held, steps_ref, sems, steps_sem) = refs[: len(slots)], refs[len(slots) :]
+    me = place_ref[0]
+    copies = windows(x_ref, held, sems, me, 1 - half_ref[0], count, width, slots)
+    steps_copy = pltpu.make_async_copy(when_ref, steps_ref, steps_sem)
+    for copy in copies:
+        copy.start()
+    steps_copy.start()
+    packed = held.shape[1] * width // LANES
+    for out in outs:
+        out[packed:, :] = pack_ref[...]
+    for k, r in enumerate(slots):
+        copies[k].wait()
+        cut_window(width, held, outs[k], k, lax.rem(me ^ r, 2) == 1)
+    steps_copy.wait()
+    now = jnp.full((1, LANES), steps_ref[0, 0], jnp.int32).astype(jnp.float32)
+    change = sigma_row(steps_ref[0, 1]) - sigma_row(steps_ref[0, 0])
+    clock_ref[...] = jnp.concatenate([now, change])
+
+
+def split_far(x, pack, steps, scalars, slots, count, halves):
+    rows, columns = x.shape
+    width = columns // halves // count
+    length = rows * width // LANES
+    results = pl.pallas_call(
+        functools.partial(far_kernel, width, count, slots),
+        in_specs=[pl.BlockSpec(memory_space=pltpu.SMEM)] * 2
+        + [pl.BlockSpec(memory_space=pltpu.HBM)] * 2
+        + [pl.BlockSpec(memory_space=pltpu.VMEM)],
+        out_shape=[
+            jax.ShapeDtypeStruct((length + pack.shape[0], LANES), jnp.bfloat16)
+            for _ in slots
+        ]
+        + [jax.ShapeDtypeStruct((2, LANES), jnp.float32)],
+        scratch_shapes=[
+            pltpu.VMEM((len(slots), rows, (width // LANES + 1) * LANES), jnp.bfloat16),
+            pltpu.SMEM((1, 2), jnp.int32),
+            pltpu.SemaphoreType.DMA((len(slots),)),
+            pltpu.SemaphoreType.DMA,
+        ],
+        compiler_params=pltpu.CompilerParams(vmem_limit_bytes=4 << 20),
+        cost_estimate=pl.CostEstimate(
             flops=0, transcendentals=0, bytes_accessed=4 * rows * columns // halves
         ),
         name="split_far",
     )(
-        *scalars,
+        *scalars[:2],
         pltpu.with_memory_space_constraint(steps, pltpu.HBM),
         pltpu.with_memory_space_constraint(x, pltpu.HBM),
-        pltpu.with_memory_space_constraint(head, pltpu.HBM),
-    )
-    return results[:count], results[count], results[count + 1]
-
-
-def near_kernel(width, count, place_ref, half_ref, x_ref, mod_ref, *refs):
+        pack,
+    )
+    return results[:-1], results[-1]
+
+
+def near_kernel(width, count, place_ref, half_ref, x_ref, *refs):
     outs, held, sems = refs[:count], refs[count], refs[count + 1]
     me = place_ref[0]
-    copies = windows(x_ref, held, sems, me, half_ref[0], count, width)
+    copies = windows(x_ref, held, sems, me, half_ref[0], count, width, range(count))
     for r in range(count - 1, -1, -1):
         copies[r].start()
-    for r in range(1, count):
-        put_modulation(outs[r], outs[0].shape[0], mod_ref[0:1, :])
     for r in range(count - 1, -1, -1):
         copies[r].wait()
         cut_window(width, held, outs[r], r, lax.rem(me ^ r, 2) == 1)
 
 
-def split_near(x, modulation, scalars, count, halves):
+def split_near(x, scalars, count, halves):
     rows, columns = x.shape
     width = columns // halves // count
     length = rows * width // LANES
     return pl.pallas_call(
         functools.partial(near_kernel, width, count),
         in_specs=[pl.BlockSpec(memory_space=pltpu.SMEM)] * 2
-        + [pl.BlockSpec(memory_space=pltpu.HBM), pl.BlockSpec(memory_space=pltpu.VMEM)],
-        out_shape=[
-            jax.ShapeDtypeStruct((length + MOD_ROWS * (r != 0), LANES), jnp.bfloat16)
-            for r in range(count)
-        ],
+        + [pl.BlockSpec(memory_space=pltpu.HBM)],
+        out_shape=[jax.ShapeDtypeStruct((length, LANES), jnp.bfloat16)] * count,
         scratch_shapes=[
             pltpu.VMEM((count, rows, (width // LANES + 1) * LANES), jnp.bfloat16),
             pltpu.SemaphoreType.DMA((count,)),
@@ -314,7 +342,7 @@
             flops=0, transcendentals=0, bytes_accessed=4 * rows * columns // halves
         ),
         name="split_near",
-    )(*scalars[:2], pltpu.with_memory_space_constraint(x, pltpu.HBM), modulation)
+    )(*scalars[:2], pltpu.with_memory_space_constraint(x, pltpu.HBM))
 
 
 def load_kernel(count, place_ref, w_ref, out_ref, sems):
@@ -394,7 +422,8 @@
             [rest[: rows // 2], rest[rows // 2 :]], axis=1
         ).astype(jnp.bfloat16)
         if riders:
-            put_modulation(outs[b], packed, riders[0][1:2, :])
+            for k, rider in enumerate(riders):
+                put_modulation(outs[b], packed + k * MOD_ROWS, rider[0:1, :])
 
 
 def attend_packed(pieces, heads, rows, riders=()):
@@ -403,7 +432,7 @@
     length = rows * heads * HEAD // LANES
     specs = [pl.BlockSpec(memory_space=pltpu.VMEM)] * (count + len(riders))
     if riders:
-        length += MOD_ROWS
+        length += MOD_ROWS * len(riders)
     out = jax.ShapeDtypeStruct((length, LANES), jnp.bfloat16)
     return pl.pallas_call(
         functools.partial(attend_kernel, heads, rows, count),
@@ -427,21 +456,23 @@
     )
 
 
-def project_kernel(rows, w_ref, *refs):
+def project_kernel(rows, first, w_ref, *refs):
     pieces, out_ref, left_ref = refs[:-2], refs[-2], refs[-1]
     gather_left(pieces, left_ref, rows)
-    for start in range(0, w_ref.shape[1], 512):
-        cut = slice(start, start + 512)
-        out_ref[:, cut] = jnp.dot(
-            left_ref[...], w_ref[:, cut], preferred_element_type=jnp.float32
-        ).astype(jnp.bfloat16)
-
-
-def project_packed(pieces, weight, rows):
-    depth, dim = weight.shape
+    tile = math.gcd(out_ref.shape[1], 5 * LANES)
+    for start in range(0, out_ref.shape[1], tile):
+        out_ref[:, start : start + tile] = jnp.dot(
+            left_ref[...],
+            w_ref[:, first + start : first + start + tile],
+            preferred_element_type=jnp.float32,
+        ).astype(out_ref.dtype)
+
+
+def project_packed(pieces, weight, rows, first, dim, dtype):
+    depth = weight.shape[0]
     return pl.pallas_call(
-        functools.partial(project_kernel, rows),
-        out_shape=jax.ShapeDtypeStruct((rows, dim), jnp.bfloat16),
+        functools.partial(project_kernel, rows, first),
+        out_shape=jax.ShapeDtypeStruct((rows, dim), dtype),
         scratch_shapes=[pltpu.VMEM((rows, depth), jnp.bfloat16)],
         compiler_params=pltpu.CompilerParams(vmem_limit_bytes=16 << 20),
         cost_estimate=pl.CostEstimate(
@@ -451,10 +482,10 @@
     )(pltpu.with_memory_space_constraint(weight, pltpu.VMEM), *pieces)
 
 
-def finish_kernel(rows, count, w_ref, *refs):
-    pieces, refs = refs[:count], refs[count:]
-    mod_ref, far_ref, hidden_ref, head_ref, latent_ref, clock_ref = refs[:6]
-    out_ref, step_ref, acc_ref, left_ref, turn_ref = refs[6:]
+def finish_kernel(rows, near_ref, *refs):
+    far, refs = refs[:2], refs[2:]
+    mod_ref, hidden_ref, head_ref, latent_ref, clock_ref, out_ref, step_ref = refs[:7]
+    acc_ref, turn_ref = refs[7:]
     steps, _, tile = acc_ref.shape
     dim = steps * tile
 
@@ -463,12 +494,11 @@
         line, offset = divmod(start, mod_ref.shape[2])
         return mod_ref[line, :, offset : offset + tile]
 
-    gather_left(pieces, left_ref, rows)
     total = jnp.zeros((rows, 1), jnp.float32)
     for i in range(steps):
         cut = slice(i * tile, (i + 1) * tile)
-        projected = jnp.dot(left_ref[...], w_ref[:, cut], preferred_element_type=jnp.float32)
-        projected = projected + far_ref[:, cut].astype(jnp.float32)
+        side, offset = divmod(i * tile, dim // 2)
+        projected = near_ref[:, cut] + far[side][:, offset : offset + tile].astype(jnp.float32)
         part = hidden_ref[:, cut].astype(jnp.float32) + modulation(0, i) * projected
         acc_ref[i] = part
         total += jnp.sum(part, axis=-1, keepdims=True)
@@ -499,26 +529,23 @@
     step_ref[...] = latent_ref[...] + clock_ref[1:2, :] * paired
 
 
-def finish(pieces, weight, far, hidden, lines, head_rows, latent, clock, rows):
-    depth, dim = weight.shape
-    count = len(pieces)
-    tile = math.gcd(dim, lines.shape[2])
+def finish(near, far, hidden, lines, head_rows, latent, clock):
+    rows, dim = near.shape
+    tile = math.gcd(dim // 2, lines.shape[2])
     patch = head_rows.shape[0]
-    inputs = (pltpu.with_memory_space_constraint(weight, pltpu.VMEM), *pieces, lines)
-    inputs += (far, hidden, head_rows, latent, clock)
+    inputs = (near, *far, lines, hidden, head_rows, latent, clock)
     result = jax.ShapeDtypeStruct((rows // 2, 2 * patch), jnp.float32)
     return pl.pallas_call(
-        functools.partial(finish_kernel, rows, count),
+        functools.partial(finish_kernel, rows),
         in_specs=[pl.BlockSpec(memory_space=pltpu.VMEM)] * len(inputs),
         out_shape=[result] * 2,
         scratch_shapes=[
             pltpu.VMEM((dim // tile, rows, tile), jnp.float32),
-            pltpu.VMEM((rows, depth), jnp.bfloat16),
             pltpu.VMEM((rows, patch), jnp.float32),
         ],
-        compiler_params=pltpu.CompilerParams(vmem_limit_bytes=16 << 20),
-        cost_estimate=pl.CostEstimate(
-            flops=2 * rows * depth * dim, transcendentals=0, bytes_accessed=2 * depth * dim
+        compiler_params=pltpu.CompilerParams(vmem_limit_bytes=8 << 20),
+        cost_estimate=pl.CostEstimate(
+            flops=2 * rows * patch * dim, transcendentals=0, bytes_accessed=8 * rows * dim
         ),
         name="finish",
     )(*inputs)
@@ -528,11 +555,10 @@
     out_ref = refs[-1]
     span = out_ref.shape[0] // (len(refs) - 1)
     for r, ref in enumerate(refs[:-1]):
-        at = ref.shape[0] - span if start is None or r == 0 else start
-        out_ref[r * span : (r + 1) * span, :] = ref[at : at + span, :]
-
-
-def collect(pieces, span, start=None):
+        out_ref[r * span : (r + 1) * span, :] = ref[start : start + span, :]
+
+
+def collect(pieces, span, start):
     return pl.pallas_call(
         functools.partial(collect_kernel, start),
         in_specs=[pl.BlockSpec(memory_space=pltpu.VMEM)] * len(pieces),
@@ -545,9 +571,9 @@
     )(*pieces)
 
 
-def arrange_kernel(count, width, packed, done, place_ref, half_ref, group_ref, *refs):
-    mine_ref, up_ref, mod_ref = refs[:3]
-    near, far = refs[3 : 3 + count], refs[3 + count : -2]
+def arrange_kernel(count, width, done, place_ref, half_ref, group_ref, *refs):
+    mine_ref, up_ref, mod_ref, mate_ref = refs[:4]
+    far = refs[4:-2]
     head_out, mod_out = refs[-2:]
     span = mine_ref.shape[0] // (2 * count)
     cut = head_out.shape[0] // 2
@@ -573,21 +599,24 @@
         head_out[:, pl.ds(start, 2 * width)] = jnp.concatenate(
             [jnp.where(first, own, other), jnp.where(first, other, own)], axis=1
         )
-        own = mod_ref[0:1, :] if r == 0 else get_modulation(near[r], packed, columns)
-        other = get_modulation(far[r], done, columns)
+        if r == 0:
+            own, other = mod_ref[0:1, :], mate_ref[...]
+        else:
+            own = get_modulation(far[r], done, columns)
+            other = get_modulation(far[r], done + MOD_ROWS, columns)
         mod_out[owner] = jnp.concatenate(
             [jnp.where(first, own, other), jnp.where(first, other, own)], axis=1
         )
 
 
-def arrange(mine, up, modulation, near, far, head, scalars, packed, done):
+def arrange(mine, up, modulation, mate, far, head, scalars, done):
     count = len(far)
     patch, width = head.shape
     columns = modulation.shape[1]
     return pl.pallas_call(
-        functools.partial(arrange_kernel, count, width, packed, done),
+        functools.partial(arrange_kernel, count, width, done),
         in_specs=[pl.BlockSpec(memory_space=pltpu.SMEM)] * 3
-        + [pl.BlockSpec(memory_space=pltpu.VMEM)] * (3 + 2 * count),
+        + [pl.BlockSpec(memory_space=pltpu.VMEM)] * (4 + count),
         out_shape=[
             jax.ShapeDtypeStruct((patch, 2 * count * width), jnp.bfloat16),
             jax.ShapeDtypeStruct((count, 1, 2 * columns), jnp.float32),
@@ -597,7 +626,7 @@
             flops=0, transcendentals=0, bytes_accessed=8 * count * patch * width
         ),
         name="arrange",
-    )(*scalars, mine, up, modulation, *near, *far)
+    )(*scalars, mine, up, modulation, mate, *far)
 
 
 def packed_body(head_inputs, hidden, out_weight, time_weight, head_weight, latent, timesteps):
@@ -629,8 +658,12 @@
     side = half[None].astype(jnp.int32)
     level = group[None].astype(jnp.int32)
     scalars = (here, side, level)
-    far_sent, pack, clock = split_far(x, head, timesteps.reshape(1, 2), scalars, count, halves)
-    far_pieces = [far_sent[0]] + [along(far_sent[r], r) for r in range(1, count)]
+    last = count // 2
+    slots = [r for r in range(count - 1, 0, -1) if r != last] + [0]
+    first, pack = split_first(x, head, scalars, last, count, halves)
+    sent, clock = split_far(x, pack, timesteps.reshape(1, 2), scalars, slots, count, halves)
+    far_sent = [first if r == last else sent[slots.index(r)] for r in range(count)]
+    far_pieces = [slanted(far_sent[r], r) for r in range(count)]
 
     other_steps = swap(timesteps, "fsdp")
     freqs = jnp.exp(
@@ -640,39 +673,43 @@
     angle = angle * freqs
     embedding = jnp.concatenate([jnp.cos(angle), jnp.sin(angle)], axis=-1).astype(jnp.bfloat16)
     modulation = jnp.dot(embedding, time_weight[0], preferred_element_type=jnp.float32)
-
-    near_sent = split_near(x, modulation, scalars, count, halves)
+    mate = swap(modulation[1:], "fsdp")
+
+    near_sent = split_near(x, scalars, count, halves)
     near_pieces = [near_sent[0]] + [along(near_sent[r], r) for r in range(1, count)]
 
     weight = load_rows(out_weight[0], here, count)
-    far_attended = attend_packed(far_pieces, heads, rows, (modulation,))
-    far_home = [slanted(far_attended[r], r) for r in range(count)]
-    partial = project_packed(far_home, weight, rows)
-    partial = swap(partial, "fsdp")
-
-    packed = far_sent[0].shape[0]
-    done = far_home[0].shape[0] - MOD_ROWS
-    line = collect([pack] + far_pieces[1:], span, packed)
+    far_attended = attend_packed(far_pieces, heads, rows, (modulation, mate))
+    far_home = [far_attended[0]]
+    far_home += [along(far_attended[r], r) for r in range(1, count)]
+    part = DIM // 2
+    partial = []
+    for k in range(2):
+        term = project_packed(far_home, weight, rows, k * part, part, jnp.bfloat16)
+        partial.append(swap(term, "fsdp"))
+
+    packed = near_sent[0].shape[0]
+    done = far_home[0].shape[0] - 2 * MOD_ROWS
+    line = collect(far_pieces, span, packed)
     other = swap(line, "fsdp")
-    mine = collect([line, other], line.shape[0])
+    mine = collect([other, line], line.shape[0], 0)
     up = swap(mine, "grp")
     head_rows, lines = arrange(
-        mine, up, modulation, near_pieces, far_home, head, scalars, packed, done
+        mine, up, modulation, mate, far_home, head, scalars, done
     )
 
     near_attended = attend_packed(near_pieces, heads, rows)
     near_home = [near_attended[0]]
     near_home += [along(near_attended[r], r) for r in range(1, count)]
+    projected = project_packed(near_home, weight, rows, 0, DIM, jnp.float32)
     velocity, stepped = finish(
-        near_home,
-        weight,
+        projected,
         partial,
         hidden.reshape(rows, DIM),
         lines,
         head_rows,
         latent.reshape(rows // 2, 2 * PATCH),
         clock,
-        rows,
     )
     carried = partner(stepped, "section", 0)
     return (velocity.reshape(latent.shape), carried.reshape(latent.shape))

time: 70.7 us -> 66.9 us (0.946)
  waiting for transfers between devices: 28.9 us -> 20.6 us
  starting transfers between devices: 26.9 us -> 30.3 us
  Pallas kernels: 12.2 us -> 13.2 us
    ppermute x9, waiting for transfers between devices: 19 us -> 8.04 us  [along(): return lax.ppermute(block, 'seq', [(i, i ^ r) for i in range(count)])]
    ppermute x4, waiting for transfers between devices: 1.71 us -> 8.38 us  [slanted(): return lax.ppermute(block, ('seq', 'fsdp'), route)]
    ppermute x4 -> x6, waiting for transfers between devices: 6.97 us -> 2.95 us  [swap(): return lax.ppermute(block, axis, [(0, 1), (1, 0)])]
    ppermute x4 -> x6, starting transfers between devices: 6.76 us -> 8.88 us  [swap(): return lax.ppermute(block, axis, [(0, 1), (1, 0)])]
    ppermute x9, starting transfers between devices: 13.4 us -> 14.6 us  [along(): return lax.ppermute(block, 'seq', [(i, i ^ r) for i in range(count)])]
    pallas_call x4 -> x7, Pallas kernels: 5.21 us -> 6.2 us  [the longest x3 2.46 us: project_packed(): pl.pallas_call(functools.partial(project_kernel, rows, first), out_shape=...]
  transfers between devices with their start and end apart: 18 -> 20, of which waited for: 9 -> 7; matrix products, arithmetic and copies ran while one was open for 1% -> 2% of each run, Pallas kernels for 10% -> 18%
where the time goes in v3:
time: 66.9 us; the launch traced here: 66.7 us
  starting transfers between devices  30.3 us (45%)
  waiting for transfers between devices  20.6 us (31%)
  Pallas kernels  13.2 us (20%)
  between operations  0.87 us (1%)
  other arithmetic  0.82 us (1%)
    ppermute x9, starting transfers between devices, along(): return lax.ppermute(block, 'seq', [(i, i ^ r) for i in range(count)])  14.6 us
    ppermute x6, starting transfers between devices, swap(): return lax.ppermute(block, axis, [(0, 1), (1, 0)])  8.88 us
    ppermute x4, waiting for transfers between devices, slanted(): return lax.ppermute(block, ('seq', 'fsdp'), route)  8.38 us
    ppermute x9, waiting for transfers between devices, along(): return lax.ppermute(block, 'seq', [(i, i ^ r) for i in range(count)])  8.04 us
    ppermute x4, starting transfers between devices, slanted(): return lax.ppermute(block, ('seq', 'fsdp'), route)  6.88 us
    ppermute x6, waiting for transfers between devices, swap(): return lax.ppermute(block, axis, [(0, 1), (1, 0)])  2.95 us
    pallas_call x1, Pallas kernels, load_rows(): pl.pallas_call(functools.partial(load_kernel, count), in_specs=[pl.BlockS...  2.95 us
    pallas_call x2, Pallas kernels, attend_packed(): pl.pallas_call(functools.partial(attend_kernel, heads, rows, count), in_s...  2.67 us
  transfers between devices with their start and end apart: 20, of which 7 were waited for; matrix products, arithmetic and copies ran while one was open for 2% of the time, Pallas kernels for 18%

profile of v3, /device:TPU:0, one launch (start us, length us, event | category | flops | bytes accessed | tf_op | source)
XLA Modules:
  0.0 66.7 jit_solution(25266158616394001)
XLA Ops:
  0.6 3.0 %collective-permute-start.6 = (s32[1,1,2]{2,1,0:T(1,128)}, s32[1,1,2]{2,1,0:T(1,128)S(1)}, u32[]{:S(2)}, u32[]{:S(2)}) collective-permute-start(s32[1,1,2]{2,1,0:T(1,128)} %param.13), channel_id=1, source_target_pairs={{0,1},{1,0},{2,3},{3,2},{4,5},{5,4},{6,7},{7,6},{8,9},{9,8},{10,11... | collective-permute-start | bytes 32 | tf_op jit(solution)/shard_map/ppermute | solution.py:645
  3.7 1.0 %split_first.1 = (bf16[576,128]{1,0:T(8,128)(2,1)S(1)}, bf16[96,128]{1,0:T(8,128)(2,1)S(1)}) custom-call(s32[1]{0:T(128)} %bitcast.place_ref, s32[1]{0:T(128)} %bitcast.2.half_ref, s32[1]{0:T(128)} %bitcast.5.group_ref, bf16[64,7680]{1,0:T(8,128)(2,1)} %bitcast.20, bf16[64,320]{1,0:T(8,128)(2,1)} %bitcast.24), custom_call_target="tpu_custom_call" | custom-call | bytes 245760 | tf_op jit(solution)/shard_map/split_first/pallas_call | solution.py:236
  4.7 2.6 %collective-permute-start.10 = (bf16[576,128]{1,0:T(8,128)(2,1)S(1)}, bf16[576,128]{1,0:T(8,128)(2,1)S(1)}, u32[]{:S(2)}, u32[]{:S(2)}) collective-permute-start(bf16[576,128]{1,0:T(8,128)(2,1)S(1)} %get-tuple-element.36), channel_id=1, source_target_pairs={{0,5},{1,4},{2,7},{3,6},{4,1},{5,0},{6,3},{7,2},{8,13},{9,12},{10,... | collective-permute-start | bytes 442376 | tf_op jit(solution)/shard_map/ppermute | solution.py:652
  7.3 1.3 %split_far.1 = (bf16[576,128]{1,0:T(8,128)(2,1)S(1)}, bf16[576,128]{1,0:T(8,128)(2,1)S(1)}, bf16[576,128]{1,0:T(8,128)(2,1)S(1)}, f32[2,128]{1,0:T(2,128)S(1)}) custom-call(s32[1]{0:T(128)} %bitcast.place_ref, s32[1]{0:T(128)} %bitcast.2.half_ref, s32[1,2]{1,0:T(1,128)} %bitcast.26, bf16[64,7680]{1,0:T(8,128)(2,1)} %bitcast.21, ...), custom_call_target="tpu_custom_call" | custom-call | bytes 983040 | tf_op jit(solution)/shard_map/split_far/pallas_call | solution.py:286
  8.7 1.6 %collective-permute-start.8 = (bf16[576,128]{1,0:T(8,128)(2,1)S(1)}, bf16[576,128]{1,0:T(8,128)(2,1)S(1)}, u32[]{:S(2)}, u32[]{:S(2)}) collective-permute-start(bf16[576,128]{1,0:T(8,128)(2,1)S(1)} %get-tuple-element.34), channel_id=1, source_target_pairs={{0,1},{1,0},{2,3},{3,2},{4,5},{5,4},{6,7},{7,6},{8,9},{9,8},{10,11... | collective-permute-start | bytes 442376 | tf_op jit(solution)/shard_map/ppermute | solution.py:652
  10.2 1.5 %collective-permute-start.9 = (bf16[576,128]{1,0:T(8,128)(2,1)S(1)}, bf16[576,128]{1,0:T(8,128)(2,1)S(1)}, u32[]{:S(2)}, u32[]{:S(2)}) collective-permute-start(bf16[576,128]{1,0:T(8,128)(2,1)S(1)} %get-tuple-element.35), channel_id=1, source_target_pairs={{0,3},{1,2},{2,1},{3,0},{4,7},{5,6},{6,5},{7,4},{8,11},{9,10},{10,... | collective-permute-start | bytes 442376 | tf_op jit(solution)/shard_map/ppermute | solution.py:652
  11.8 1.1 %collective-permute-start.11 = (bf16[576,128]{1,0:T(8,128)(2,1)S(1)}, bf16[576,128]{1,0:T(8,128)(2,1)S(1)}, u32[]{:S(2)}, u32[]{:S(2)}) collective-permute-start(bf16[576,128]{1,0:T(8,128)(2,1)S(1)} %get-tuple-element.37), channel_id=1, source_target_pairs={{0,7},{1,6},{2,5},{3,4},{4,3},{5,2},{6,1},{7,0},{8,15},{9,14},{10,... | collective-permute-start | bytes 442376 | tf_op jit(solution)/shard_map/ppermute | solution.py:652
  13.0 0.8 %cosine_convert_fusion = (bf16[2,128]{1,0:T(2,128)(2,1)S(1)}, f32[2,128]{1,0:T(2,128)S(1)}) fusion(f32[128]{0:T(128)S(1)} %multiply_exponential_fusion, f32[2,128]{1,0:T(2,128)S(1)} %get-tuple-element.33.refs_6_, f32[]{:T(128)} %bitcast.8, pred[2]{0:T(512)(128)(4,1)} %constant.16.clone.1), kind=kLoop, calls=%fused_computation.6 | loop fusion | flops 768 | bytes 3078 | tf_op jit(solution)/shard_map/convert | solution.py:767
  13.8 2.8 %collective-permute-done.10.refs_4_.refs_2_ = bf16[576,128]{1,0:T(8,128)(2,1)S(1)} collective-permute-done((bf16[576,128]{1,0:T(8,128)(2,1)S(1)}, bf16[576,128]{1,0:T(8,128)(2,1)S(1)}, u32[]{:S(2)}, u32[]{:S(2)}) %collective-permute-start.10) | collective-permute-done | bytes 147488 | tf_op jit(solution)/shard_map/ppermute | solution.py:652
  16.7 5.5 %collective-permute-done.8.refs_2_.refs_0_ = bf16[576,128]{1,0:T(8,128)(2,1)S(1)} collective-permute-done((bf16[576,128]{1,0:T(8,128)(2,1)S(1)}, bf16[576,128]{1,0:T(8,128)(2,1)S(1)}, u32[]{:S(2)}, u32[]{:S(2)}) %collective-permute-start.8) | collective-permute-done | bytes 147488 | tf_op jit(solution)/shard_map/ppermute | solution.py:652
  22.2 1.4 %collective-permute-start.17 = (bf16[384,128]{1,0:T(8,128)(2,1)S(1)}, bf16[384,128]{1,0:T(8,128)(2,1)S(1)}, u32[]{:S(2)}, u32[]{:S(2)}) collective-permute-start(bf16[384,128]{1,0:T(8,128)(2,1)S(1)} %collect.2.refs_1_), channel_id=1, source_target_pairs={{0,1},{1,0},{2,3},{3,2},{4,5},{5,4},{6,7},{7,6},{8,9},{9,8},{10,11... | collective-permute-start | bytes 294920 | tf_op jit(solution)/shard_map/ppermute | solution.py:645
  24.6 2.9 %collective-permute-done.7.refs_1_.refs_3_ = f32[1,960]{1,0:T(1,128)S(1)} collective-permute-done((f32[1,960]{1,0:T(1,128)S(1)}, f32[1,960]{1,0:T(1,128)S(1)}, u32[]{:S(2)}, u32[]{:S(2)}) %collective-permute-start.7) | collective-permute-done | bytes 3872 | tf_op jit(solution)/shard_map/ppermute | solution.py:645
  27.5 1.3 %attend_packed.3 = (bf16[192,128]{1,0:T(8,128)(2,1)S(1)}, bf16[192,128]{1,0:T(8,128)(2,1)S(1)}, bf16[192,128]{1,0:T(8,128)(2,1)S(1)}, bf16[192,128]{1,0:T(8,128)(2,1)S(1)}) custom-call(f32[2,960]{1,0:T(2,128)S(1)} %fusion.refs_0_.refs_2_, f32[1,960]{1,0:T(1,128)S(1)} %collective-permute-done.7.refs_1_.refs_3_, ...), custom_call_target="tpu_custom_call" | custom-call | flops 83886080 | bytes 655360 | tf_op jit(solution)/shard_map/attend_packed/pallas_call | solution.py:437
  29.2 1.4 %split_near.1 = (bf16[480,128]{1,0:T(8,128)(2,1)S(1)}, bf16[480,128]{1,0:T(8,128)(2,1)S(1)}, bf16[480,128]{1,0:T(8,128)(2,1)S(1)}, bf16[480,128]{1,0:T(8,128)(2,1)S(1)}) custom-call(s32[1]{0:T(128)} %bitcast.place_ref, s32[1]{0:T(128)} %bitcast.2.half_ref, bf16[64,7680]{1,0:T(8,128)(2,1)} %bitcast.22), custom_call_target="tpu_custom_call" | custom-call | bytes 983040 | tf_op jit(solution)/shard_map/split_near/pallas_call | solution.py:331
  30.6 1.8 %collective-permute-start = (bf16[480,128]{1,0:T(8,128)(2,1)S(1)}, bf16[480,128]{1,0:T(8,128)(2,1)S(1)}, u32[]{:S(2)}, u32[]{:S(2)}) collective-permute-start(bf16[480,128]{1,0:T(8,128)(2,1)S(1)} %get-tuple-element.25), channel_id=1, source_target_pairs={{0,2},{2,0},{4,6},{6,4},{1,3},{3,1},{5,7},{7,5},{8,10},{10,8},{12,... | collective-permute-start | bytes 368648 | tf_op jit(solution)/shard_map/ppermute | solution.py:642
  32.4 1.3 %collective-permute-start.1 = (bf16[480,128]{1,0:T(8,128)(2,1)S(1)}, bf16[480,128]{1,0:T(8,128)(2,1)S(1)}, u32[]{:S(2)}, u32[]{:S(2)}) collective-permute-start(bf16[480,128]{1,0:T(8,128)(2,1)S(1)} %get-tuple-element.26), channel_id=1, source_target_pairs={{0,4},{2,6},{4,0},{6,2},{1,5},{3,7},{5,1},{7,3},{8,12},{10,14},{12... | collective-permute-start | bytes 368648 | tf_op jit(solution)/shard_map/ppermute | solution.py:642
  33.7 1.6 %collective-permute-start.13 = (bf16[192,128]{1,0:T(8,128)(2,1)S(1)}, bf16[192,128]{1,0:T(8,128)(2,1)S(1)}, u32[]{:S(2)}, u32[]{:S(2)}) collective-permute-start(bf16[192,128]{1,0:T(8,128)(2,1)S(1)} %get-tuple-element.40), channel_id=1, source_target_pairs={{0,4},{2,6},{4,0},{6,2},{1,5},{3,7},{5,1},{7,3},{8,12},{10,14},{12... | collective-permute-start | bytes 147464 | tf_op jit(solution)/shard_map/ppermute | solution.py:642
  35.4 2.5 %collective-permute-start.14 = (bf16[192,128]{1,0:T(8,128)(2,1)S(1)}, bf16[192,128]{1,0:T(8,128)(2,1)S(1)}, u32[]{:S(2)}, u32[]{:S(2)}) collective-permute-start(bf16[192,128]{1,0:T(8,128)(2,1)S(1)} %get-tuple-element.41), channel_id=1, source_target_pairs={{0,6},{2,4},{4,2},{6,0},{1,7},{3,5},{5,3},{7,1},{8,14},{10,12},{12... | collective-permute-start | bytes 147464 | tf_op jit(solution)/shard_map/ppermute | solution.py:642
  37.9 1.3 %collective-permute-start.2 = (bf16[480,128]{1,0:T(8,128)(2,1)S(1)}, bf16[480,128]{1,0:T(8,128)(2,1)S(1)}, u32[]{:S(2)}, u32[]{:S(2)}) collective-permute-start(bf16[480,128]{1,0:T(8,128)(2,1)S(1)} %get-tuple-element.27), channel_id=1, source_target_pairs={{0,6},{2,4},{4,2},{6,0},{1,7},{3,5},{5,3},{7,1},{8,14},{10,12},{12... | collective-permute-start | bytes 368648 | tf_op jit(solution)/shard_map/ppermute | solution.py:642
  39.2 2.9 %load_rows.1.w_ref = bf16[1280,2560]{1,0:T(8,128)(2,1)S(1)} custom-call(s32[1]{0:T(128)} %bitcast.place_ref, bf16[1280,2560]{1,0:T(8,128)(2,1)} %bitcast.23), custom_call_target="tpu_custom_call" | custom-call | bytes 13107200 | tf_op jit(solution)/shard_map/load_rows/pallas_call | solution.py:366
  42.2 3.8 %collective-permute-done.13.refs_2_.refs_6_ = bf16[192,128]{1,0:T(8,128)(2,1)S(1)} collective-permute-done((bf16[192,128]{1,0:T(8,128)(2,1)S(1)}, bf16[192,128]{1,0:T(8,128)(2,1)S(1)}, u32[]{:S(2)}, u32[]{:S(2)}) %collective-permute-start.13) | collective-permute-done | bytes 49184 | tf_op jit(solution)/shard_map/ppermute | solution.py:642
  46.0 1.5 %collective-permute-start.18 = (bf16[768,128]{1,0:T(8,128)(2,1)S(1)}, bf16[768,128]{1,0:T(8,128)(2,1)S(1)}, u32[]{:S(2)}, u32[]{:S(2)}) collective-permute-start(bf16[768,128]{1,0:T(8,128)(2,1)S(1)} %collect.3.refs_0_), channel_id=1, source_target_pairs={{0,16},{16,0},{1,17},{17,1},{2,18},{18,2},{3,19},{19,3},{4,20},{20... | collective-permute-start | bytes 589832 | tf_op jit(solution)/shard_map/ppermute | solution.py:645
  48.2 1.0 %collective-permute-start.15 = (bf16[64,1280]{1,0:T(8,128)(2,1)S(1)}, bf16[64,1280]{1,0:T(8,128)(2,1)S(1)}, u32[]{:S(2)}, u32[]{:S(2)}) collective-permute-start(bf16[64,1280]{1,0:T(8,128)(2,1)S(1)} %project_packed.4), channel_id=1, source_target_pairs={{0,1},{1,0},{2,3},{3,2},{4,5},{5,4},{6,7},{7,6},{8,9},{9,8},{10,11... | collective-permute-start | bytes 491528 | tf_op jit(solution)/shard_map/ppermute | solution.py:645
  49.9 1.2 %collective-permute-start.16 = (bf16[64,1280]{1,0:T(8,128)(2,1)S(1)}, bf16[64,1280]{1,0:T(8,128)(2,1)S(1)}, u32[]{:S(2)}, u32[]{:S(2)}) collective-permute-start(bf16[64,1280]{1,0:T(8,128)(2,1)S(1)} %project_packed.5), channel_id=1, source_target_pairs={{0,1},{1,0},{2,3},{3,2},{4,5},{5,4},{6,7},{7,6},{8,9},{9,8},{10,11... | collective-permute-start | bytes 491528 | tf_op jit(solution)/shard_map/ppermute | solution.py:645
  51.1 1.3 %attend_packed.2 = (bf16[160,128]{1,0:T(8,128)(2,1)S(1)}, bf16[160,128]{1,0:T(8,128)(2,1)S(1)}, bf16[160,128]{1,0:T(8,128)(2,1)S(1)}, bf16[160,128]{1,0:T(8,128)(2,1)S(1)}) custom-call(bf16[480,128]{1,0:T(8,128)(2,1)S(1)} %get-tuple-element.24.refs_0_, bf16[480,128]{1,0:T(8,128)(2,1)S(1)} %collective-permute-done.refs_1_, ...), custom_call_target="tpu_custom_call" | custom-call | flops 83886080 | bytes 655360 | tf_op jit(solution)/shard_map/attend_packed/pallas_call | solution.py:437
  52.5 3.1 %collective-permute-start.4 = (bf16[160,128]{1,0:T(8,128)(2,1)S(1)}, bf16[160,128]{1,0:T(8,128)(2,1)S(1)}, u32[]{:S(2)}, u32[]{:S(2)}) collective-permute-start(bf16[160,128]{1,0:T(8,128)(2,1)S(1)} %get-tuple-element.30), channel_id=1, source_target_pairs={{0,4},{2,6},{4,0},{6,2},{1,5},{3,7},{5,1},{7,3},{8,12},{10,14},{12... | collective-permute-start | bytes 122888 | tf_op jit(solution)/shard_map/ppermute | solution.py:642
  55.6 0.9 %collective-permute-done.3.refs_1_ = bf16[160,128]{1,0:T(8,128)(2,1)S(1)} collective-permute-done((bf16[160,128]{1,0:T(8,128)(2,1)S(1)}, bf16[160,128]{1,0:T(8,128)(2,1)S(1)}, u32[]{:S(2)}, u32[]{:S(2)}) %collective-permute-start.3) | collective-permute-done | bytes 40992 | tf_op jit(solution)/shard_map/ppermute | solution.py:642
  56.5 2.5 %collective-permute-start.5 = (bf16[160,128]{1,0:T(8,128)(2,1)S(1)}, bf16[160,128]{1,0:T(8,128)(2,1)S(1)}, u32[]{:S(2)}, u32[]{:S(2)}) collective-permute-start(bf16[160,128]{1,0:T(8,128)(2,1)S(1)} %get-tuple-element.31), channel_id=1, source_target_pairs={{0,6},{2,4},{4,2},{6,0},{1,7},{3,5},{5,3},{7,1},{8,14},{10,12},{12... | collective-permute-start | bytes 122888 | tf_op jit(solution)/shard_map/ppermute | solution.py:642
  59.0 3.3 %collective-permute-done.5.refs_3_ = bf16[160,128]{1,0:T(8,128)(2,1)S(1)} collective-permute-done((bf16[160,128]{1,0:T(8,128)(2,1)S(1)}, bf16[160,128]{1,0:T(8,128)(2,1)S(1)}, u32[]{:S(2)}, u32[]{:S(2)}) %collective-permute-start.5) | collective-permute-done | bytes 40992 | tf_op jit(solution)/shard_map/ppermute | solution.py:642
  62.3 1.1 %project_packed.3.near_ref = f32[64,2560]{1,0:T(8,128)S(1)} custom-call(bf16[1280,2560]{1,0:T(8,128)(2,1)S(1)} %load_rows.1.w_ref, bf16[160,128]{1,0:T(8,128)(2,1)S(1)} %get-tuple-element.28.refs_0_, bf16[160,128]{1,0:T(8,128)(2,1)S(1)} %collective-permute-done.3.refs_1_, bf16[160,128]{1,0:T(8,128)(2,1)S(1)} %collective-permute-done.4.refs_2_, ...), custom_call_target="tpu_custom_call" | custom-call | flops 419430400 | bytes 6553600 | tf_op jit(solution)/shard_map/project_packed/pallas_call | solution.py:473
  63.7 1.2 %finish.1 = (f32[32,128]{1,0:T(8,128)}, f32[32,128]{1,0:T(8,128)S(1)}) custom-call(f32[64,2560]{1,0:T(8,128)S(1)} %project_packed.3.near_ref, bf16[64,1280]{1,0:T(8,128)(2,1)S(1)} %collective-permute-done.15.refs_0_, bf16[64,1280]{1,0:T(8,128)(2,1)S(1)} %collective-permute-done.16.refs_1_, f32[4,1,1920]{2,1,0:T(1,128)S(1)} %get-tuple-element.42.refs_2_, ...), custom_call_target="tpu_custom_call" | custom-call | flops 20971520 | bytes 1310720 | tf_op jit(solution)/shard_map/finish/pallas_call | solution.py:538
  64.9 1.2 %collective-permute-done.19 = f32[32,128]{1,0:T(8,128)S(1)} collective-permute-done((f32[32,128]{1,0:T(8,128)S(1)}, f32[32,128]{1,0:T(8,128)S(1)}, u32[]{:S(2)}, u32[]{:S(2)}) %collective-permute-start.19) | collective-permute-done | bytes 16416 | tf_op jit(solution)/shard_map/ppermute | solution.py:27
  (33 shorter events, 3.6 us)
Async XLA Ops:
  0.6 23.0 %copy-start = (bf16[1,256,960]{1,2,0:T(8,128)(2,1)S(1)}, bf16[1,256,960]{1,2,0:T(8,128)(2,1)}, u32[]{:S(2)}) copy-start(bf16[1,256,960]{1,2,0:T(8,128)(2,1)} %param.10) | copy-start | bytes 1474564
  0.6 12.3 %collective-permute-start.6 = (s32[1,1,2]{2,1,0:T(1,128)}, s32[1,1,2]{2,1,0:T(1,128)S(1)}, u32[]{:S(2)}, u32[]{:S(2)}) collective-permute-start(s32[1,1,2]{2,1,0:T(1,128)} %param.13), channel_id=1, source_target_pairs={{0,1},{1,0},{2,3},{3,2},{4,5},{5,4},{6,7},{7,6},{8,9},{9,8},{10,11... | collective-permute-start | bytes 32 | tf_op jit(solution)/shard_map/ppermute | solution.py:645
  4.7 12.0 %collective-permute-start.10 = (bf16[576,128]{1,0:T(8,128)(2,1)S(1)}, bf16[576,128]{1,0:T(8,128)(2,1)S(1)}, u32[]{:S(2)}, u32[]{:S(2)}) collective-permute-start(bf16[576,128]{1,0:T(8,128)(2,1)S(1)} %get-tuple-element.36), channel_id=1, source_target_pairs={{0,5},{1,4},{2,7},{3,6},{4,1},{5,0},{6,3},{7,2},{8,13},{9,12},{10,... | collective-permute-start | bytes 442376 | tf_op jit(solution)/shard_map/ppermute | solution.py:652
  8.7 13.5 %collective-permute-start.8 = (bf16[576,128]{1,0:T(8,128)(2,1)S(1)}, bf16[576,128]{1,0:T(8,128)(2,1)S(1)}, u32[]{:S(2)}, u32[]{:S(2)}) collective-permute-start(bf16[576,128]{1,0:T(8,128)(2,1)S(1)} %get-tuple-element.34), channel_id=1, source_target_pairs={{0,1},{1,0},{2,3},{3,2},{4,5},{5,4},{6,7},{7,6},{8,9},{9,8},{10,11... | collective-permute-start | bytes 442376 | tf_op jit(solution)/shard_map/ppermute | solution.py:652
  10.2 12.0 %collective-permute-start.9 = (bf16[576,128]{1,0:T(8,128)(2,1)S(1)}, bf16[576,128]{1,0:T(8,128)(2,1)S(1)}, u32[]{:S(2)}, u32[]{:S(2)}) collective-permute-start(bf16[576,128]{1,0:T(8,128)(2,1)S(1)} %get-tuple-element.35), channel_id=1, source_target_pairs={{0,3},{1,2},{2,1},{3,0},{4,7},{5,6},{6,5},{7,4},{8,11},{9,10},{10,... | collective-permute-start | bytes 442376 | tf_op jit(solution)/shard_map/ppermute | solution.py:652
  11.8 10.4 %collective-permute-start.11 = (bf16[576,128]{1,0:T(8,128)(2,1)S(1)}, bf16[576,128]{1,0:T(8,128)(2,1)S(1)}, u32[]{:S(2)}, u32[]{:S(2)}) collective-permute-start(bf16[576,128]{1,0:T(8,128)(2,1)S(1)} %get-tuple-element.37), channel_id=1, source_target_pairs={{0,7},{1,6},{2,5},{3,4},{4,3},{5,2},{6,1},{7,0},{8,15},{9,14},{10,... | collective-permute-start | bytes 442376 | tf_op jit(solution)/shard_map/ppermute | solution.py:652
  22.2 15.7 %collective-permute-start.17 = (bf16[384,128]{1,0:T(8,128)(2,1)S(1)}, bf16[384,128]{1,0:T(8,128)(2,1)S(1)}, u32[]{:S(2)}, u32[]{:S(2)}) collective-permute-start(bf16[384,128]{1,0:T(8,128)(2,1)S(1)} %collect.2.refs_1_), channel_id=1, source_target_pairs={{0,1},{1,0},{2,3},{3,2},{4,5},{5,4},{6,7},{7,6},{8,9},{9,8},{10,11... | collective-permute-start | bytes 294920 | tf_op jit(solution)/shard_map/ppermute | solution.py:645
  23.9 3.7 %collective-permute-start.7 = (f32[1,960]{1,0:T(1,128)S(1)}, f32[1,960]{1,0:T(1,128)S(1)}, u32[]{:S(2)}, u32[]{:S(2)}) collective-permute-start(f32[1,960]{1,0:T(1,128)S(1)} %slice.10), channel_id=1, source_target_pairs={{0,1},{1,0},{2,3},{3,2},{4,5},{5,4},{6,7},{7,6},{8,9},{9,8},{10,11... | collective-permute-start | bytes 11528 | tf_op jit(solution)/shard_map/ppermute | solution.py:645
  28.9 6.5 %collective-permute-start.12 = (bf16[192,128]{1,0:T(8,128)(2,1)S(1)}, bf16[192,128]{1,0:T(8,128)(2,1)S(1)}, u32[]{:S(2)}, u32[]{:S(2)}) collective-permute-start(bf16[192,128]{1,0:T(8,128)(2,1)S(1)} %get-tuple-element.39), channel_id=1, source_target_pairs={{0,2},{2,0},{4,6},{6,4},{1,3},{3,1},{5,7},{7,5},{8,10},{10,8},{12,... | collective-permute-start | bytes 147464 | tf_op jit(solution)/shard_map/ppermute | solution.py:642
  30.6 19.2 %collective-permute-start = (bf16[480,128]{1,0:T(8,128)(2,1)S(1)}, bf16[480,128]{1,0:T(8,128)(2,1)S(1)}, u32[]{:S(2)}, u32[]{:S(2)}) collective-permute-start(bf16[480,128]{1,0:T(8,128)(2,1)S(1)} %get-tuple-element.25), channel_id=1, source_target_pairs={{0,2},{2,0},{4,6},{6,4},{1,3},{3,1},{5,7},{7,5},{8,10},{10,8},{12,... | collective-permute-start | bytes 368648 | tf_op jit(solution)/shard_map/ppermute | solution.py:642
  32.4 18.6 %collective-permute-start.1 = (bf16[480,128]{1,0:T(8,128)(2,1)S(1)}, bf16[480,128]{1,0:T(8,128)(2,1)S(1)}, u32[]{:S(2)}, u32[]{:S(2)}) collective-permute-start(bf16[480,128]{1,0:T(8,128)(2,1)S(1)} %get-tuple-element.26), channel_id=1, source_target_pairs={{0,4},{2,6},{4,0},{6,2},{1,5},{3,7},{5,1},{7,3},{8,12},{10,14},{12... | collective-permute-start | bytes 368648 | tf_op jit(solution)/shard_map/ppermute | solution.py:642
  33.7 12.3 %collective-permute-start.13 = (bf16[192,128]{1,0:T(8,128)(2,1)S(1)}, bf16[192,128]{1,0:T(8,128)(2,1)S(1)}, u32[]{:S(2)}, u32[]{:S(2)}) collective-permute-start(bf16[192,128]{1,0:T(8,128)(2,1)S(1)} %get-tuple-element.40), channel_id=1, source_target_pairs={{0,4},{2,6},{4,0},{6,2},{1,5},{3,7},{5,1},{7,3},{8,12},{10,14},{12... | collective-permute-start | bytes 147464 | tf_op jit(solution)/shard_map/ppermute | solution.py:642
  35.4 12.2 %collective-permute-start.14 = (bf16[192,128]{1,0:T(8,128)(2,1)S(1)}, bf16[192,128]{1,0:T(8,128)(2,1)S(1)}, u32[]{:S(2)}, u32[]{:S(2)}) collective-permute-start(bf16[192,128]{1,0:T(8,128)(2,1)S(1)} %get-tuple-element.41), channel_id=1, source_target_pairs={{0,6},{2,4},{4,2},{6,0},{1,7},{3,5},{5,3},{7,1},{8,14},{10,12},{12... | collective-permute-start | bytes 147464 | tf_op jit(solution)/shard_map/ppermute | solution.py:642
  37.9 13.2 %collective-permute-start.2 = (bf16[480,128]{1,0:T(8,128)(2,1)S(1)}, bf16[480,128]{1,0:T(8,128)(2,1)S(1)}, u32[]{:S(2)}, u32[]{:S(2)}) collective-permute-start(bf16[480,128]{1,0:T(8,128)(2,1)S(1)} %get-tuple-element.27), channel_id=1, source_target_pairs={{0,6},{2,4},{4,2},{6,0},{1,7},{3,5},{5,3},{7,1},{8,14},{10,12},{12... | collective-permute-start | bytes 368648 | tf_op jit(solution)/shard_map/ppermute | solution.py:642
  46.0 17.4 %collective-permute-start.18 = (bf16[768,128]{1,0:T(8,128)(2,1)S(1)}, bf16[768,128]{1,0:T(8,128)(2,1)S(1)}, u32[]{:S(2)}, u32[]{:S(2)}) collective-permute-start(bf16[768,128]{1,0:T(8,128)(2,1)S(1)} %collect.3.refs_0_), channel_id=1, source_target_pairs={{0,16},{16,0},{1,17},{17,1},{2,18},{18,2},{3,19},{19,3},{4,20},{20... | collective-permute-start | bytes 589832 | tf_op jit(solution)/shard_map/ppermute | solution.py:645
  48.2 15.4 %copy-start.1 = (bf16[1,1,64,2560]{3,2,1,0:T(8,128)(2,1)S(1)}, bf16[1,1,64,2560]{3,2,1,0:T(8,128)(2,1)}, u32[]{:S(2)}) copy-start(bf16[1,1,64,2560]{3,2,1,0:T(8,128)(2,1)} %param.8) | copy-start | bytes 983044
  48.2 15.4 %copy-start.2 = (f32[1,1,32,128]{3,2,1,0:T(8,128)S(1)}, f32[1,1,32,128]{3,2,1,0:T(8,128)}, u32[]{:S(2)}) copy-start(f32[1,1,32,128]{3,2,1,0:T(8,128)} %param.12) | copy-start | bytes 49156
  48.2 15.4 %collective-permute-start.15 = (bf16[64,1280]{1,0:T(8,128)(2,1)S(1)}, bf16[64,1280]{1,0:T(8,128)(2,1)S(1)}, u32[]{:S(2)}, u32[]{:S(2)}) collective-permute-start(bf16[64,1280]{1,0:T(8,128)(2,1)S(1)} %project_packed.4), channel_id=1, source_target_pairs={{0,1},{1,0},{2,3},{3,2},{4,5},{5,4},{6,7},{7,6},{8,9},{9,8},{10,11... | collective-permute-start | bytes 491528 | tf_op jit(solution)/shard_map/ppermute | solution.py:645
  49.9 13.8 %collective-permute-start.16 = (bf16[64,1280]{1,0:T(8,128)(2,1)S(1)}, bf16[64,1280]{1,0:T(8,128)(2,1)S(1)}, u32[]{:S(2)}, u32[]{:S(2)}) collective-permute-start(bf16[64,1280]{1,0:T(8,128)(2,1)S(1)} %project_packed.5), channel_id=1, source_target_pairs={{0,1},{1,0},{2,3},{3,2},{4,5},{5,4},{6,7},{7,6},{8,9},{9,8},{10,11... | collective-permute-start | bytes 491528 | tf_op jit(solution)/shard_map/ppermute | solution.py:645
  52.4 4.1 %collective-permute-start.3 = (bf16[160,128]{1,0:T(8,128)(2,1)S(1)}, bf16[160,128]{1,0:T(8,128)(2,1)S(1)}, u32[]{:S(2)}, u32[]{:S(2)}) collective-permute-start(bf16[160,128]{1,0:T(8,128)(2,1)S(1)} %get-tuple-element.29), channel_id=1, source_target_pairs={{0,2},{2,0},{4,6},{6,4},{1,3},{3,1},{5,7},{7,5},{8,10},{10,8},{12,... | collective-permute-start | bytes 122888 | tf_op jit(solution)/shard_map/ppermute | solution.py:642
  52.5 6.5 %collective-permute-start.4 = (bf16[160,128]{1,0:T(8,128)(2,1)S(1)}, bf16[160,128]{1,0:T(8,128)(2,1)S(1)}, u32[]{:S(2)}, u32[]{:S(2)}) collective-permute-start(bf16[160,128]{1,0:T(8,128)(2,1)S(1)} %get-tuple-element.30), channel_id=1, source_target_pairs={{0,4},{2,6},{4,0},{6,2},{1,5},{3,7},{5,1},{7,3},{8,12},{10,14},{12... | collective-permute-start | bytes 122888 | tf_op jit(solution)/shard_map/ppermute | solution.py:642
  56.5 5.8 %collective-permute-start.5 = (bf16[160,128]{1,0:T(8,128)(2,1)S(1)}, bf16[160,128]{1,0:T(8,128)(2,1)S(1)}, u32[]{:S(2)}, u32[]{:S(2)}) collective-permute-start(bf16[160,128]{1,0:T(8,128)(2,1)S(1)} %get-tuple-element.31), channel_id=1, source_target_pairs={{0,6},{2,4},{4,2},{6,0},{1,7},{3,5},{5,3},{7,1},{8,14},{10,12},{12... | collective-permute-start | bytes 122888 | tf_op jit(solution)/shard_map/ppermute | solution.py:642
  64.9 1.2 %collective-permute-start.19 = (f32[32,128]{1,0:T(8,128)S(1)}, f32[32,128]{1,0:T(8,128)S(1)}, u32[]{:S(2)}, u32[]{:S(2)}) collective-permute-start(f32[32,128]{1,0:T(8,128)S(1)} %get-tuple-element.45), channel_id=1, source_target_pairs={{0,8},{8,0},{1,9},{9,1},{2,10},{10,2},{3,11},{11,3},{4,12},{12,4},... | collective-permute-start | bytes 49160 | tf_op jit(solution)/shard_map/ppermute | solution.py:27

commit v4 on v3

--- a/solution.py
+++ b/solution.py
@@ -259,7 +259,7 @@
     )
 
 
-def far_kernel(width, count, slots, place_ref, half_ref, when_ref, x_ref, pack_ref, *refs):
+def far_kernel(width, count, slots, rider, place_ref, half_ref, when_ref, x_ref, pack_ref, *refs):
     outs, (clock_ref, held, steps_ref, sems, steps_sem) = refs[: len(slots)], refs[len(slots) :]
     me = place_ref[0]
     copies = windows(x_ref, held, sems, me, 1 - half_ref[0], count, width, slots)
@@ -268,8 +268,7 @@
         copy.start()
     steps_copy.start()
     packed = held.shape[1] * width // LANES
-    for out in outs:
-        out[packed:, :] = pack_ref[...]
+    outs[slots.index(rider)][packed:, :] = pack_ref[...]
     for k, r in enumerate(slots):
         copies[k].wait()
         cut_window(width, held, outs[k], k, lax.rem(me ^ r, 2) == 1)
@@ -279,18 +278,18 @@
     clock_ref[...] = jnp.concatenate([now, change])
 
 
-def split_far(x, pack, steps, scalars, slots, count, halves):
+def split_far(x, pack, steps, scalars, slots, rider, count, halves):
     rows, columns = x.shape
     width = columns // halves // count
     length = rows * width // LANES
     results = pl.pallas_call(
-        functools.partial(far_kernel, width, count, slots),
+        functools.partial(far_kernel, width, count, slots, rider),
         in_specs=[pl.BlockSpec(memory_space=pltpu.SMEM)] * 2
         + [pl.BlockSpec(memory_space=pltpu.HBM)] * 2
         + [pl.BlockSpec(memory_space=pltpu.VMEM)],
         out_shape=[
-            jax.ShapeDtypeStruct((length + pack.shape[0], LANES), jnp.bfloat16)
-            for _ in slots
+            jax.ShapeDtypeStruct((length + pack.shape[0] * (r == rider), LANES), jnp.bfloat16)
+            for r in slots
         ]
         + [jax.ShapeDtypeStruct((2, LANES), jnp.float32)],
         scratch_shapes=[
@@ -422,8 +421,10 @@
             [rest[: rows // 2], rest[rows // 2 :]], axis=1
         ).astype(jnp.bfloat16)
         if riders:
-            for k, rider in enumerate(riders):
-                put_modulation(outs[b], packed + k * MOD_ROWS, rider[0:1, :])
+            mod_ref, other_ref = riders
+            put_modulation(outs[b], packed, mod_ref[0:1, :])
+            packed += MOD_ROWS
+            outs[b][packed : packed + MOD_ROWS, :] = other_ref[other_ref.shape[0] - MOD_ROWS :, :]
 
 
 def attend_packed(pieces, heads, rows, riders=()):
@@ -456,30 +457,41 @@
     )
 
 
-def project_kernel(rows, first, w_ref, *refs):
-    pieces, out_ref, left_ref = refs[:-2], refs[-2], refs[-1]
+def project_kernel(rows, first, slots, w_ref, *refs):
+    pieces, rest = refs[: len(slots)], refs[len(slots) :]
+    out_ref, left_ref = rest[-2:]
     gather_left(pieces, left_ref, rows)
+    depth = left_ref.shape[1] // len(slots)
     tile = math.gcd(out_ref.shape[1], 5 * LANES)
     for start in range(0, out_ref.shape[1], tile):
-        out_ref[:, start : start + tile] = jnp.dot(
-            left_ref[...],
-            w_ref[:, first + start : first + start + tile],
-            preferred_element_type=jnp.float32,
-        ).astype(out_ref.dtype)
-
-
-def project_packed(pieces, weight, rows, first, dim, dtype):
-    depth = weight.shape[0]
+        cut = slice(first + start, first + start + tile)
+        here = slice(start, start + tile)
+        right = [w_ref[r * depth : (r + 1) * depth, cut] for r in slots]
+        term = jnp.dot(
+            left_ref[...], jnp.concatenate(right, axis=0), preferred_element_type=jnp.float32
+        )
+        if len(rest) == 3:
+            term = rest[0][:, here] + term
+        out_ref[:, here] = term.astype(out_ref.dtype)
+
+
+def project_packed(pieces, slots, count, weight, rows, first, dim, dtype, base=()):
+    depth = weight.shape[0] // count
+    held = pltpu.with_memory_space_constraint(weight, pltpu.VMEM)
+    inputs = (*pieces, *base)
     return pl.pallas_call(
-        functools.partial(project_kernel, rows, first),
+        functools.partial(project_kernel, rows, first, slots),
+        in_specs=[pl.BlockSpec(memory_space=pltpu.VMEM)] * (1 + len(inputs)),
         out_shape=jax.ShapeDtypeStruct((rows, dim), dtype),
-        scratch_shapes=[pltpu.VMEM((rows, depth), jnp.bfloat16)],
+        scratch_shapes=[pltpu.VMEM((rows, depth * len(slots)), jnp.bfloat16)],
         compiler_params=pltpu.CompilerParams(vmem_limit_bytes=16 << 20),
         cost_estimate=pl.CostEstimate(
-            flops=2 * rows * depth * dim, transcendentals=0, bytes_accessed=2 * depth * dim
+            flops=2 * rows * depth * len(slots) * dim,
+            transcendentals=0,
+            bytes_accessed=2 * depth * len(slots) * dim,
         ),
         name="project_packed",
-    )(pltpu.with_memory_space_constraint(weight, pltpu.VMEM), *pieces)
+    )(held, *inputs)
 
 
 def finish_kernel(rows, near_ref, *refs):
@@ -551,29 +563,50 @@
     )(*inputs)
 
 
-def collect_kernel(start, *refs):
+def collect_kernel(starts, *refs):
     out_ref = refs[-1]
-    span = out_ref.shape[0] // (len(refs) - 1)
-    for r, ref in enumerate(refs[:-1]):
-        out_ref[r * span : (r + 1) * span, :] = ref[start : start + span, :]
-
-
-def collect(pieces, span, start):
+    span = out_ref.shape[0] // len(starts)
+    for k, (which, start) in enumerate(starts):
+        out_ref[k * span : (k + 1) * span, :] = refs[which][start : start + span, :]
+
+
+def collect(pieces, starts, span):
     return pl.pallas_call(
-        functools.partial(collect_kernel, start),
+        functools.partial(collect_kernel, starts),
         in_specs=[pl.BlockSpec(memory_space=pltpu.VMEM)] * len(pieces),
-        out_shape=jax.ShapeDtypeStruct((len(pieces) * span, LANES), jnp.bfloat16),
+        out_shape=jax.ShapeDtypeStruct((len(starts) * span, LANES), jnp.bfloat16),
         compiler_params=pltpu.CompilerParams(vmem_limit_bytes=4 << 20),
         cost_estimate=pl.CostEstimate(
-            flops=0, transcendentals=0, bytes_accessed=4 * len(pieces) * span * LANES
+            flops=0, transcendentals=0, bytes_accessed=4 * len(starts) * span * LANES
         ),
         name="collect",
     )(*pieces)
 
 
+def line_kernel(starts, *refs):
+    pieces, (mod_ref, out_ref) = refs[:-2], refs[-2:]
+    span = (out_ref.shape[0] - MOD_ROWS) // len(starts)
+    for k, start in enumerate(starts):
+        out_ref[k * span : (k + 1) * span, :] = pieces[k][start : start + span, :]
+    put_modulation(out_ref, out_ref.shape[0] - MOD_ROWS, mod_ref[1:2, :])
+
+
+def collect_line(pieces, starts, span, modulation):
+    return pl.pallas_call(
+        functools.partial(line_kernel, starts),
+        in_specs=[pl.BlockSpec(memory_space=pltpu.VMEM)] * (len(pieces) + 1),
+        out_shape=jax.ShapeDtypeStruct((len(starts) * span + MOD_ROWS, LANES), jnp.bfloat16),
+        compiler_params=pltpu.CompilerParams(vmem_limit_bytes=4 << 20),
+        cost_estimate=pl.CostEstimate(
+            flops=0, transcendentals=0, bytes_accessed=4 * len(starts) * span * LANES
+        ),
+        name="collect_line",
+    )(*pieces, modulation)
+
+
 def arrange_kernel(count, width, done, place_ref, half_ref, group_ref, *refs):
-    mine_ref, up_ref, mod_ref, mate_ref = refs[:4]
-    far = refs[4:-2]
+    mine_ref, up_ref, mod_ref, other_ref = refs[:4]
+    near = refs[4:-2]
     head_out, mod_out = refs[-2:]
     span = mine_ref.shape[0] // (2 * count)
     cut = head_out.shape[0] // 2
@@ -600,17 +633,18 @@
             [jnp.where(first, own, other), jnp.where(first, other, own)], axis=1
         )
         if r == 0:
-            own, other = mod_ref[0:1, :], mate_ref[...]
+            own = mod_ref[0:1, :]
+            other = get_modulation(other_ref, other_ref.shape[0] - MOD_ROWS, columns)
         else:
-            own = get_modulation(far[r], done, columns)
-            other = get_modulation(far[r], done + MOD_ROWS, columns)
+            own = get_modulation(near[r], done, columns)
+            other = get_modulation(near[r], done + MOD_ROWS, columns)
         mod_out[owner] = jnp.concatenate(
             [jnp.where(first, own, other), jnp.where(first, other, own)], axis=1
         )
 
 
-def arrange(mine, up, modulation, mate, far, head, scalars, done):
-    count = len(far)
+def arrange(mine, up, modulation, other, near, head, scalars, done):
+    count = len(near)
     patch, width = head.shape
     columns = modulation.shape[1]
     return pl.pallas_call(
@@ -626,7 +660,7 @@
             flops=0, transcendentals=0, bytes_accessed=8 * count * patch * width
         ),
         name="arrange",
-    )(*scalars, mine, up, modulation, mate, *far)
+    )(*scalars, mine, up, modulation, other, *near)
 
 
 def packed_body(head_inputs, hidden, out_weight, time_weight, head_weight, latent, timesteps):
@@ -661,7 +695,7 @@
     last = count // 2
     slots = [r for r in range(count - 1, 0, -1) if r != last] + [0]
     first, pack = split_first(x, head, scalars, last, count, halves)
-    sent, clock = split_far(x, pack, timesteps.reshape(1, 2), scalars, slots, count, halves)
+    sent, clock = split_far(x, pack, timesteps.reshape(1, 2), scalars, slots, 1, count, halves)
     far_sent = [first if r == last else sent[slots.index(r)] for r in range(count)]
     far_pieces = [slanted(far_sent[r], r) for r in range(count)]
 
@@ -673,35 +707,45 @@
     angle = angle * freqs
     embedding = jnp.concatenate([jnp.cos(angle), jnp.sin(angle)], axis=-1).astype(jnp.bfloat16)
     modulation = jnp.dot(embedding, time_weight[0], preferred_element_type=jnp.float32)
-    mate = swap(modulation[1:], "fsdp")
 
     near_sent = split_near(x, scalars, count, halves)
     near_pieces = [near_sent[0]] + [along(near_sent[r], r) for r in range(1, count)]
 
     weight = load_rows(out_weight[0], here, count)
-    far_attended = attend_packed(far_pieces, heads, rows, (modulation, mate))
+    far_attended = attend_packed(far_pieces, heads, rows)
     far_home = [far_attended[0]]
     far_home += [along(far_attended[r], r) for r in range(1, count)]
     part = DIM // 2
     partial = []
     for k in range(2):
-        term = project_packed(far_home, weight, rows, k * part, part, jnp.bfloat16)
+        term = project_packed(
+            far_home, range(count), count, weight, rows, k * part, part, jnp.bfloat16
+        )
         partial.append(swap(term, "fsdp"))
 
     packed = near_sent[0].shape[0]
-    done = far_home[0].shape[0] - 2 * MOD_ROWS
-    line = collect(far_pieces, span, packed)
+    relay = collect([far_pieces[2]], [(0, packed)], span)
+    relayed = along(relay, 1)
+    line = collect_line(
+        [pack, far_pieces[1], far_pieces[2], relayed], [0, packed, packed, 0], span, modulation
+    )
     other = swap(line, "fsdp")
-    mine = collect([other, line], line.shape[0], 0)
+    own_slots = [(0 if r == 0 else 1, r * span) for r in range(count)]
+    far_slots = [(1 if r == 0 else 0, r * span) for r in range(count)]
+    mine = collect([line, other], own_slots + far_slots, span)
     up = swap(mine, "grp")
-    head_rows, lines = arrange(
-        mine, up, modulation, mate, far_home, head, scalars, done
-    )
-
-    near_attended = attend_packed(near_pieces, heads, rows)
+    near_attended = attend_packed(near_pieces, heads, rows, (modulation, other))
     near_home = [near_attended[0]]
     near_home += [along(near_attended[r], r) for r in range(1, count)]
-    projected = project_packed(near_home, weight, rows, 0, DIM, jnp.float32)
+    done = near_home[0].shape[0] - 2 * MOD_ROWS
+    head_rows, lines = arrange(mine, up, modulation, other, near_home, head, scalars, done)
+    others = [r for r in range(count) if r != 1]
+    most = project_packed(
+        [near_home[r] for r in others], others, count, weight, rows, 0, DIM, jnp.float32
+    )
+    projected = project_packed(
+        [near_home[1]], [1], count, weight, rows, 0, DIM, jnp.float32, (most,)
+    )
     velocity, stepped = finish(
         projected,
         partial,
@@ -724,7 +768,7 @@
         and FREQ == 2 * LANES
         and 2 * PATCH == LANES
         and mesh.shape["grp"] == 2
-        and count & (count - 1) == 0
+        and count == 4
         and HEADS % (halves * count) == 0
         and 3 * DIM // (halves * count) <= 8 * LANES
         and DIM % (halves * count) == 0

time: 66.9 us -> 58.5 us (0.87)
  waiting for transfers between devices: 20.6 us -> 12.6 us
    ppermute x9 -> x10, waiting for transfers between devices: 8.04 us -> 3.39 us  [along(): return lax.ppermute(block, 'seq', [(i, i ^ r) for i in range(count)])]
    ppermute x6 -> x5, waiting for transfers between devices: 2.95 us -> 0.01 us  [swap(): return lax.ppermute(block, axis, [(0, 1), (1, 0)])]
    ppermute x4, starting transfers between devices: 6.88 us -> 5.98 us  [slanted(): return lax.ppermute(block, ('seq', 'fsdp'), route)]
    ppermute x9 -> x10, starting transfers between devices: 14.6 us -> 15.4 us  [along(): return lax.ppermute(block, 'seq', [(i, i ^ r) for i in range(count)])]
    ppermute x6 -> x5, starting transfers between devices: 8.88 us -> 8.29 us  [swap(): return lax.ppermute(block, axis, [(0, 1), (1, 0)])]
    pallas_call x6 -> x8, Pallas kernels: 3.82 us -> 4.11 us  [the longest x4 2.74 us: project_packed(): pl.pallas_call(functools.partial(project_kernel, rows, first, slots), in_...]
  transfers between devices with their start and end apart: 20 -> 20, of which waited for: 7 -> 6; matrix products, arithmetic and copies ran while one was open for 2% -> 2% of each run, Pallas kernels for 18% -> 21%
where the time goes in v4:
time: 58.5 us; the launch traced here: 58.3 us
  starting transfers between devices  29.7 us (51%)
  Pallas kernels  13.5 us (23%)
  waiting for transfers between devices  12.6 us (22%)
  between operations  0.86 us (1%)
  other arithmetic  0.82 us (1%)
  local copies, waits for them, and re-layouts  0.62 us (1%)
    ppermute x10, starting transfers between devices, along(): return lax.ppermute(block, 'seq', [(i, i ^ r) for i in range(count)])  15.4 us
    ppermute x5, starting transfers between devices, swap(): return lax.ppermute(block, axis, [(0, 1), (1, 0)])  8.29 us
    ppermute x4, waiting for transfers between devices, slanted(): return lax.ppermute(block, ('seq', 'fsdp'), route)  8 us
    ppermute x4, starting transfers between devices, slanted(): return lax.ppermute(block, ('seq', 'fsdp'), route)  5.98 us
    ppermute x10, waiting for transfers between devices, along(): return lax.ppermute(block, 'seq', [(i, i ^ r) for i in range(count)])  3.39 us
    pallas_call x1, Pallas kernels, load_rows(): pl.pallas_call(functools.partial(load_kernel, count), in_specs=[pl.BlockS...  2.95 us
    pallas_call x4, Pallas kernels, project_packed(): pl.pallas_call(functools.partial(project_kernel, rows, first, slots), in_...  2.74 us
    pallas_call x2, Pallas kernels, attend_packed(): pl.pallas_call(functools.partial(attend_kernel, heads, rows, count), in_s...  2.67 us
  transfers between devices with their start and end apart: 20, of which 6 were waited for; matrix products, arithmetic and copies ran while one was open for 2% of the time, Pallas kernels for 21%

profile of v4, /device:TPU:0, one launch (start us, length us, event | category | flops | bytes accessed | tf_op | source)
XLA Modules:
  0.0 58.3 jit_solution(3076716863093036940)
XLA Ops:
  0.6 3.0 %collective-permute-start = (s32[1,1,2]{2,1,0:T(1,128)}, s32[1,1,2]{2,1,0:T(1,128)S(1)}, u32[]{:S(2)}, u32[]{:S(2)}) collective-permute-start(s32[1,1,2]{2,1,0:T(1,128)} %param.13), channel_id=1, source_target_pairs={{0,1},{1,0},{2,3},{3,2},{4,5},{5,4},{6,7},{7,6},{8,9},{9,8},{10,11... | collective-permute-start | bytes 32 | tf_op jit(solution)/shard_map/ppermute | solution.py:679
  3.7 1.0 %split_first.1 = (bf16[576,128]{1,0:T(8,128)(2,1)S(1)}, bf16[96,128]{1,0:T(8,128)(2,1)S(1)}) custom-call(s32[1]{0:T(128)} %bitcast.place_ref, s32[1]{0:T(128)} %bitcast.2.half_ref, s32[1]{0:T(128)} %bitcast.5.group_ref, bf16[64,7680]{1,0:T(8,128)(2,1)} %bitcast.20, bf16[64,320]{1,0:T(8,128)(2,1)} %bitcast.24), custom_call_target="tpu_custom_call" | custom-call | bytes 245760 | tf_op jit(solution)/shard_map/split_first/pallas_call | solution.py:236
  4.7 2.6 %collective-permute-start.2 = (bf16[576,128]{1,0:T(8,128)(2,1)S(1)}, bf16[576,128]{1,0:T(8,128)(2,1)S(1)}, u32[]{:S(2)}, u32[]{:S(2)}) collective-permute-start(bf16[576,128]{1,0:T(8,128)(2,1)S(1)} %get-tuple-element.27), channel_id=1, source_target_pairs={{0,5},{1,4},{2,7},{3,6},{4,1},{5,0},{6,3},{7,2},{8,13},{9,12},{10,... | collective-permute-start | bytes 442376 | tf_op jit(solution)/shard_map/ppermute | solution.py:686
  7.3 1.3 %split_far.1 = (bf16[480,128]{1,0:T(8,128)(2,1)S(1)}, bf16[576,128]{1,0:T(8,128)(2,1)S(1)}, bf16[480,128]{1,0:T(8,128)(2,1)S(1)}, f32[2,128]{1,0:T(2,128)S(1)}) custom-call(s32[1]{0:T(128)} %bitcast.place_ref, s32[1]{0:T(128)} %bitcast.2.half_ref, s32[1,2]{1,0:T(1,128)} %bitcast.26, bf16[64,7680]{1,0:T(8,128)(2,1)} %bitcast.21, ...), custom_call_target="tpu_custom_call" | custom-call | bytes 983040 | tf_op jit(solution)/shard_map/split_far/pallas_call | solution.py:285
  8.7 1.6 %collective-permute-start.11 = (bf16[480,128]{1,0:T(8,128)(2,1)S(1)}, bf16[480,128]{1,0:T(8,128)(2,1)S(1)}, u32[]{:S(2)}, u32[]{:S(2)}) collective-permute-start(bf16[480,128]{1,0:T(8,128)(2,1)S(1)} %get-tuple-element.36), channel_id=1, source_target_pairs={{0,1},{1,0},{2,3},{3,2},{4,5},{5,4},{6,7},{7,6},{8,9},{9,8},{10,11... | collective-permute-start | bytes 368648 | tf_op jit(solution)/shard_map/ppermute | solution.py:686
  10.2 1.3 %collective-permute-start.12 = (bf16[480,128]{1,0:T(8,128)(2,1)S(1)}, bf16[480,128]{1,0:T(8,128)(2,1)S(1)}, u32[]{:S(2)}, u32[]{:S(2)}) collective-permute-start(bf16[480,128]{1,0:T(8,128)(2,1)S(1)} %get-tuple-element.37), channel_id=1, source_target_pairs={{0,7},{1,6},{2,5},{3,4},{4,3},{5,2},{6,1},{7,0},{8,15},{9,14},{10,... | collective-permute-start | bytes 368648 | tf_op jit(solution)/shard_map/ppermute | solution.py:686
  12.1 0.8 %cosine_convert_fusion = (bf16[2,128]{1,0:T(2,128)(2,1)S(1)}, f32[2,128]{1,0:T(2,128)S(1)}) fusion(f32[128]{0:T(128)S(1)} %multiply_exponential_fusion, f32[2,128]{1,0:T(2,128)S(1)} %get-tuple-element.25.refs_6_, f32[]{:T(128)} %bitcast.8, pred[2]{0:T(512)(128)(4,1)} %constant.16.clone.1), kind=kLoop, calls=%fused_computation.6 | loop fusion | flops 768 | bytes 3078 | tf_op jit(solution)/shard_map/convert | solution.py:811
  12.9 5.7 %collective-permute-done.2.refs_0_.refs_2_ = bf16[576,128]{1,0:T(8,128)(2,1)S(1)} collective-permute-done((bf16[576,128]{1,0:T(8,128)(2,1)S(1)}, bf16[576,128]{1,0:T(8,128)(2,1)S(1)}, u32[]{:S(2)}, u32[]{:S(2)}) %collective-permute-start.2) | collective-permute-done | bytes 147488 | tf_op jit(solution)/shard_map/ppermute | solution.py:686
  18.8 2.3 %collective-permute-done.1.refs_1_ = bf16[576,128]{1,0:T(8,128)(2,1)S(1)} collective-permute-done((bf16[576,128]{1,0:T(8,128)(2,1)S(1)}, bf16[576,128]{1,0:T(8,128)(2,1)S(1)}, u32[]{:S(2)}, u32[]{:S(2)}) %collective-permute-start.1) | collective-permute-done | bytes 147488 | tf_op jit(solution)/shard_map/ppermute | solution.py:686
  21.1 1.3 %collective-permute-done.3.refs_3_ = bf16[96,128]{1,0:T(8,128)(2,1)S(1)} collective-permute-done((bf16[96,128]{1,0:T(8,128)(2,1)S(1)}, bf16[96,128]{1,0:T(8,128)(2,1)S(1)}, u32[]{:S(2)}, u32[]{:S(2)}) %collective-permute-start.3) | collective-permute-done | bytes 24608 | tf_op jit(solution)/shard_map/ppermute | solution.py:676
  22.9 1.4 %split_near.1 = (bf16[480,128]{1,0:T(8,128)(2,1)S(1)}, bf16[480,128]{1,0:T(8,128)(2,1)S(1)}, bf16[480,128]{1,0:T(8,128)(2,1)S(1)}, bf16[480,128]{1,0:T(8,128)(2,1)S(1)}) custom-call(s32[1]{0:T(128)} %bitcast.place_ref, s32[1]{0:T(128)} %bitcast.2.half_ref, bf16[64,7680]{1,0:T(8,128)(2,1)} %bitcast.22), custom_call_target="tpu_custom_call" | custom-call | bytes 983040 | tf_op jit(solution)/shard_map/split_near/pallas_call | solution.py:330
  24.4 1.3 %attend_packed.3 = (bf16[160,128]{1,0:T(8,128)(2,1)S(1)}, bf16[160,128]{1,0:T(8,128)(2,1)S(1)}, bf16[160,128]{1,0:T(8,128)(2,1)S(1)}, bf16[160,128]{1,0:T(8,128)(2,1)S(1)}) custom-call(bf16[480,128]{1,0:T(8,128)(2,1)S(1)} %collective-permute-done.11.refs_0_, bf16[576,128]{1,0:T(8,128)(2,1)S(1)} %collective-permute-done.1.refs_1_, ...), custom_call_target="tpu_custom_call" | custom-call | flops 83886080 | bytes 655360 | tf_op jit(solution)/shard_map/attend_packed/pallas_call | solution.py:438
  25.8 2.0 %collective-permute-start.13 = (bf16[160,128]{1,0:T(8,128)(2,1)S(1)}, bf16[160,128]{1,0:T(8,128)(2,1)S(1)}, u32[]{:S(2)}, u32[]{:S(2)}) collective-permute-start(bf16[160,128]{1,0:T(8,128)(2,1)S(1)} %get-tuple-element.39), channel_id=1, source_target_pairs={{0,2},{2,0},{4,6},{6,4},{1,3},{3,1},{5,7},{7,5},{8,10},{10,8},{12,... | collective-permute-start | bytes 122888 | tf_op jit(solution)/shard_map/ppermute | solution.py:676
  27.8 1.6 %collective-permute-start.14 = (bf16[160,128]{1,0:T(8,128)(2,1)S(1)}, bf16[160,128]{1,0:T(8,128)(2,1)S(1)}, u32[]{:S(2)}, u32[]{:S(2)}) collective-permute-start(bf16[160,128]{1,0:T(8,128)(2,1)S(1)} %get-tuple-element.40), channel_id=1, source_target_pairs={{0,4},{2,6},{4,0},{6,2},{1,5},{3,7},{5,1},{7,3},{8,12},{10,14},{12... | collective-permute-start | bytes 122888 | tf_op jit(solution)/shard_map/ppermute | solution.py:676
  29.4 1.4 %collective-permute-start.15 = (bf16[160,128]{1,0:T(8,128)(2,1)S(1)}, bf16[160,128]{1,0:T(8,128)(2,1)S(1)}, u32[]{:S(2)}, u32[]{:S(2)}) collective-permute-start(bf16[160,128]{1,0:T(8,128)(2,1)S(1)} %get-tuple-element.41), channel_id=1, source_target_pairs={{0,6},{2,4},{4,2},{6,0},{1,7},{3,5},{5,3},{7,1},{8,14},{10,12},{12... | collective-permute-start | bytes 122888 | tf_op jit(solution)/shard_map/ppermute | solution.py:676
  30.7 2.8 %collective-permute-start.6 = (bf16[480,128]{1,0:T(8,128)(2,1)S(1)}, bf16[480,128]{1,0:T(8,128)(2,1)S(1)}, u32[]{:S(2)}, u32[]{:S(2)}) collective-permute-start(bf16[480,128]{1,0:T(8,128)(2,1)S(1)} %get-tuple-element.30), channel_id=1, source_target_pairs={{0,4},{2,6},{4,0},{6,2},{1,5},{3,7},{5,1},{7,3},{8,12},{10,14},{12... | collective-permute-start | bytes 368648 | tf_op jit(solution)/shard_map/ppermute | solution.py:676
  34.1 2.9 %load_rows.1.w_ref = bf16[1280,2560]{1,0:T(8,128)(2,1)S(1)} custom-call(s32[1]{0:T(128)} %bitcast.place_ref, bf16[1280,2560]{1,0:T(8,128)(2,1)} %bitcast.23), custom_call_target="tpu_custom_call" | custom-call | bytes 13107200 | tf_op jit(solution)/shard_map/load_rows/pallas_call | solution.py:365
  37.1 2.7 %collective-permute-start.18 = (bf16[768,128]{1,0:T(8,128)(2,1)S(1)}, bf16[768,128]{1,0:T(8,128)(2,1)S(1)}, u32[]{:S(2)}, u32[]{:S(2)}) collective-permute-start(bf16[768,128]{1,0:T(8,128)(2,1)S(1)} %collect.3.refs_0_), channel_id=1, source_target_pairs={{0,16},{16,0},{1,17},{17,1},{2,18},{18,2},{3,19},{19,3},{4,20},{20... | collective-permute-start | bytes 589832 | tf_op jit(solution)/shard_map/ppermute | solution.py:679
  39.8 0.7 %project_packed.6 = bf16[64,1280]{1,0:T(8,128)(2,1)S(1)} custom-call(bf16[1280,2560]{1,0:T(8,128)(2,1)S(1)} %load_rows.1.w_ref, bf16[160,128]{1,0:T(8,128)(2,1)S(1)} %get-tuple-element.38.refs_0_, bf16[160,128]{1,0:T(8,128)(2,1)S(1)} %collective-permute-done.13.refs_1_, bf16[160,128]{1,0:T(8,128)(2,1)S(1)} %collective-permute-done.14.refs_2_, ...), custom_call_target="tpu_custom_call" | custom-call | flops 209715200 | bytes 3276800 | tf_op jit(solution)/shard_map/project_packed/pallas_call | solution.py:482
  40.4 1.6 %collective-permute-start.16 = (bf16[64,1280]{1,0:T(8,128)(2,1)S(1)}, bf16[64,1280]{1,0:T(8,128)(2,1)S(1)}, u32[]{:S(2)}, u32[]{:S(2)}) collective-permute-start(bf16[64,1280]{1,0:T(8,128)(2,1)S(1)} %project_packed.6), channel_id=1, source_target_pairs={{0,1},{1,0},{2,3},{3,2},{4,5},{5,4},{6,7},{7,6},{8,9},{9,8},{10,11... | collective-permute-start | bytes 491528 | tf_op jit(solution)/shard_map/ppermute | solution.py:679
  42.0 0.7 %project_packed.7 = bf16[64,1280]{1,0:T(8,128)(2,1)S(1)} custom-call(bf16[1280,2560]{1,0:T(8,128)(2,1)S(1)} %load_rows.1.w_ref, bf16[160,128]{1,0:T(8,128)(2,1)S(1)} %get-tuple-element.38.refs_0_, bf16[160,128]{1,0:T(8,128)(2,1)S(1)} %collective-permute-done.13.refs_1_, bf16[160,128]{1,0:T(8,128)(2,1)S(1)} %collective-permute-done.14.refs_2_, ...), custom_call_target="tpu_custom_call" | custom-call | flops 209715200 | bytes 3276800 | tf_op jit(solution)/shard_map/project_packed/pallas_call | solution.py:482
  42.7 0.6 %collective-permute-start.17 = (bf16[64,1280]{1,0:T(8,128)(2,1)S(1)}, bf16[64,1280]{1,0:T(8,128)(2,1)S(1)}, u32[]{:S(2)}, u32[]{:S(2)}) collective-permute-start(bf16[64,1280]{1,0:T(8,128)(2,1)S(1)} %project_packed.7), channel_id=1, source_target_pairs={{0,1},{1,0},{2,3},{3,2},{4,5},{5,4},{6,7},{7,6},{8,9},{9,8},{10,11... | collective-permute-start | bytes 491528 | tf_op jit(solution)/shard_map/ppermute | solution.py:679
  43.3 1.3 %attend_packed.2 = (bf16[192,128]{1,0:T(8,128)(2,1)S(1)}, bf16[192,128]{1,0:T(8,128)(2,1)S(1)}, bf16[192,128]{1,0:T(8,128)(2,1)S(1)}, bf16[192,128]{1,0:T(8,128)(2,1)S(1)}) custom-call(f32[2,960]{1,0:T(2,128)S(1)} %fusion.refs_4_.refs_0_.refs_2_, bf16[400,128]{1,0:T(8,128)(2,1)S(1)} %collective-permute-done.4.refs_1_.refs_3_, ...), custom_call_target="tpu_custom_call" | custom-call | flops 83886080 | bytes 655360 | tf_op jit(solution)/shard_map/attend_packed/pallas_call | solution.py:438
  44.6 2.9 %collective-permute-start.9 = (bf16[192,128]{1,0:T(8,128)(2,1)S(1)}, bf16[192,128]{1,0:T(8,128)(2,1)S(1)}, u32[]{:S(2)}, u32[]{:S(2)}) collective-permute-start(bf16[192,128]{1,0:T(8,128)(2,1)S(1)} %get-tuple-element.34), channel_id=1, source_target_pairs={{0,4},{2,6},{4,0},{6,2},{1,5},{3,7},{5,1},{7,3},{8,12},{10,14},{12... | collective-permute-start | bytes 147464 | tf_op jit(solution)/shard_map/ppermute | solution.py:676
  47.5 1.8 %collective-permute-start.10 = (bf16[192,128]{1,0:T(8,128)(2,1)S(1)}, bf16[192,128]{1,0:T(8,128)(2,1)S(1)}, u32[]{:S(2)}, u32[]{:S(2)}) collective-permute-start(bf16[192,128]{1,0:T(8,128)(2,1)S(1)} %get-tuple-element.35), channel_id=1, source_target_pairs={{0,6},{2,4},{4,2},{6,0},{1,7},{3,5},{5,3},{7,1},{8,14},{10,12},{12... | collective-permute-start | bytes 147464 | tf_op jit(solution)/shard_map/ppermute | solution.py:676
  49.3 0.9 %collective-permute-done.9.refs_1_.refs_6_ = bf16[192,128]{1,0:T(8,128)(2,1)S(1)} collective-permute-done((bf16[192,128]{1,0:T(8,128)(2,1)S(1)}, bf16[192,128]{1,0:T(8,128)(2,1)S(1)}, u32[]{:S(2)}, u32[]{:S(2)}) %collective-permute-start.9) | collective-permute-done | bytes 49184 | tf_op jit(solution)/shard_map/ppermute | solution.py:676
  50.2 2.2 %collective-permute-start.8 = (bf16[192,128]{1,0:T(8,128)(2,1)S(1)}, bf16[192,128]{1,0:T(8,128)(2,1)S(1)}, u32[]{:S(2)}, u32[]{:S(2)}) collective-permute-start(bf16[192,128]{1,0:T(8,128)(2,1)S(1)} %get-tuple-element.32), channel_id=1, source_target_pairs={{0,2},{2,0},{4,6},{6,4},{1,3},{3,1},{5,7},{7,5},{8,10},{10,8},{12,... | collective-permute-start | bytes 147464 | tf_op jit(solution)/shard_map/ppermute | solution.py:676
  52.4 1.2 %collective-permute-done.10.refs_2_.refs_7_ = bf16[192,128]{1,0:T(8,128)(2,1)S(1)} collective-permute-done((bf16[192,128]{1,0:T(8,128)(2,1)S(1)}, bf16[192,128]{1,0:T(8,128)(2,1)S(1)}, u32[]{:S(2)}, u32[]{:S(2)}) %collective-permute-start.10) | collective-permute-done | bytes 49184 | tf_op jit(solution)/shard_map/ppermute | solution.py:676
  53.6 0.9 %project_packed.4.refs_1_ = f32[64,2560]{1,0:T(8,128)S(1)} custom-call(bf16[1280,2560]{1,0:T(8,128)(2,1)S(1)} %load_rows.1.w_ref, bf16[192,128]{1,0:T(8,128)(2,1)S(1)} %get-tuple-element.33.refs_0_.refs_4_, bf16[192,128]{1,0:T(8,128)(2,1)S(1)} %collective-permute-done.9.refs_1_.refs_6_, bf16[192,128]{1,0:T(8,128)(2,1)S(1)} %collective-permute-done.10.refs_2_.refs_7_), custom_call_target="tpu_custom_call" | custom-call | flops 314572800 | bytes 4915200 | tf_op jit(solution)/shard_map/project_packed/pallas_call | solution.py:482
  55.3 1.2 %finish.1 = (f32[32,128]{1,0:T(8,128)}, f32[32,128]{1,0:T(8,128)S(1)}) custom-call(f32[64,2560]{1,0:T(8,128)S(1)} %project_packed.5.near_ref, bf16[64,1280]{1,0:T(8,128)(2,1)S(1)} %collective-permute-done.16.refs_0_, bf16[64,1280]{1,0:T(8,128)(2,1)S(1)} %collective-permute-done.17.refs_1_, f32[4,1,1920]{2,1,0:T(1,128)S(1)} %get-tuple-element.42.refs_2_, ...), custom_call_target="tpu_custom_call" | custom-call | flops 20971520 | bytes 1310720 | tf_op jit(solution)/shard_map/finish/pallas_call | solution.py:550
  56.5 1.2 %collective-permute-done.19 = f32[32,128]{1,0:T(8,128)S(1)} collective-permute-done((f32[32,128]{1,0:T(8,128)S(1)}, f32[32,128]{1,0:T(8,128)S(1)}, u32[]{:S(2)}, u32[]{:S(2)}) %collective-permute-start.19) | collective-permute-done | bytes 16416 | tf_op jit(solution)/shard_map/ppermute | solution.py:27
  57.7 0.6 %copy.10 = f32[1,1,32,128]{3,2,1,0:T(8,128)} copy(f32[1,1,32,128]{3,2,1,0:T(8,128)S(1)} %bitcast.25) | data formatting | bytes 32768
  (34 shorter events, 2.7 us)
Async XLA Ops:
  0.6 17.9 %copy-start = (bf16[1,256,960]{1,2,0:T(8,128)(2,1)S(1)}, bf16[1,256,960]{1,2,0:T(8,128)(2,1)}, u32[]{:S(2)}) copy-start(bf16[1,256,960]{1,2,0:T(8,128)(2,1)} %param.10) | copy-start | bytes 1474564
  0.6 11.4 %collective-permute-start = (s32[1,1,2]{2,1,0:T(1,128)}, s32[1,1,2]{2,1,0:T(1,128)S(1)}, u32[]{:S(2)}, u32[]{:S(2)}) collective-permute-start(s32[1,1,2]{2,1,0:T(1,128)} %param.13), channel_id=1, source_target_pairs={{0,1},{1,0},{2,3},{3,2},{4,5},{5,4},{6,7},{7,6},{8,9},{9,8},{10,11... | collective-permute-start | bytes 32 | tf_op jit(solution)/shard_map/ppermute | solution.py:679
  4.7 13.9 %collective-permute-start.2 = (bf16[576,128]{1,0:T(8,128)(2,1)S(1)}, bf16[576,128]{1,0:T(8,128)(2,1)S(1)}, u32[]{:S(2)}, u32[]{:S(2)}) collective-permute-start(bf16[576,128]{1,0:T(8,128)(2,1)S(1)} %get-tuple-element.27), channel_id=1, source_target_pairs={{0,5},{1,4},{2,7},{3,6},{4,1},{5,0},{6,3},{7,2},{8,13},{9,12},{10,... | collective-permute-start | bytes 442376 | tf_op jit(solution)/shard_map/ppermute | solution.py:686
  8.7 15.7 %collective-permute-start.11 = (bf16[480,128]{1,0:T(8,128)(2,1)S(1)}, bf16[480,128]{1,0:T(8,128)(2,1)S(1)}, u32[]{:S(2)}, u32[]{:S(2)}) collective-permute-start(bf16[480,128]{1,0:T(8,128)(2,1)S(1)} %get-tuple-element.36), channel_id=1, source_target_pairs={{0,1},{1,0},{2,3},{3,2},{4,5},{5,4},{6,7},{7,6},{8,9},{9,8},{10,11... | collective-permute-start | bytes 368648 | tf_op jit(solution)/shard_map/ppermute | solution.py:686
  10.2 14.2 %collective-permute-start.12 = (bf16[480,128]{1,0:T(8,128)(2,1)S(1)}, bf16[480,128]{1,0:T(8,128)(2,1)S(1)}, u32[]{:S(2)}, u32[]{:S(2)}) collective-permute-start(bf16[480,128]{1,0:T(8,128)(2,1)S(1)} %get-tuple-element.37), channel_id=1, source_target_pairs={{0,7},{1,6},{2,5},{3,4},{4,3},{5,2},{6,1},{7,0},{8,15},{9,14},{10,... | collective-permute-start | bytes 368648 | tf_op jit(solution)/shard_map/ppermute | solution.py:686
  11.5 9.6 %collective-permute-start.1 = (bf16[576,128]{1,0:T(8,128)(2,1)S(1)}, bf16[576,128]{1,0:T(8,128)(2,1)S(1)}, u32[]{:S(2)}, u32[]{:S(2)}) collective-permute-start(bf16[576,128]{1,0:T(8,128)(2,1)S(1)} %get-tuple-element.26), channel_id=1, source_target_pairs={{0,3},{1,2},{2,1},{3,0},{4,7},{5,6},{6,5},{7,4},{8,11},{9,10},{10,... | collective-permute-start | bytes 442376 | tf_op jit(solution)/shard_map/ppermute | solution.py:686
  18.6 3.8 %collective-permute-start.3 = (bf16[96,128]{1,0:T(8,128)(2,1)S(1)}, bf16[96,128]{1,0:T(8,128)(2,1)S(1)}, u32[]{:S(2)}, u32[]{:S(2)}) collective-permute-start(bf16[96,128]{1,0:T(8,128)(2,1)S(1)} %collect.2), channel_id=1, source_target_pairs={{0,2},{2,0},{4,6},{6,4},{1,3},{3,1},{5,7},{7,5},{8,10},{10,8},{12,... | collective-permute-start | bytes 73736 | tf_op jit(solution)/shard_map/ppermute | solution.py:676
  22.4 11.2 %collective-permute-start.4 = (bf16[400,128]{1,0:T(8,128)(2,1)S(1)}, bf16[400,128]{1,0:T(8,128)(2,1)S(1)}, u32[]{:S(2)}, u32[]{:S(2)}) collective-permute-start(bf16[400,128]{1,0:T(8,128)(2,1)S(1)} %collect_line.1.refs_0_), channel_id=1, source_target_pairs={{0,1},{1,0},{2,3},{3,2},{4,5},{5,4},{6,7},{7,6},{8,9},{9,8},{10,11... | collective-permute-start | bytes 307208 | tf_op jit(solution)/shard_map/ppermute | solution.py:679
  24.2 18.4 %collective-permute-start.5 = (bf16[480,128]{1,0:T(8,128)(2,1)S(1)}, bf16[480,128]{1,0:T(8,128)(2,1)S(1)}, u32[]{:S(2)}, u32[]{:S(2)}) collective-permute-start(bf16[480,128]{1,0:T(8,128)(2,1)S(1)} %get-tuple-element.29), channel_id=1, source_target_pairs={{0,2},{2,0},{4,6},{6,4},{1,3},{3,1},{5,7},{7,5},{8,10},{10,8},{12,... | collective-permute-start | bytes 368648 | tf_op jit(solution)/shard_map/ppermute | solution.py:676
  25.8 5.0 %collective-permute-start.13 = (bf16[160,128]{1,0:T(8,128)(2,1)S(1)}, bf16[160,128]{1,0:T(8,128)(2,1)S(1)}, u32[]{:S(2)}, u32[]{:S(2)}) collective-permute-start(bf16[160,128]{1,0:T(8,128)(2,1)S(1)} %get-tuple-element.39), channel_id=1, source_target_pairs={{0,2},{2,0},{4,6},{6,4},{1,3},{3,1},{5,7},{7,5},{8,10},{10,8},{12,... | collective-permute-start | bytes 122888 | tf_op jit(solution)/shard_map/ppermute | solution.py:676
  27.8 9.4 %collective-permute-start.14 = (bf16[160,128]{1,0:T(8,128)(2,1)S(1)}, bf16[160,128]{1,0:T(8,128)(2,1)S(1)}, u32[]{:S(2)}, u32[]{:S(2)}) collective-permute-start(bf16[160,128]{1,0:T(8,128)(2,1)S(1)} %get-tuple-element.40), channel_id=1, source_target_pairs={{0,4},{2,6},{4,0},{6,2},{1,5},{3,7},{5,1},{7,3},{8,12},{10,14},{12... | collective-permute-start | bytes 122888 | tf_op jit(solution)/shard_map/ppermute | solution.py:676
  29.4 10.4 %collective-permute-start.15 = (bf16[160,128]{1,0:T(8,128)(2,1)S(1)}, bf16[160,128]{1,0:T(8,128)(2,1)S(1)}, u32[]{:S(2)}, u32[]{:S(2)}) collective-permute-start(bf16[160,128]{1,0:T(8,128)(2,1)S(1)} %get-tuple-element.41), channel_id=1, source_target_pairs={{0,6},{2,4},{4,2},{6,0},{1,7},{3,5},{5,3},{7,1},{8,14},{10,12},{12... | collective-permute-start | bytes 122888 | tf_op jit(solution)/shard_map/ppermute | solution.py:676
  30.7 12.5 %collective-permute-start.6 = (bf16[480,128]{1,0:T(8,128)(2,1)S(1)}, bf16[480,128]{1,0:T(8,128)(2,1)S(1)}, u32[]{:S(2)}, u32[]{:S(2)}) collective-permute-start(bf16[480,128]{1,0:T(8,128)(2,1)S(1)} %get-tuple-element.30), channel_id=1, source_target_pairs={{0,4},{2,6},{4,0},{6,2},{1,5},{3,7},{5,1},{7,3},{8,12},{10,14},{12... | collective-permute-start | bytes 368648 | tf_op jit(solution)/shard_map/ppermute | solution.py:676
  33.6 9.7 %collective-permute-start.7 = (bf16[480,128]{1,0:T(8,128)(2,1)S(1)}, bf16[480,128]{1,0:T(8,128)(2,1)S(1)}, u32[]{:S(2)}, u32[]{:S(2)}) collective-permute-start(bf16[480,128]{1,0:T(8,128)(2,1)S(1)} %get-tuple-element.31), channel_id=1, source_target_pairs={{0,6},{2,4},{4,2},{6,0},{1,7},{3,5},{5,3},{7,1},{8,14},{10,12},{12... | collective-permute-start | bytes 368648 | tf_op jit(solution)/shard_map/ppermute | solution.py:676
  37.1 17.9 %collective-permute-start.18 = (bf16[768,128]{1,0:T(8,128)(2,1)S(1)}, bf16[768,128]{1,0:T(8,128)(2,1)S(1)}, u32[]{:S(2)}, u32[]{:S(2)}) collective-permute-start(bf16[768,128]{1,0:T(8,128)(2,1)S(1)} %collect.3.refs_0_), channel_id=1, source_target_pairs={{0,16},{16,0},{1,17},{17,1},{2,18},{18,2},{3,19},{19,3},{4,20},{20... | collective-permute-start | bytes 589832 | tf_op jit(solution)/shard_map/ppermute | solution.py:679
  40.4 14.8 %collective-permute-start.16 = (bf16[64,1280]{1,0:T(8,128)(2,1)S(1)}, bf16[64,1280]{1,0:T(8,128)(2,1)S(1)}, u32[]{:S(2)}, u32[]{:S(2)}) collective-permute-start(bf16[64,1280]{1,0:T(8,128)(2,1)S(1)} %project_packed.6), channel_id=1, source_target_pairs={{0,1},{1,0},{2,3},{3,2},{4,5},{5,4},{6,7},{7,6},{8,9},{9,8},{10,11... | collective-permute-start | bytes 491528 | tf_op jit(solution)/shard_map/ppermute | solution.py:679
  42.7 12.6 %collective-permute-start.17 = (bf16[64,1280]{1,0:T(8,128)(2,1)S(1)}, bf16[64,1280]{1,0:T(8,128)(2,1)S(1)}, u32[]{:S(2)}, u32[]{:S(2)}) collective-permute-start(bf16[64,1280]{1,0:T(8,128)(2,1)S(1)} %project_packed.7), channel_id=1, source_target_pairs={{0,1},{1,0},{2,3},{3,2},{4,5},{5,4},{6,7},{7,6},{8,9},{9,8},{10,11... | collective-permute-start | bytes 491528 | tf_op jit(solution)/shard_map/ppermute | solution.py:679
  44.6 5.6 %collective-permute-start.9 = (bf16[192,128]{1,0:T(8,128)(2,1)S(1)}, bf16[192,128]{1,0:T(8,128)(2,1)S(1)}, u32[]{:S(2)}, u32[]{:S(2)}) collective-permute-start(bf16[192,128]{1,0:T(8,128)(2,1)S(1)} %get-tuple-element.34), channel_id=1, source_target_pairs={{0,4},{2,6},{4,0},{6,2},{1,5},{3,7},{5,1},{7,3},{8,12},{10,14},{12... | collective-permute-start | bytes 147464 | tf_op jit(solution)/shard_map/ppermute | solution.py:676
  47.5 6.1 %collective-permute-start.10 = (bf16[192,128]{1,0:T(8,128)(2,1)S(1)}, bf16[192,128]{1,0:T(8,128)(2,1)S(1)}, u32[]{:S(2)}, u32[]{:S(2)}) collective-permute-start(bf16[192,128]{1,0:T(8,128)(2,1)S(1)} %get-tuple-element.35), channel_id=1, source_target_pairs={{0,6},{2,4},{4,2},{6,0},{1,7},{3,5},{5,3},{7,1},{8,14},{10,12},{12... | collective-permute-start | bytes 147464 | tf_op jit(solution)/shard_map/ppermute | solution.py:676
  50.2 4.4 %collective-permute-start.8 = (bf16[192,128]{1,0:T(8,128)(2,1)S(1)}, bf16[192,128]{1,0:T(8,128)(2,1)S(1)}, u32[]{:S(2)}, u32[]{:S(2)}) collective-permute-start(bf16[192,128]{1,0:T(8,128)(2,1)S(1)} %get-tuple-element.32), channel_id=1, source_target_pairs={{0,2},{2,0},{4,6},{6,4},{1,3},{3,1},{5,7},{7,5},{8,10},{10,8},{12,... | collective-permute-start | bytes 147464 | tf_op jit(solution)/shard_map/ppermute | solution.py:676
  53.6 1.6 %copy-start.1 = (bf16[1,1,64,2560]{3,2,1,0:T(8,128)(2,1)S(1)}, bf16[1,1,64,2560]{3,2,1,0:T(8,128)(2,1)}, u32[]{:S(2)}) copy-start(bf16[1,1,64,2560]{3,2,1,0:T(8,128)(2,1)} %param.8) | copy-start | bytes 983044
  53.6 1.7 %copy-start.2 = (f32[1,1,32,128]{3,2,1,0:T(8,128)S(1)}, f32[1,1,32,128]{3,2,1,0:T(8,128)}, u32[]{:S(2)}) copy-start(f32[1,1,32,128]{3,2,1,0:T(8,128)} %param.12) | copy-start | bytes 49156
  56.5 1.2 %collective-permute-start.19 = (f32[32,128]{1,0:T(8,128)S(1)}, f32[32,128]{1,0:T(8,128)S(1)}, u32[]{:S(2)}, u32[]{:S(2)}) collective-permute-start(f32[32,128]{1,0:T(8,128)S(1)} %get-tuple-element.45), channel_id=1, source_target_pairs={{0,8},{8,0},{1,9},{9,1},{2,10},{10,2},{3,11},{11,3},{4,12},{12,4},... | collective-permute-start | bytes 49160 | tf_op jit(solution)/shard_map/ppermute | solution.py:27

commit v5 on v4

--- a/solution.py
+++ b/solution.py
@@ -251,7 +251,6 @@
         cost_estimate=pl.CostEstimate(
             flops=0, transcendentals=0, bytes_accessed=4 * rows * width
         ),
-        name="split_first",
     )(
         *scalars,
         pltpu.with_memory_space_constraint(x, pltpu.HBM),
@@ -302,7 +301,6 @@
         cost_estimate=pl.CostEstimate(
             flops=0, transcendentals=0, bytes_accessed=4 * rows * columns // halves
         ),
-        name="split_far",
     )(
         *scalars[:2],
         pltpu.with_memory_space_constraint(steps, pltpu.HBM),
@@ -340,7 +338,6 @@
         cost_estimate=pl.CostEstimate(
             flops=0, transcendentals=0, bytes_accessed=4 * rows * columns // halves
         ),
-        name="split_near",
     )(*scalars[:2], pltpu.with_memory_space_constraint(x, pltpu.HBM))
 
 
@@ -375,7 +372,6 @@
         cost_estimate=pl.CostEstimate(
             flops=0, transcendentals=0, bytes_accessed=2 * weight.size * 2
         ),
-        name="load_rows",
     )(place, pltpu.with_memory_space_constraint(weight, pltpu.HBM))
 
 
@@ -445,7 +441,6 @@
             transcendentals=heads * total * total,
             bytes_accessed=8 * total * heads * HEAD,
         ),
-        name="attend_packed",
     )(*riders, *pieces)
 
 
@@ -490,7 +485,6 @@
             transcendentals=0,
             bytes_accessed=2 * depth * len(slots) * dim,
         ),
-        name="project_packed",
     )(held, *inputs)
 
 
@@ -559,7 +553,6 @@
         cost_estimate=pl.CostEstimate(
             flops=2 * rows * patch * dim, transcendentals=0, bytes_accessed=8 * rows * dim
         ),
-        name="finish",
     )(*inputs)
 
 
@@ -579,7 +572,6 @@
         cost_estimate=pl.CostEstimate(
             flops=0, transcendentals=0, bytes_accessed=4 * len(starts) * span * LANES
         ),
-        name="collect",
     )(*pieces)
 
 
@@ -600,7 +592,6 @@
         cost_estimate=pl.CostEstimate(
             flops=0, transcendentals=0, bytes_accessed=4 * len(starts) * span * LANES
         ),
-        name="collect_line",
     )(*pieces, modulation)
 
 
@@ -659,7 +650,6 @@
         cost_estimate=pl.CostEstimate(
             flops=0, transcendentals=0, bytes_accessed=8 * count * patch * width
         ),
-        name="arrange",
     )(*scalars, mine, up, modulation, other, *near)
 
 

time: 58.5 us -> 58.5 us (level)
  no operation moved by 1% of the time
where the time goes in v5:
time: 58.5 us; the launch traced here: 58.3 us
  starting transfers between devices  29.7 us (51%)
  Pallas kernels  13.5 us (23%)
  waiting for transfers between devices  12.6 us (22%)
  between operations  0.86 us (1%)
  other arithmetic  0.82 us (1%)
  local copies, waits for them, and re-layouts  0.62 us (1%)
    ppermute x10, starting transfers between devices, along(): return lax.ppermute(block, 'seq', [(i, i ^ r) for i in range(count)])  15.4 us
    ppermute x5, starting transfers between devices, swap(): return lax.ppermute(block, axis, [(0, 1), (1, 0)])  8.29 us
    ppermute x4, waiting for transfers between devices, slanted(): return lax.ppermute(block, ('seq', 'fsdp'), route)  8 us
    ppermute x4, starting transfers between devices, slanted(): return lax.ppermute(block, ('seq', 'fsdp'), route)  5.98 us
    ppermute x10, waiting for transfers between devices, along(): return lax.ppermute(block, 'seq', [(i, i ^ r) for i in range(count)])  3.39 us
    pallas_call x1, Pallas kernels, load_rows(): pl.pallas_call(functools.partial(load_kernel, count), in_specs=[pl.BlockS...  2.95 us
    pallas_call x4, Pallas kernels, project_packed(): pl.pallas_call(functools.partial(project_kernel, rows, first, slots), in_...  2.74 us
    pallas_call x2, Pallas kernels, attend_packed(): pl.pallas_call(functools.partial(attend_kernel, heads, rows, count), in_s...  2.67 us
  transfers between devices with their start and end apart: 20, of which 6 were waited for; matrix products, arithmetic and copies ran while one was open for 2% of the time, Pallas kernels for 21%

profile of v5, /device:TPU:0, one launch (start us, length us, event | category | flops | bytes accessed | tf_op | source)
XLA Modules:
  0.0 58.3 jit_solution(3076716863093036940)
XLA Ops:
  0.6 3.0 %collective-permute-start = (s32[1,1,2]{2,1,0:T(1,128)}, s32[1,1,2]{2,1,0:T(1,128)S(1)}, u32[]{:S(2)}, u32[]{:S(2)}) collective-permute-start(s32[1,1,2]{2,1,0:T(1,128)} %param.13), channel_id=1, source_target_pairs={{0,1},{1,0},{2,3},{3,2},{4,5},{5,4},{6,7},{7,6},{8,9},{9,8},{10,11... | collective-permute-start | bytes 32 | tf_op jit(solution)/shard_map/ppermute | solution.py:669
  3.7 1.0 %shard_map.87 = (bf16[576,128]{1,0:T(8,128)(2,1)S(1)}, bf16[96,128]{1,0:T(8,128)(2,1)S(1)}) custom-call(s32[1]{0:T(128)} %bitcast.place_ref, s32[1]{0:T(128)} %bitcast.2.half_ref, s32[1]{0:T(128)} %bitcast.5.group_ref, bf16[64,7680]{1,0:T(8,128)(2,1)} %bitcast.20, bf16[64,320]{1,0:T(8,128)(2,1)} %bitcast.24), custom_call_target="tpu_custom_call" | custom-call | bytes 245760 | tf_op jit(solution)/shard_map/pallas_call | solution.py:236
  4.7 2.6 %collective-permute-start.2 = (bf16[576,128]{1,0:T(8,128)(2,1)S(1)}, bf16[576,128]{1,0:T(8,128)(2,1)S(1)}, u32[]{:S(2)}, u32[]{:S(2)}) collective-permute-start(bf16[576,128]{1,0:T(8,128)(2,1)S(1)} %get-tuple-element.27), channel_id=1, source_target_pairs={{0,5},{1,4},{2,7},{3,6},{4,1},{5,0},{6,3},{7,2},{8,13},{9,12},{10,... | collective-permute-start | bytes 442376 | tf_op jit(solution)/shard_map/ppermute | solution.py:676
  7.3 1.3 %shard_map.88 = (bf16[480,128]{1,0:T(8,128)(2,1)S(1)}, bf16[576,128]{1,0:T(8,128)(2,1)S(1)}, bf16[480,128]{1,0:T(8,128)(2,1)S(1)}, f32[2,128]{1,0:T(2,128)S(1)}) custom-call(s32[1]{0:T(128)} %bitcast.place_ref, s32[1]{0:T(128)} %bitcast.2.half_ref, s32[1,2]{1,0:T(1,128)} %bitcast.26, bf16[64,7680]{1,0:T(8,128)(2,1)} %bitcast.21, ...), custom_call_target="tpu_custom_call" | custom-call | bytes 983040 | tf_op jit(solution)/shard_map/pallas_call | solution.py:284
  8.7 1.6 %collective-permute-start.11 = (bf16[480,128]{1,0:T(8,128)(2,1)S(1)}, bf16[480,128]{1,0:T(8,128)(2,1)S(1)}, u32[]{:S(2)}, u32[]{:S(2)}) collective-permute-start(bf16[480,128]{1,0:T(8,128)(2,1)S(1)} %get-tuple-element.36), channel_id=1, source_target_pairs={{0,1},{1,0},{2,3},{3,2},{4,5},{5,4},{6,7},{7,6},{8,9},{9,8},{10,11... | collective-permute-start | bytes 368648 | tf_op jit(solution)/shard_map/ppermute | solution.py:676
  10.2 1.3 %collective-permute-start.12 = (bf16[480,128]{1,0:T(8,128)(2,1)S(1)}, bf16[480,128]{1,0:T(8,128)(2,1)S(1)}, u32[]{:S(2)}, u32[]{:S(2)}) collective-permute-start(bf16[480,128]{1,0:T(8,128)(2,1)S(1)} %get-tuple-element.37), channel_id=1, source_target_pairs={{0,7},{1,6},{2,5},{3,4},{4,3},{5,2},{6,1},{7,0},{8,15},{9,14},{10,... | collective-permute-start | bytes 368648 | tf_op jit(solution)/shard_map/ppermute | solution.py:676
  12.1 0.8 %cosine_convert_fusion = (bf16[2,128]{1,0:T(2,128)(2,1)S(1)}, f32[2,128]{1,0:T(2,128)S(1)}) fusion(f32[128]{0:T(128)S(1)} %multiply_exponential_fusion, f32[2,128]{1,0:T(2,128)S(1)} %get-tuple-element.25.refs_6_, f32[]{:T(128)} %bitcast.8, pred[2]{0:T(512)(128)(4,1)} %constant.16.clone.1), kind=kLoop, calls=%fused_computation.6 | loop fusion | flops 768 | bytes 3078 | tf_op jit(solution)/shard_map/convert | solution.py:801
  12.9 5.7 %collective-permute-done.2.refs_0_.refs_2_ = bf16[576,128]{1,0:T(8,128)(2,1)S(1)} collective-permute-done((bf16[576,128]{1,0:T(8,128)(2,1)S(1)}, bf16[576,128]{1,0:T(8,128)(2,1)S(1)}, u32[]{:S(2)}, u32[]{:S(2)}) %collective-permute-start.2) | collective-permute-done | bytes 147488 | tf_op jit(solution)/shard_map/ppermute | solution.py:676
  18.8 2.3 %collective-permute-done.1.refs_1_ = bf16[576,128]{1,0:T(8,128)(2,1)S(1)} collective-permute-done((bf16[576,128]{1,0:T(8,128)(2,1)S(1)}, bf16[576,128]{1,0:T(8,128)(2,1)S(1)}, u32[]{:S(2)}, u32[]{:S(2)}) %collective-permute-start.1) | collective-permute-done | bytes 147488 | tf_op jit(solution)/shard_map/ppermute | solution.py:676
  21.1 1.3 %collective-permute-done.3.refs_3_ = bf16[96,128]{1,0:T(8,128)(2,1)S(1)} collective-permute-done((bf16[96,128]{1,0:T(8,128)(2,1)S(1)}, bf16[96,128]{1,0:T(8,128)(2,1)S(1)}, u32[]{:S(2)}, u32[]{:S(2)}) %collective-permute-start.3) | collective-permute-done | bytes 24608 | tf_op jit(solution)/shard_map/ppermute | solution.py:666
  22.9 1.4 %shard_map.91 = (bf16[480,128]{1,0:T(8,128)(2,1)S(1)}, bf16[480,128]{1,0:T(8,128)(2,1)S(1)}, bf16[480,128]{1,0:T(8,128)(2,1)S(1)}, bf16[480,128]{1,0:T(8,128)(2,1)S(1)}) custom-call(s32[1]{0:T(128)} %bitcast.place_ref, s32[1]{0:T(128)} %bitcast.2.half_ref, bf16[64,7680]{1,0:T(8,128)(2,1)} %bitcast.22), custom_call_target="tpu_custom_call" | custom-call | bytes 983040 | tf_op jit(solution)/shard_map/pallas_call | solution.py:328
  24.4 1.3 %shard_map.95 = (bf16[160,128]{1,0:T(8,128)(2,1)S(1)}, bf16[160,128]{1,0:T(8,128)(2,1)S(1)}, bf16[160,128]{1,0:T(8,128)(2,1)S(1)}, bf16[160,128]{1,0:T(8,128)(2,1)S(1)}) custom-call(bf16[480,128]{1,0:T(8,128)(2,1)S(1)} %collective-permute-done.11.refs_0_, bf16[576,128]{1,0:T(8,128)(2,1)S(1)} %collective-permute-done.1.refs_1_, ...), custom_call_target="tpu_custom_call" | custom-call | flops 83886080 | bytes 655360 | tf_op jit(solution)/shard_map/pallas_call | solution.py:434
  25.8 2.0 %collective-permute-start.13 = (bf16[160,128]{1,0:T(8,128)(2,1)S(1)}, bf16[160,128]{1,0:T(8,128)(2,1)S(1)}, u32[]{:S(2)}, u32[]{:S(2)}) collective-permute-start(bf16[160,128]{1,0:T(8,128)(2,1)S(1)} %get-tuple-element.39), channel_id=1, source_target_pairs={{0,2},{2,0},{4,6},{6,4},{1,3},{3,1},{5,7},{7,5},{8,10},{10,8},{12,... | collective-permute-start | bytes 122888 | tf_op jit(solution)/shard_map/ppermute | solution.py:666
  27.8 1.6 %collective-permute-start.14 = (bf16[160,128]{1,0:T(8,128)(2,1)S(1)}, bf16[160,128]{1,0:T(8,128)(2,1)S(1)}, u32[]{:S(2)}, u32[]{:S(2)}) collective-permute-start(bf16[160,128]{1,0:T(8,128)(2,1)S(1)} %get-tuple-element.40), channel_id=1, source_target_pairs={{0,4},{2,6},{4,0},{6,2},{1,5},{3,7},{5,1},{7,3},{8,12},{10,14},{12... | collective-permute-start | bytes 122888 | tf_op jit(solution)/shard_map/ppermute | solution.py:666
  29.4 1.4 %collective-permute-start.15 = (bf16[160,128]{1,0:T(8,128)(2,1)S(1)}, bf16[160,128]{1,0:T(8,128)(2,1)S(1)}, u32[]{:S(2)}, u32[]{:S(2)}) collective-permute-start(bf16[160,128]{1,0:T(8,128)(2,1)S(1)} %get-tuple-element.41), channel_id=1, source_target_pairs={{0,6},{2,4},{4,2},{6,0},{1,7},{3,5},{5,3},{7,1},{8,14},{10,12},{12... | collective-permute-start | bytes 122888 | tf_op jit(solution)/shard_map/ppermute | solution.py:666
  30.7 2.8 %collective-permute-start.6 = (bf16[480,128]{1,0:T(8,128)(2,1)S(1)}, bf16[480,128]{1,0:T(8,128)(2,1)S(1)}, u32[]{:S(2)}, u32[]{:S(2)}) collective-permute-start(bf16[480,128]{1,0:T(8,128)(2,1)S(1)} %get-tuple-element.30), channel_id=1, source_target_pairs={{0,4},{2,6},{4,0},{6,2},{1,5},{3,7},{5,1},{7,3},{8,12},{10,14},{12... | collective-permute-start | bytes 368648 | tf_op jit(solution)/shard_map/ppermute | solution.py:666
  34.1 2.9 %shard_map.86.w_ref = bf16[1280,2560]{1,0:T(8,128)(2,1)S(1)} custom-call(s32[1]{0:T(128)} %bitcast.place_ref, bf16[1280,2560]{1,0:T(8,128)(2,1)} %bitcast.23), custom_call_target="tpu_custom_call" | custom-call | bytes 13107200 | tf_op jit(solution)/shard_map/pallas_call | solution.py:362
  37.1 2.7 %collective-permute-start.18 = (bf16[768,128]{1,0:T(8,128)(2,1)S(1)}, bf16[768,128]{1,0:T(8,128)(2,1)S(1)}, u32[]{:S(2)}, u32[]{:S(2)}) collective-permute-start(bf16[768,128]{1,0:T(8,128)(2,1)S(1)} %shard_map.98.refs_0_), channel_id=1, source_target_pairs={{0,16},{16,0},{1,17},{17,1},{2,18},{18,2},{3,19},{19,3},{4,20},{20... | collective-permute-start | bytes 589832 | tf_op jit(solution)/shard_map/ppermute | solution.py:669
  39.8 0.7 %shard_map.96 = bf16[64,1280]{1,0:T(8,128)(2,1)S(1)} custom-call(bf16[1280,2560]{1,0:T(8,128)(2,1)S(1)} %shard_map.86.w_ref, bf16[160,128]{1,0:T(8,128)(2,1)S(1)} %get-tuple-element.38.refs_0_, bf16[160,128]{1,0:T(8,128)(2,1)S(1)} %collective-permute-done.13.refs_1_, bf16[160,128]{1,0:T(8,128)(2,1)S(1)} %collective-permute-done.14.refs_2_, ...), custom_call_target="tpu_custom_call" | custom-call | flops 209715200 | bytes 3276800 | tf_op jit(solution)/shard_map/pallas_call | solution.py:477
  40.4 1.6 %collective-permute-start.16 = (bf16[64,1280]{1,0:T(8,128)(2,1)S(1)}, bf16[64,1280]{1,0:T(8,128)(2,1)S(1)}, u32[]{:S(2)}, u32[]{:S(2)}) collective-permute-start(bf16[64,1280]{1,0:T(8,128)(2,1)S(1)} %shard_map.96), channel_id=1, source_target_pairs={{0,1},{1,0},{2,3},{3,2},{4,5},{5,4},{6,7},{7,6},{8,9},{9,8},{10,11... | collective-permute-start | bytes 491528 | tf_op jit(solution)/shard_map/ppermute | solution.py:669
  42.0 0.7 %shard_map.97 = bf16[64,1280]{1,0:T(8,128)(2,1)S(1)} custom-call(bf16[1280,2560]{1,0:T(8,128)(2,1)S(1)} %shard_map.86.w_ref, bf16[160,128]{1,0:T(8,128)(2,1)S(1)} %get-tuple-element.38.refs_0_, bf16[160,128]{1,0:T(8,128)(2,1)S(1)} %collective-permute-done.13.refs_1_, bf16[160,128]{1,0:T(8,128)(2,1)S(1)} %collective-permute-done.14.refs_2_, ...), custom_call_target="tpu_custom_call" | custom-call | flops 209715200 | bytes 3276800 | tf_op jit(solution)/shard_map/pallas_call | solution.py:477
  42.7 0.6 %collective-permute-start.17 = (bf16[64,1280]{1,0:T(8,128)(2,1)S(1)}, bf16[64,1280]{1,0:T(8,128)(2,1)S(1)}, u32[]{:S(2)}, u32[]{:S(2)}) collective-permute-start(bf16[64,1280]{1,0:T(8,128)(2,1)S(1)} %shard_map.97), channel_id=1, source_target_pairs={{0,1},{1,0},{2,3},{3,2},{4,5},{5,4},{6,7},{7,6},{8,9},{9,8},{10,11... | collective-permute-start | bytes 491528 | tf_op jit(solution)/shard_map/ppermute | solution.py:669
  43.3 1.3 %shard_map.92 = (bf16[192,128]{1,0:T(8,128)(2,1)S(1)}, bf16[192,128]{1,0:T(8,128)(2,1)S(1)}, bf16[192,128]{1,0:T(8,128)(2,1)S(1)}, bf16[192,128]{1,0:T(8,128)(2,1)S(1)}) custom-call(f32[2,960]{1,0:T(2,128)S(1)} %fusion.refs_4_.refs_0_.refs_2_, bf16[400,128]{1,0:T(8,128)(2,1)S(1)} %collective-permute-done.4.refs_1_.refs_3_, ...), custom_call_target="tpu_custom_call" | custom-call | flops 83886080 | bytes 655360 | tf_op jit(solution)/shard_map/pallas_call | solution.py:434
  44.6 2.9 %collective-permute-start.9 = (bf16[192,128]{1,0:T(8,128)(2,1)S(1)}, bf16[192,128]{1,0:T(8,128)(2,1)S(1)}, u32[]{:S(2)}, u32[]{:S(2)}) collective-permute-start(bf16[192,128]{1,0:T(8,128)(2,1)S(1)} %get-tuple-element.34), channel_id=1, source_target_pairs={{0,4},{2,6},{4,0},{6,2},{1,5},{3,7},{5,1},{7,3},{8,12},{10,14},{12... | collective-permute-start | bytes 147464 | tf_op jit(solution)/shard_map/ppermute | solution.py:666
  47.5 1.8 %collective-permute-start.10 = (bf16[192,128]{1,0:T(8,128)(2,1)S(1)}, bf16[192,128]{1,0:T(8,128)(2,1)S(1)}, u32[]{:S(2)}, u32[]{:S(2)}) collective-permute-start(bf16[192,128]{1,0:T(8,128)(2,1)S(1)} %get-tuple-element.35), channel_id=1, source_target_pairs={{0,6},{2,4},{4,2},{6,0},{1,7},{3,5},{5,3},{7,1},{8,14},{10,12},{12... | collective-permute-start | bytes 147464 | tf_op jit(solution)/shard_map/ppermute | solution.py:666
  49.3 0.9 %collective-permute-done.9.refs_1_.refs_6_ = bf16[192,128]{1,0:T(8,128)(2,1)S(1)} collective-permute-done((bf16[192,128]{1,0:T(8,128)(2,1)S(1)}, bf16[192,128]{1,0:T(8,128)(2,1)S(1)}, u32[]{:S(2)}, u32[]{:S(2)}) %collective-permute-start.9) | collective-permute-done | bytes 49184 | tf_op jit(solution)/shard_map/ppermute | solution.py:666
  50.2 2.2 %collective-permute-start.8 = (bf16[192,128]{1,0:T(8,128)(2,1)S(1)}, bf16[192,128]{1,0:T(8,128)(2,1)S(1)}, u32[]{:S(2)}, u32[]{:S(2)}) collective-permute-start(bf16[192,128]{1,0:T(8,128)(2,1)S(1)} %get-tuple-element.32), channel_id=1, source_target_pairs={{0,2},{2,0},{4,6},{6,4},{1,3},{3,1},{5,7},{7,5},{8,10},{10,8},{12,... | collective-permute-start | bytes 147464 | tf_op jit(solution)/shard_map/ppermute | solution.py:666
  52.4 1.2 %collective-permute-done.10.refs_2_.refs_7_ = bf16[192,128]{1,0:T(8,128)(2,1)S(1)} collective-permute-done((bf16[192,128]{1,0:T(8,128)(2,1)S(1)}, bf16[192,128]{1,0:T(8,128)(2,1)S(1)}, u32[]{:S(2)}, u32[]{:S(2)}) %collective-permute-start.10) | collective-permute-done | bytes 49184 | tf_op jit(solution)/shard_map/ppermute | solution.py:666
  53.6 0.9 %shard_map.93.refs_1_ = f32[64,2560]{1,0:T(8,128)S(1)} custom-call(bf16[1280,2560]{1,0:T(8,128)(2,1)S(1)} %shard_map.86.w_ref, bf16[192,128]{1,0:T(8,128)(2,1)S(1)} %get-tuple-element.33.refs_0_.refs_4_, bf16[192,128]{1,0:T(8,128)(2,1)S(1)} %collective-permute-done.9.refs_1_.refs_6_, bf16[192,128]{1,0:T(8,128)(2,1)S(1)} %collective-permute-done.10.refs_2_.refs_7_), custom_call_target="tpu_custom_call" | custom-call | flops 314572800 | bytes 4915200 | tf_op jit(solution)/shard_map/pallas_call | solution.py:477
  55.3 1.2 %shard_map.100 = (f32[32,128]{1,0:T(8,128)}, f32[32,128]{1,0:T(8,128)S(1)}) custom-call(f32[64,2560]{1,0:T(8,128)S(1)} %shard_map.94.near_ref, bf16[64,1280]{1,0:T(8,128)(2,1)S(1)} %collective-permute-done.16.refs_0_, bf16[64,1280]{1,0:T(8,128)(2,1)S(1)} %collective-permute-done.17.refs_1_, f32[4,1,1920]{2,1,0:T(1,128)S(1)} %get-tuple-element.42.refs_2_, ...), custom_call_target="tpu_custom_call" | custom-call | flops 20971520 | bytes 1310720 | tf_op jit(solution)/shard_map/pallas_call | solution.py:544
  56.5 1.2 %collective-permute-done.19 = f32[32,128]{1,0:T(8,128)S(1)} collective-permute-done((f32[32,128]{1,0:T(8,128)S(1)}, f32[32,128]{1,0:T(8,128)S(1)}, u32[]{:S(2)}, u32[]{:S(2)}) %collective-permute-start.19) | collective-permute-done | bytes 16416 | tf_op jit(solution)/shard_map/ppermute | solution.py:27
  57.7 0.6 %copy.10 = f32[1,1,32,128]{3,2,1,0:T(8,128)} copy(f32[1,1,32,128]{3,2,1,0:T(8,128)S(1)} %bitcast.25) | data formatting | bytes 32768
  (34 shorter events, 2.7 us)
Async XLA Ops:
  0.6 17.9 %copy-start = (bf16[1,256,960]{1,2,0:T(8,128)(2,1)S(1)}, bf16[1,256,960]{1,2,0:T(8,128)(2,1)}, u32[]{:S(2)}) copy-start(bf16[1,256,960]{1,2,0:T(8,128)(2,1)} %param.10) | copy-start | bytes 1474564
  0.6 11.4 %collective-permute-start = (s32[1,1,2]{2,1,0:T(1,128)}, s32[1,1,2]{2,1,0:T(1,128)S(1)}, u32[]{:S(2)}, u32[]{:S(2)}) collective-permute-start(s32[1,1,2]{2,1,0:T(1,128)} %param.13), channel_id=1, source_target_pairs={{0,1},{1,0},{2,3},{3,2},{4,5},{5,4},{6,7},{7,6},{8,9},{9,8},{10,11... | collective-permute-start | bytes 32 | tf_op jit(solution)/shard_map/ppermute | solution.py:669
  4.7 13.9 %collective-permute-start.2 = (bf16[576,128]{1,0:T(8,128)(2,1)S(1)}, bf16[576,128]{1,0:T(8,128)(2,1)S(1)}, u32[]{:S(2)}, u32[]{:S(2)}) collective-permute-start(bf16[576,128]{1,0:T(8,128)(2,1)S(1)} %get-tuple-element.27), channel_id=1, source_target_pairs={{0,5},{1,4},{2,7},{3,6},{4,1},{5,0},{6,3},{7,2},{8,13},{9,12},{10,... | collective-permute-start | bytes 442376 | tf_op jit(solution)/shard_map/ppermute | solution.py:676
  8.7 15.7 %collective-permute-start.11 = (bf16[480,128]{1,0:T(8,128)(2,1)S(1)}, bf16[480,128]{1,0:T(8,128)(2,1)S(1)}, u32[]{:S(2)}, u32[]{:S(2)}) collective-permute-start(bf16[480,128]{1,0:T(8,128)(2,1)S(1)} %get-tuple-element.36), channel_id=1, source_target_pairs={{0,1},{1,0},{2,3},{3,2},{4,5},{5,4},{6,7},{7,6},{8,9},{9,8},{10,11... | collective-permute-start | bytes 368648 | tf_op jit(solution)/shard_map/ppermute | solution.py:676
  10.2 14.2 %collective-permute-start.12 = (bf16[480,128]{1,0:T(8,128)(2,1)S(1)}, bf16[480,128]{1,0:T(8,128)(2,1)S(1)}, u32[]{:S(2)}, u32[]{:S(2)}) collective-permute-start(bf16[480,128]{1,0:T(8,128)(2,1)S(1)} %get-tuple-element.37), channel_id=1, source_target_pairs={{0,7},{1,6},{2,5},{3,4},{4,3},{5,2},{6,1},{7,0},{8,15},{9,14},{10,... | collective-permute-start | bytes 368648 | tf_op jit(solution)/shard_map/ppermute | solution.py:676
  11.5 9.6 %collective-permute-start.1 = (bf16[576,128]{1,0:T(8,128)(2,1)S(1)}, bf16[576,128]{1,0:T(8,128)(2,1)S(1)}, u32[]{:S(2)}, u32[]{:S(2)}) collective-permute-start(bf16[576,128]{1,0:T(8,128)(2,1)S(1)} %get-tuple-element.26), channel_id=1, source_target_pairs={{0,3},{1,2},{2,1},{3,0},{4,7},{5,6},{6,5},{7,4},{8,11},{9,10},{10,... | collective-permute-start | bytes 442376 | tf_op jit(solution)/shard_map/ppermute | solution.py:676
  18.6 3.8 %collective-permute-start.3 = (bf16[96,128]{1,0:T(8,128)(2,1)S(1)}, bf16[96,128]{1,0:T(8,128)(2,1)S(1)}, u32[]{:S(2)}, u32[]{:S(2)}) collective-permute-start(bf16[96,128]{1,0:T(8,128)(2,1)S(1)} %shard_map.89), channel_id=1, source_target_pairs={{0,2},{2,0},{4,6},{6,4},{1,3},{3,1},{5,7},{7,5},{8,10},{10,8},{12,... | collective-permute-start | bytes 73736 | tf_op jit(solution)/shard_map/ppermute | solution.py:666
  22.4 11.2 %collective-permute-start.4 = (bf16[400,128]{1,0:T(8,128)(2,1)S(1)}, bf16[400,128]{1,0:T(8,128)(2,1)S(1)}, u32[]{:S(2)}, u32[]{:S(2)}) collective-permute-start(bf16[400,128]{1,0:T(8,128)(2,1)S(1)} %shard_map.90.refs_0_), channel_id=1, source_target_pairs={{0,1},{1,0},{2,3},{3,2},{4,5},{5,4},{6,7},{7,6},{8,9},{9,8},{10,11... | collective-permute-start | bytes 307208 | tf_op jit(solution)/shard_map/ppermute | solution.py:669
  24.2 18.4 %collective-permute-start.5 = (bf16[480,128]{1,0:T(8,128)(2,1)S(1)}, bf16[480,128]{1,0:T(8,128)(2,1)S(1)}, u32[]{:S(2)}, u32[]{:S(2)}) collective-permute-start(bf16[480,128]{1,0:T(8,128)(2,1)S(1)} %get-tuple-element.29), channel_id=1, source_target_pairs={{0,2},{2,0},{4,6},{6,4},{1,3},{3,1},{5,7},{7,5},{8,10},{10,8},{12,... | collective-permute-start | bytes 368648 | tf_op jit(solution)/shard_map/ppermute | solution.py:666
  25.8 5.0 %collective-permute-start.13 = (bf16[160,128]{1,0:T(8,128)(2,1)S(1)}, bf16[160,128]{1,0:T(8,128)(2,1)S(1)}, u32[]{:S(2)}, u32[]{:S(2)}) collective-permute-start(bf16[160,128]{1,0:T(8,128)(2,1)S(1)} %get-tuple-element.39), channel_id=1, source_target_pairs={{0,2},{2,0},{4,6},{6,4},{1,3},{3,1},{5,7},{7,5},{8,10},{10,8},{12,... | collective-permute-start | bytes 122888 | tf_op jit(solution)/shard_map/ppermute | solution.py:666
  27.8 9.4 %collective-permute-start.14 = (bf16[160,128]{1,0:T(8,128)(2,1)S(1)}, bf16[160,128]{1,0:T(8,128)(2,1)S(1)}, u32[]{:S(2)}, u32[]{:S(2)}) collective-permute-start(bf16[160,128]{1,0:T(8,128)(2,1)S(1)} %get-tuple-element.40), channel_id=1, source_target_pairs={{0,4},{2,6},{4,0},{6,2},{1,5},{3,7},{5,1},{7,3},{8,12},{10,14},{12... | collective-permute-start | bytes 122888 | tf_op jit(solution)/shard_map/ppermute | solution.py:666
  29.4 10.4 %collective-permute-start.15 = (bf16[160,128]{1,0:T(8,128)(2,1)S(1)}, bf16[160,128]{1,0:T(8,128)(2,1)S(1)}, u32[]{:S(2)}, u32[]{:S(2)}) collective-permute-start(bf16[160,128]{1,0:T(8,128)(2,1)S(1)} %get-tuple-element.41), channel_id=1, source_target_pairs={{0,6},{2,4},{4,2},{6,0},{1,7},{3,5},{5,3},{7,1},{8,14},{10,12},{12... | collective-permute-start | bytes 122888 | tf_op jit(solution)/shard_map/ppermute | solution.py:666
  30.7 12.5 %collective-permute-start.6 = (bf16[480,128]{1,0:T(8,128)(2,1)S(1)}, bf16[480,128]{1,0:T(8,128)(2,1)S(1)}, u32[]{:S(2)}, u32[]{:S(2)}) collective-permute-start(bf16[480,128]{1,0:T(8,128)(2,1)S(1)} %get-tuple-element.30), channel_id=1, source_target_pairs={{0,4},{2,6},{4,0},{6,2},{1,5},{3,7},{5,1},{7,3},{8,12},{10,14},{12... | collective-permute-start | bytes 368648 | tf_op jit(solution)/shard_map/ppermute | solution.py:666
  33.6 9.7 %collective-permute-start.7 = (bf16[480,128]{1,0:T(8,128)(2,1)S(1)}, bf16[480,128]{1,0:T(8,128)(2,1)S(1)}, u32[]{:S(2)}, u32[]{:S(2)}) collective-permute-start(bf16[480,128]{1,0:T(8,128)(2,1)S(1)} %get-tuple-element.31), channel_id=1, source_target_pairs={{0,6},{2,4},{4,2},{6,0},{1,7},{3,5},{5,3},{7,1},{8,14},{10,12},{12... | collective-permute-start | bytes 368648 | tf_op jit(solution)/shard_map/ppermute | solution.py:666
  37.1 17.9 %collective-permute-start.18 = (bf16[768,128]{1,0:T(8,128)(2,1)S(1)}, bf16[768,128]{1,0:T(8,128)(2,1)S(1)}, u32[]{:S(2)}, u32[]{:S(2)}) collective-permute-start(bf16[768,128]{1,0:T(8,128)(2,1)S(1)} %shard_map.98.refs_0_), channel_id=1, source_target_pairs={{0,16},{16,0},{1,17},{17,1},{2,18},{18,2},{3,19},{19,3},{4,20},{20... | collective-permute-start | bytes 589832 | tf_op jit(solution)/shard_map/ppermute | solution.py:669
  40.4 14.8 %collective-permute-start.16 = (bf16[64,1280]{1,0:T(8,128)(2,1)S(1)}, bf16[64,1280]{1,0:T(8,128)(2,1)S(1)}, u32[]{:S(2)}, u32[]{:S(2)}) collective-permute-start(bf16[64,1280]{1,0:T(8,128)(2,1)S(1)} %shard_map.96), channel_id=1, source_target_pairs={{0,1},{1,0},{2,3},{3,2},{4,5},{5,4},{6,7},{7,6},{8,9},{9,8},{10,11... | collective-permute-start | bytes 491528 | tf_op jit(solution)/shard_map/ppermute | solution.py:669
  42.7 12.6 %collective-permute-start.17 = (bf16[64,1280]{1,0:T(8,128)(2,1)S(1)}, bf16[64,1280]{1,0:T(8,128)(2,1)S(1)}, u32[]{:S(2)}, u32[]{:S(2)}) collective-permute-start(bf16[64,1280]{1,0:T(8,128)(2,1)S(1)} %shard_map.97), channel_id=1, source_target_pairs={{0,1},{1,0},{2,3},{3,2},{4,5},{5,4},{6,7},{7,6},{8,9},{9,8},{10,11... | collective-permute-start | bytes 491528 | tf_op jit(solution)/shard_map/ppermute | solution.py:669
  44.6 5.6 %collective-permute-start.9 = (bf16[192,128]{1,0:T(8,128)(2,1)S(1)}, bf16[192,128]{1,0:T(8,128)(2,1)S(1)}, u32[]{:S(2)}, u32[]{:S(2)}) collective-permute-start(bf16[192,128]{1,0:T(8,128)(2,1)S(1)} %get-tuple-element.34), channel_id=1, source_target_pairs={{0,4},{2,6},{4,0},{6,2},{1,5},{3,7},{5,1},{7,3},{8,12},{10,14},{12... | collective-permute-start | bytes 147464 | tf_op jit(solution)/shard_map/ppermute | solution.py:666
  47.5 6.1 %collective-permute-start.10 = (bf16[192,128]{1,0:T(8,128)(2,1)S(1)}, bf16[192,128]{1,0:T(8,128)(2,1)S(1)}, u32[]{:S(2)}, u32[]{:S(2)}) collective-permute-start(bf16[192,128]{1,0:T(8,128)(2,1)S(1)} %get-tuple-element.35), channel_id=1, source_target_pairs={{0,6},{2,4},{4,2},{6,0},{1,7},{3,5},{5,3},{7,1},{8,14},{10,12},{12... | collective-permute-start | bytes 147464 | tf_op jit(solution)/shard_map/ppermute | solution.py:666
  50.2 4.4 %collective-permute-start.8 = (bf16[192,128]{1,0:T(8,128)(2,1)S(1)}, bf16[192,128]{1,0:T(8,128)(2,1)S(1)}, u32[]{:S(2)}, u32[]{:S(2)}) collective-permute-start(bf16[192,128]{1,0:T(8,128)(2,1)S(1)} %get-tuple-element.32), channel_id=1, source_target_pairs={{0,2},{2,0},{4,6},{6,4},{1,3},{3,1},{5,7},{7,5},{8,10},{10,8},{12,... | collective-permute-start | bytes 147464 | tf_op jit(solution)/shard_map/ppermute | solution.py:666
  53.6 1.6 %copy-start.1 = (bf16[1,1,64,2560]{3,2,1,0:T(8,128)(2,1)S(1)}, bf16[1,1,64,2560]{3,2,1,0:T(8,128)(2,1)}, u32[]{:S(2)}) copy-start(bf16[1,1,64,2560]{3,2,1,0:T(8,128)(2,1)} %param.8) | copy-start | bytes 983044
  53.6 1.7 %copy-start.2 = (f32[1,1,32,128]{3,2,1,0:T(8,128)S(1)}, f32[1,1,32,128]{3,2,1,0:T(8,128)}, u32[]{:S(2)}) copy-start(f32[1,1,32,128]{3,2,1,0:T(8,128)} %param.12) | copy-start | bytes 49156
  56.5 1.2 %collective-permute-start.19 = (f32[32,128]{1,0:T(8,128)S(1)}, f32[32,128]{1,0:T(8,128)S(1)}, u32[]{:S(2)}, u32[]{:S(2)}) collective-permute-start(f32[32,128]{1,0:T(8,128)S(1)} %get-tuple-element.45), channel_id=1, source_target_pairs={{0,8},{8,0},{1,9},{9,1},{2,10},{10,2},{3,11},{11,3},{4,12},{12,4},... | collective-permute-start | bytes 49160 | tf_op jit(solution)/shard_map/ppermute | solution.py:27

commit v6 on v5

--- a/solution.py
+++ b/solution.py
@@ -503,7 +503,9 @@
     total = jnp.zeros((rows, 1), jnp.float32)
     for i in range(steps):
         cut = slice(i * tile, (i + 1) * tile)
-        side, offset = divmod(i * tile, dim // 2)
+        bound = far[0].shape[1]
+        side = int(i * tile >= bound)
+        offset = i * tile - side * bound
         projected = near_ref[:, cut] + far[side][:, offset : offset + tile].astype(jnp.float32)
         part = hidden_ref[:, cut].astype(jnp.float32) + modulation(0, i) * projected
         acc_ref[i] = part
@@ -537,7 +539,7 @@
 
 def finish(near, far, hidden, lines, head_rows, latent, clock):
     rows, dim = near.shape
-    tile = math.gcd(dim // 2, lines.shape[2])
+    tile = math.gcd(far[0].shape[1], far[1].shape[1], lines.shape[2])
     patch = head_rows.shape[0]
     inputs = (near, *far, lines, hidden, head_rows, latent, clock)
     result = jax.ShapeDtypeStruct((rows // 2, 2 * patch), jnp.float32)
@@ -705,11 +707,18 @@
     far_attended = attend_packed(far_pieces, heads, rows)
     far_home = [far_attended[0]]
     far_home += [along(far_attended[r], r) for r in range(1, count)]
-    part = DIM // 2
+    bounds = [0, DIM // 4, DIM]
     partial = []
     for k in range(2):
         term = project_packed(
-            far_home, range(count), count, weight, rows, k * part, part, jnp.bfloat16
+            far_home,
+            range(count),
+            count,
+            weight,
+            rows,
+            bounds[k],
+            bounds[k + 1] - bounds[k],
+            jnp.bfloat16,
         )
         partial.append(swap(term, "fsdp"))
 

time: 58.5 us -> 62 us (1.060)
  waiting for transfers between devices: 12.6 us -> 17.3 us
  starting transfers between devices: 29.7 us -> 28.3 us
    ppermute x10, waiting for transfers between devices: 3.39 us -> 7.66 us  [along(): return lax.ppermute(block, 'seq', [(i, i ^ r) for i in range(count)])]
    ppermute x10, starting transfers between devices: 15.4 us -> 14.7 us  [along(): return lax.ppermute(block, 'seq', [(i, i ^ r) for i in range(count)])]
    ppermute x5, starting transfers between devices: 8.29 us -> 7.63 us  [swap(): return lax.ppermute(block, axis, [(0, 1), (1, 0)])]
  transfers between devices with their start and end apart: 20 -> 20, of which waited for: 6 -> 6; matrix products, arithmetic and copies ran while one was open for 2% -> 2% of each run, Pallas kernels for 21% -> 20%
where the time goes in v6:
time: 62 us; the launch traced here: 61.8 us
  starting transfers between devices  28.3 us (46%)
  waiting for transfers between devices  17.3 us (28%)
  Pallas kernels  13.6 us (22%)
  between operations  0.86 us (1%)
  other arithmetic  0.82 us (1%)
  local copies, waits for them, and re-layouts  0.62 us (1%)
    ppermute x10, starting transfers between devices, along(): return lax.ppermute(block, 'seq', [(i, i ^ r) for i in range(count)])  14.7 us
    ppermute x4, waiting for transfers between devices, slanted(): return lax.ppermute(block, ('seq', 'fsdp'), route)  8.48 us
    ppermute x10, waiting for transfers between devices, along(): return lax.ppermute(block, 'seq', [(i, i ^ r) for i in range(count)])  7.66 us
    ppermute x5, starting transfers between devices, swap(): return lax.ppermute(block, axis, [(0, 1), (1, 0)])  7.63 us
    ppermute x4, starting transfers between devices, slanted(): return lax.ppermute(block, ('seq', 'fsdp'), route)  5.98 us
    pallas_call x1, Pallas kernels, load_rows(): pl.pallas_call(functools.partial(load_kernel, count), in_specs=[pl.BlockS...  2.95 us
    pallas_call x4, Pallas kernels, project_packed(): pl.pallas_call(functools.partial(project_kernel, rows, first, slots), in_...  2.78 us
    pallas_call x2, Pallas kernels, attend_packed(): pl.pallas_call(functools.partial(attend_kernel, heads, rows, count), in_s...  2.67 us
  transfers between devices with their start and end apart: 20, of which 6 were waited for; matrix products, arithmetic and copies ran while one was open for 2% of the time, Pallas kernels for 20%

profile of v6, /device:TPU:0, one launch (start us, length us, event | category | flops | bytes accessed | tf_op | source)
XLA Modules:
  0.0 61.8 jit_solution(3609972698876603269)
XLA Ops:
  0.6 3.0 %collective-permute-start = (s32[1,1,2]{2,1,0:T(1,128)}, s32[1,1,2]{2,1,0:T(1,128)S(1)}, u32[]{:S(2)}, u32[]{:S(2)}) collective-permute-start(s32[1,1,2]{2,1,0:T(1,128)} %param.13), channel_id=1, source_target_pairs={{0,1},{1,0},{2,3},{3,2},{4,5},{5,4},{6,7},{7,6},{8,9},{9,8},{10,11... | collective-permute-start | bytes 32 | tf_op jit(solution)/shard_map/ppermute | solution.py:671
  3.7 1.0 %shard_map.87 = (bf16[576,128]{1,0:T(8,128)(2,1)S(1)}, bf16[96,128]{1,0:T(8,128)(2,1)S(1)}) custom-call(s32[1]{0:T(128)} %bitcast.place_ref, s32[1]{0:T(128)} %bitcast.2.half_ref, s32[1]{0:T(128)} %bitcast.5.group_ref, bf16[64,7680]{1,0:T(8,128)(2,1)} %bitcast.20, bf16[64,320]{1,0:T(8,128)(2,1)} %bitcast.24), custom_call_target="tpu_custom_call" | custom-call | bytes 245760 | tf_op jit(solution)/shard_map/pallas_call | solution.py:236
  4.7 2.6 %collective-permute-start.2 = (bf16[576,128]{1,0:T(8,128)(2,1)S(1)}, bf16[576,128]{1,0:T(8,128)(2,1)S(1)}, u32[]{:S(2)}, u32[]{:S(2)}) collective-permute-start(bf16[576,128]{1,0:T(8,128)(2,1)S(1)} %get-tuple-element.27), channel_id=1, source_target_pairs={{0,5},{1,4},{2,7},{3,6},{4,1},{5,0},{6,3},{7,2},{8,13},{9,12},{10,... | collective-permute-start | bytes 442376 | tf_op jit(solution)/shard_map/ppermute | solution.py:678
  7.3 1.3 %shard_map.88 = (bf16[480,128]{1,0:T(8,128)(2,1)S(1)}, bf16[576,128]{1,0:T(8,128)(2,1)S(1)}, bf16[480,128]{1,0:T(8,128)(2,1)S(1)}, f32[2,128]{1,0:T(2,128)S(1)}) custom-call(s32[1]{0:T(128)} %bitcast.place_ref, s32[1]{0:T(128)} %bitcast.2.half_ref, s32[1,2]{1,0:T(1,128)} %bitcast.26, bf16[64,7680]{1,0:T(8,128)(2,1)} %bitcast.21, ...), custom_call_target="tpu_custom_call" | custom-call | bytes 983040 | tf_op jit(solution)/shard_map/pallas_call | solution.py:284
  8.7 1.6 %collective-permute-start.11 = (bf16[480,128]{1,0:T(8,128)(2,1)S(1)}, bf16[480,128]{1,0:T(8,128)(2,1)S(1)}, u32[]{:S(2)}, u32[]{:S(2)}) collective-permute-start(bf16[480,128]{1,0:T(8,128)(2,1)S(1)} %get-tuple-element.36), channel_id=1, source_target_pairs={{0,1},{1,0},{2,3},{3,2},{4,5},{5,4},{6,7},{7,6},{8,9},{9,8},{10,11... | collective-permute-start | bytes 368648 | tf_op jit(solution)/shard_map/ppermute | solution.py:678
  10.2 1.3 %collective-permute-start.12 = (bf16[480,128]{1,0:T(8,128)(2,1)S(1)}, bf16[480,128]{1,0:T(8,128)(2,1)S(1)}, u32[]{:S(2)}, u32[]{:S(2)}) collective-permute-start(bf16[480,128]{1,0:T(8,128)(2,1)S(1)} %get-tuple-element.37), channel_id=1, source_target_pairs={{0,7},{1,6},{2,5},{3,4},{4,3},{5,2},{6,1},{7,0},{8,15},{9,14},{10,... | collective-permute-start | bytes 368648 | tf_op jit(solution)/shard_map/ppermute | solution.py:678
  12.1 0.8 %cosine_convert_fusion = (bf16[2,128]{1,0:T(2,128)(2,1)S(1)}, f32[2,128]{1,0:T(2,128)S(1)}) fusion(f32[128]{0:T(128)S(1)} %multiply_exponential_fusion, f32[2,128]{1,0:T(2,128)S(1)} %get-tuple-element.25.refs_6_, f32[]{:T(128)} %bitcast.8, pred[2]{0:T(512)(128)(4,1)} %constant.16.clone.1), kind=kLoop, calls=%fused_computation.6 | loop fusion | flops 768 | bytes 3078 | tf_op jit(solution)/shard_map/convert | solution.py:810
  12.9 5.7 %collective-permute-done.2.refs_0_.refs_2_ = bf16[576,128]{1,0:T(8,128)(2,1)S(1)} collective-permute-done((bf16[576,128]{1,0:T(8,128)(2,1)S(1)}, bf16[576,128]{1,0:T(8,128)(2,1)S(1)}, u32[]{:S(2)}, u32[]{:S(2)}) %collective-permute-start.2) | collective-permute-done | bytes 147488 | tf_op jit(solution)/shard_map/ppermute | solution.py:678
  18.6 2.8 %collective-permute-done.11.refs_0_ = bf16[480,128]{1,0:T(8,128)(2,1)S(1)} collective-permute-done((bf16[480,128]{1,0:T(8,128)(2,1)S(1)}, bf16[480,128]{1,0:T(8,128)(2,1)S(1)}, u32[]{:S(2)}, u32[]{:S(2)}) %collective-permute-start.11) | collective-permute-done | bytes 122912 | tf_op jit(solution)/shard_map/ppermute | solution.py:678
  21.4 1.3 %shard_map.95 = (bf16[160,128]{1,0:T(8,128)(2,1)S(1)}, bf16[160,128]{1,0:T(8,128)(2,1)S(1)}, bf16[160,128]{1,0:T(8,128)(2,1)S(1)}, bf16[160,128]{1,0:T(8,128)(2,1)S(1)}) custom-call(bf16[480,128]{1,0:T(8,128)(2,1)S(1)} %collective-permute-done.11.refs_0_, bf16[576,128]{1,0:T(8,128)(2,1)S(1)} %collective-permute-done.1.refs_1_, ...), custom_call_target="tpu_custom_call" | custom-call | flops 83886080 | bytes 655360 | tf_op jit(solution)/shard_map/pallas_call | solution.py:434
  22.7 0.7 %collective-permute-start.13 = (bf16[160,128]{1,0:T(8,128)(2,1)S(1)}, bf16[160,128]{1,0:T(8,128)(2,1)S(1)}, u32[]{:S(2)}, u32[]{:S(2)}) collective-permute-start(bf16[160,128]{1,0:T(8,128)(2,1)S(1)} %get-tuple-element.39), channel_id=1, source_target_pairs={{0,2},{2,0},{4,6},{6,4},{1,3},{3,1},{5,7},{7,5},{8,10},{10,8},{12,... | collective-permute-start | bytes 122888 | tf_op jit(solution)/shard_map/ppermute | solution.py:668
  23.5 2.9 %collective-permute-start.14 = (bf16[160,128]{1,0:T(8,128)(2,1)S(1)}, bf16[160,128]{1,0:T(8,128)(2,1)S(1)}, u32[]{:S(2)}, u32[]{:S(2)}) collective-permute-start(bf16[160,128]{1,0:T(8,128)(2,1)S(1)} %get-tuple-element.40), channel_id=1, source_target_pairs={{0,4},{2,6},{4,0},{6,2},{1,5},{3,7},{5,1},{7,3},{8,12},{10,14},{12... | collective-permute-start | bytes 122888 | tf_op jit(solution)/shard_map/ppermute | solution.py:668
  26.4 0.8 %collective-permute-start.15 = (bf16[160,128]{1,0:T(8,128)(2,1)S(1)}, bf16[160,128]{1,0:T(8,128)(2,1)S(1)}, u32[]{:S(2)}, u32[]{:S(2)}) collective-permute-start(bf16[160,128]{1,0:T(8,128)(2,1)S(1)} %get-tuple-element.41), channel_id=1, source_target_pairs={{0,6},{2,4},{4,2},{6,0},{1,7},{3,5},{5,3},{7,1},{8,14},{10,12},{12... | collective-permute-start | bytes 122888 | tf_op jit(solution)/shard_map/ppermute | solution.py:668
  27.5 1.3 %collective-permute-start.4 = (bf16[400,128]{1,0:T(8,128)(2,1)S(1)}, bf16[400,128]{1,0:T(8,128)(2,1)S(1)}, u32[]{:S(2)}, u32[]{:S(2)}) collective-permute-start(bf16[400,128]{1,0:T(8,128)(2,1)S(1)} %shard_map.90.refs_0_), channel_id=1, source_target_pairs={{0,1},{1,0},{2,3},{3,2},{4,5},{5,4},{6,7},{7,6},{8,9},{9,8},{10,11... | collective-permute-start | bytes 307208 | tf_op jit(solution)/shard_map/ppermute | solution.py:671
  28.8 2.9 %shard_map.86.w_ref = bf16[1280,2560]{1,0:T(8,128)(2,1)S(1)} custom-call(s32[1]{0:T(128)} %bitcast.place_ref, bf16[1280,2560]{1,0:T(8,128)(2,1)} %bitcast.23), custom_call_target="tpu_custom_call" | custom-call | bytes 13107200 | tf_op jit(solution)/shard_map/pallas_call | solution.py:362
  32.2 0.9 %shard_map.97 = bf16[64,1920]{1,0:T(8,128)(2,1)S(1)} custom-call(bf16[1280,2560]{1,0:T(8,128)(2,1)S(1)} %shard_map.86.w_ref, bf16[160,128]{1,0:T(8,128)(2,1)S(1)} %get-tuple-element.38.refs_0_, bf16[160,128]{1,0:T(8,128)(2,1)S(1)} %collective-permute-done.13.refs_1_, bf16[160,128]{1,0:T(8,128)(2,1)S(1)} %collective-permute-done.14.refs_2_, ...), custom_call_target="tpu_custom_call" | custom-call | flops 314572800 | bytes 4915200 | tf_op jit(solution)/shard_map/pallas_call | solution.py:477
  33.1 1.0 %collective-permute-start.17 = (bf16[64,1920]{1,0:T(8,128)(2,1)S(1)}, bf16[64,1920]{1,0:T(8,128)(2,1)S(1)}, u32[]{:S(2)}, u32[]{:S(2)}) collective-permute-start(bf16[64,1920]{1,0:T(8,128)(2,1)S(1)} %shard_map.97), channel_id=1, source_target_pairs={{0,1},{1,0},{2,3},{3,2},{4,5},{5,4},{6,7},{7,6},{8,9},{9,8},{10,11... | collective-permute-start | bytes 737288 | tf_op jit(solution)/shard_map/ppermute | solution.py:671
  34.1 1.4 %shard_map.91 = (bf16[480,128]{1,0:T(8,128)(2,1)S(1)}, bf16[480,128]{1,0:T(8,128)(2,1)S(1)}, bf16[480,128]{1,0:T(8,128)(2,1)S(1)}, bf16[480,128]{1,0:T(8,128)(2,1)S(1)}) custom-call(s32[1]{0:T(128)} %bitcast.place_ref, s32[1]{0:T(128)} %bitcast.2.half_ref, bf16[64,7680]{1,0:T(8,128)(2,1)} %bitcast.22), custom_call_target="tpu_custom_call" | custom-call | bytes 983040 | tf_op jit(solution)/shard_map/pallas_call | solution.py:328
  35.6 3.0 %collective-permute-start.6 = (bf16[480,128]{1,0:T(8,128)(2,1)S(1)}, bf16[480,128]{1,0:T(8,128)(2,1)S(1)}, u32[]{:S(2)}, u32[]{:S(2)}) collective-permute-start(bf16[480,128]{1,0:T(8,128)(2,1)S(1)} %get-tuple-element.30), channel_id=1, source_target_pairs={{0,4},{2,6},{4,0},{6,2},{1,5},{3,7},{5,1},{7,3},{8,12},{10,14},{12... | collective-permute-start | bytes 368648 | tf_op jit(solution)/shard_map/ppermute | solution.py:668
  38.6 1.3 %collective-permute-start.7 = (bf16[480,128]{1,0:T(8,128)(2,1)S(1)}, bf16[480,128]{1,0:T(8,128)(2,1)S(1)}, u32[]{:S(2)}, u32[]{:S(2)}) collective-permute-start(bf16[480,128]{1,0:T(8,128)(2,1)S(1)} %get-tuple-element.31), channel_id=1, source_target_pairs={{0,6},{2,4},{4,2},{6,0},{1,7},{3,5},{5,3},{7,1},{8,14},{10,12},{12... | collective-permute-start | bytes 368648 | tf_op jit(solution)/shard_map/ppermute | solution.py:668
  40.0 1.6 %collective-permute-start.18 = (bf16[768,128]{1,0:T(8,128)(2,1)S(1)}, bf16[768,128]{1,0:T(8,128)(2,1)S(1)}, u32[]{:S(2)}, u32[]{:S(2)}) collective-permute-start(bf16[768,128]{1,0:T(8,128)(2,1)S(1)} %shard_map.98.refs_0_), channel_id=1, source_target_pairs={{0,16},{16,0},{1,17},{17,1},{2,18},{18,2},{3,19},{19,3},{4,20},{20... | collective-permute-start | bytes 589832 | tf_op jit(solution)/shard_map/ppermute | solution.py:671
  41.5 5.3 %collective-permute-done.6.refs_4_ = bf16[480,128]{1,0:T(8,128)(2,1)S(1)} collective-permute-done((bf16[480,128]{1,0:T(8,128)(2,1)S(1)}, bf16[480,128]{1,0:T(8,128)(2,1)S(1)}, u32[]{:S(2)}, u32[]{:S(2)}) %collective-permute-start.6) | collective-permute-done | bytes 122912 | tf_op jit(solution)/shard_map/ppermute | solution.py:668
  46.9 1.3 %shard_map.92 = (bf16[192,128]{1,0:T(8,128)(2,1)S(1)}, bf16[192,128]{1,0:T(8,128)(2,1)S(1)}, bf16[192,128]{1,0:T(8,128)(2,1)S(1)}, bf16[192,128]{1,0:T(8,128)(2,1)S(1)}) custom-call(f32[2,960]{1,0:T(2,128)S(1)} %fusion.refs_4_.refs_0_.refs_2_, bf16[400,128]{1,0:T(8,128)(2,1)S(1)} %collective-permute-done.4.refs_1_.refs_3_, ...), custom_call_target="tpu_custom_call" | custom-call | flops 83886080 | bytes 655360 | tf_op jit(solution)/shard_map/pallas_call | solution.py:434
  48.2 3.0 %collective-permute-start.9 = (bf16[192,128]{1,0:T(8,128)(2,1)S(1)}, bf16[192,128]{1,0:T(8,128)(2,1)S(1)}, u32[]{:S(2)}, u32[]{:S(2)}) collective-permute-start(bf16[192,128]{1,0:T(8,128)(2,1)S(1)} %get-tuple-element.34), channel_id=1, source_target_pairs={{0,4},{2,6},{4,0},{6,2},{1,5},{3,7},{5,1},{7,3},{8,12},{10,14},{12... | collective-permute-start | bytes 147464 | tf_op jit(solution)/shard_map/ppermute | solution.py:668
  51.2 1.3 %collective-permute-start.10 = (bf16[192,128]{1,0:T(8,128)(2,1)S(1)}, bf16[192,128]{1,0:T(8,128)(2,1)S(1)}, u32[]{:S(2)}, u32[]{:S(2)}) collective-permute-start(bf16[192,128]{1,0:T(8,128)(2,1)S(1)} %get-tuple-element.35), channel_id=1, source_target_pairs={{0,6},{2,4},{4,2},{6,0},{1,7},{3,5},{5,3},{7,1},{8,14},{10,12},{12... | collective-permute-start | bytes 147464 | tf_op jit(solution)/shard_map/ppermute | solution.py:668
  53.0 0.7 %collective-permute-start.16 = (bf16[64,640]{1,0:T(8,128)(2,1)S(1)}, bf16[64,640]{1,0:T(8,128)(2,1)S(1)}, u32[]{:S(2)}, u32[]{:S(2)}) collective-permute-start(bf16[64,640]{1,0:T(8,128)(2,1)S(1)} %shard_map.96), channel_id=1, source_target_pairs={{0,1},{1,0},{2,3},{3,2},{4,5},{5,4},{6,7},{7,6},{8,9},{9,8},{10,11... | collective-permute-start | bytes 245768 | tf_op jit(solution)/shard_map/ppermute | solution.py:671
  53.7 1.5 %collective-permute-start.8 = (bf16[192,128]{1,0:T(8,128)(2,1)S(1)}, bf16[192,128]{1,0:T(8,128)(2,1)S(1)}, u32[]{:S(2)}, u32[]{:S(2)}) collective-permute-start(bf16[192,128]{1,0:T(8,128)(2,1)S(1)} %get-tuple-element.32), channel_id=1, source_target_pairs={{0,2},{2,0},{4,6},{6,4},{1,3},{3,1},{5,7},{7,5},{8,10},{10,8},{12,... | collective-permute-start | bytes 147464 | tf_op jit(solution)/shard_map/ppermute | solution.py:668
  55.2 1.9 %collective-permute-done.10.refs_2_.refs_7_ = bf16[192,128]{1,0:T(8,128)(2,1)S(1)} collective-permute-done((bf16[192,128]{1,0:T(8,128)(2,1)S(1)}, bf16[192,128]{1,0:T(8,128)(2,1)S(1)}, u32[]{:S(2)}, u32[]{:S(2)}) %collective-permute-start.10) | collective-permute-done | bytes 49184 | tf_op jit(solution)/shard_map/ppermute | solution.py:668
  57.1 0.9 %shard_map.93.refs_1_ = f32[64,2560]{1,0:T(8,128)S(1)} custom-call(bf16[1280,2560]{1,0:T(8,128)(2,1)S(1)} %shard_map.86.w_ref, bf16[192,128]{1,0:T(8,128)(2,1)S(1)} %get-tuple-element.33.refs_0_.refs_4_, bf16[192,128]{1,0:T(8,128)(2,1)S(1)} %collective-permute-done.9.refs_1_.refs_6_, bf16[192,128]{1,0:T(8,128)(2,1)S(1)} %collective-permute-done.10.refs_2_.refs_7_), custom_call_target="tpu_custom_call" | custom-call | flops 314572800 | bytes 4915200 | tf_op jit(solution)/shard_map/pallas_call | solution.py:477
  58.8 1.2 %shard_map.100 = (f32[32,128]{1,0:T(8,128)}, f32[32,128]{1,0:T(8,128)S(1)}) custom-call(f32[64,2560]{1,0:T(8,128)S(1)} %shard_map.94.near_ref, bf16[64,640]{1,0:T(8,128)(2,1)S(1)} %collective-permute-done.16.refs_0_, bf16[64,1920]{1,0:T(8,128)(2,1)S(1)} %collective-permute-done.17.refs_1_, f32[4,1,1920]{2,1,0:T(1,128)S(1)} %get-tuple-element.42.refs_2_, ...), custom_call_target="tpu_custom_call" | custom-call | flops 20971520 | bytes 1310720 | tf_op jit(solution)/shard_map/pallas_call | solution.py:546
  60.0 1.2 %collective-permute-done.19 = f32[32,128]{1,0:T(8,128)S(1)} collective-permute-done((f32[32,128]{1,0:T(8,128)S(1)}, f32[32,128]{1,0:T(8,128)S(1)}, u32[]{:S(2)}, u32[]{:S(2)}) %collective-permute-start.19) | collective-permute-done | bytes 16416 | tf_op jit(solution)/shard_map/ppermute | solution.py:27
  61.2 0.6 copy.10
  (34 shorter events, 2.4 us)
Async XLA Ops:
  0.6 26.6 %copy-start = (bf16[1,256,960]{1,2,0:T(8,128)(2,1)S(1)}, bf16[1,256,960]{1,2,0:T(8,128)(2,1)}, u32[]{:S(2)}) copy-start(bf16[1,256,960]{1,2,0:T(8,128)(2,1)} %param.10) | copy-start | bytes 1474564
  0.6 11.4 %collective-permute-start = (s32[1,1,2]{2,1,0:T(1,128)}, s32[1,1,2]{2,1,0:T(1,128)S(1)}, u32[]{:S(2)}, u32[]{:S(2)}) collective-permute-start(s32[1,1,2]{2,1,0:T(1,128)} %param.13), channel_id=1, source_target_pairs={{0,1},{1,0},{2,3},{3,2},{4,5},{5,4},{6,7},{7,6},{8,9},{9,8},{10,11... | collective-permute-start | bytes 32 | tf_op jit(solution)/shard_map/ppermute | solution.py:671
  4.7 13.9 %collective-permute-start.2 = (bf16[576,128]{1,0:T(8,128)(2,1)S(1)}, bf16[576,128]{1,0:T(8,128)(2,1)S(1)}, u32[]{:S(2)}, u32[]{:S(2)}) collective-permute-start(bf16[576,128]{1,0:T(8,128)(2,1)S(1)} %get-tuple-element.27), channel_id=1, source_target_pairs={{0,5},{1,4},{2,7},{3,6},{4,1},{5,0},{6,3},{7,2},{8,13},{9,12},{10,... | collective-permute-start | bytes 442376 | tf_op jit(solution)/shard_map/ppermute | solution.py:678
  8.7 12.7 %collective-permute-start.11 = (bf16[480,128]{1,0:T(8,128)(2,1)S(1)}, bf16[480,128]{1,0:T(8,128)(2,1)S(1)}, u32[]{:S(2)}, u32[]{:S(2)}) collective-permute-start(bf16[480,128]{1,0:T(8,128)(2,1)S(1)} %get-tuple-element.36), channel_id=1, source_target_pairs={{0,1},{1,0},{2,3},{3,2},{4,5},{5,4},{6,7},{7,6},{8,9},{9,8},{10,11... | collective-permute-start | bytes 368648 | tf_op jit(solution)/shard_map/ppermute | solution.py:678
  10.2 11.2 %collective-permute-start.12 = (bf16[480,128]{1,0:T(8,128)(2,1)S(1)}, bf16[480,128]{1,0:T(8,128)(2,1)S(1)}, u32[]{:S(2)}, u32[]{:S(2)}) collective-permute-start(bf16[480,128]{1,0:T(8,128)(2,1)S(1)} %get-tuple-element.37), channel_id=1, source_target_pairs={{0,7},{1,6},{2,5},{3,4},{4,3},{5,2},{6,1},{7,0},{8,15},{9,14},{10,... | collective-permute-start | bytes 368648 | tf_op jit(solution)/shard_map/ppermute | solution.py:678
  11.5 9.8 %collective-permute-start.1 = (bf16[576,128]{1,0:T(8,128)(2,1)S(1)}, bf16[576,128]{1,0:T(8,128)(2,1)S(1)}, u32[]{:S(2)}, u32[]{:S(2)}) collective-permute-start(bf16[576,128]{1,0:T(8,128)(2,1)S(1)} %get-tuple-element.26), channel_id=1, source_target_pairs={{0,3},{1,2},{2,1},{3,0},{4,7},{5,6},{6,5},{7,4},{8,11},{9,10},{10,... | collective-permute-start | bytes 442376 | tf_op jit(solution)/shard_map/ppermute | solution.py:678
  18.6 8.9 %collective-permute-start.3 = (bf16[96,128]{1,0:T(8,128)(2,1)S(1)}, bf16[96,128]{1,0:T(8,128)(2,1)S(1)}, u32[]{:S(2)}, u32[]{:S(2)}) collective-permute-start(bf16[96,128]{1,0:T(8,128)(2,1)S(1)} %shard_map.89), channel_id=1, source_target_pairs={{0,2},{2,0},{4,6},{6,4},{1,3},{3,1},{5,7},{7,5},{8,10},{10,8},{12,... | collective-permute-start | bytes 73736 | tf_op jit(solution)/shard_map/ppermute | solution.py:668
  22.7 9.0 %collective-permute-start.13 = (bf16[160,128]{1,0:T(8,128)(2,1)S(1)}, bf16[160,128]{1,0:T(8,128)(2,1)S(1)}, u32[]{:S(2)}, u32[]{:S(2)}) collective-permute-start(bf16[160,128]{1,0:T(8,128)(2,1)S(1)} %get-tuple-element.39), channel_id=1, source_target_pairs={{0,2},{2,0},{4,6},{6,4},{1,3},{3,1},{5,7},{7,5},{8,10},{10,8},{12,... | collective-permute-start | bytes 122888 | tf_op jit(solution)/shard_map/ppermute | solution.py:668
  23.5 8.3 %collective-permute-start.14 = (bf16[160,128]{1,0:T(8,128)(2,1)S(1)}, bf16[160,128]{1,0:T(8,128)(2,1)S(1)}, u32[]{:S(2)}, u32[]{:S(2)}) collective-permute-start(bf16[160,128]{1,0:T(8,128)(2,1)S(1)} %get-tuple-element.40), channel_id=1, source_target_pairs={{0,4},{2,6},{4,0},{6,2},{1,5},{3,7},{5,1},{7,3},{8,12},{10,14},{12... | collective-permute-start | bytes 122888 | tf_op jit(solution)/shard_map/ppermute | solution.py:668
  26.4 5.8 %collective-permute-start.15 = (bf16[160,128]{1,0:T(8,128)(2,1)S(1)}, bf16[160,128]{1,0:T(8,128)(2,1)S(1)}, u32[]{:S(2)}, u32[]{:S(2)}) collective-permute-start(bf16[160,128]{1,0:T(8,128)(2,1)S(1)} %get-tuple-element.41), channel_id=1, source_target_pairs={{0,6},{2,4},{4,2},{6,0},{1,7},{3,5},{5,3},{7,1},{8,14},{10,12},{12... | collective-permute-start | bytes 122888 | tf_op jit(solution)/shard_map/ppermute | solution.py:668
  27.5 12.5 %collective-permute-start.4 = (bf16[400,128]{1,0:T(8,128)(2,1)S(1)}, bf16[400,128]{1,0:T(8,128)(2,1)S(1)}, u32[]{:S(2)}, u32[]{:S(2)}) collective-permute-start(bf16[400,128]{1,0:T(8,128)(2,1)S(1)} %shard_map.90.refs_0_), channel_id=1, source_target_pairs={{0,1},{1,0},{2,3},{3,2},{4,5},{5,4},{6,7},{7,6},{8,9},{9,8},{10,11... | collective-permute-start | bytes 307208 | tf_op jit(solution)/shard_map/ppermute | solution.py:671
  33.1 25.6 %collective-permute-start.17 = (bf16[64,1920]{1,0:T(8,128)(2,1)S(1)}, bf16[64,1920]{1,0:T(8,128)(2,1)S(1)}, u32[]{:S(2)}, u32[]{:S(2)}) collective-permute-start(bf16[64,1920]{1,0:T(8,128)(2,1)S(1)} %shard_map.97), channel_id=1, source_target_pairs={{0,1},{1,0},{2,3},{3,2},{4,5},{5,4},{6,7},{7,6},{8,9},{9,8},{10,11... | collective-permute-start | bytes 737288 | tf_op jit(solution)/shard_map/ppermute | solution.py:671
  35.5 6.1 %collective-permute-start.5 = (bf16[480,128]{1,0:T(8,128)(2,1)S(1)}, bf16[480,128]{1,0:T(8,128)(2,1)S(1)}, u32[]{:S(2)}, u32[]{:S(2)}) collective-permute-start(bf16[480,128]{1,0:T(8,128)(2,1)S(1)} %get-tuple-element.29), channel_id=1, source_target_pairs={{0,2},{2,0},{4,6},{6,4},{1,3},{3,1},{5,7},{7,5},{8,10},{10,8},{12,... | collective-permute-start | bytes 368648 | tf_op jit(solution)/shard_map/ppermute | solution.py:668
  35.6 11.3 %collective-permute-start.6 = (bf16[480,128]{1,0:T(8,128)(2,1)S(1)}, bf16[480,128]{1,0:T(8,128)(2,1)S(1)}, u32[]{:S(2)}, u32[]{:S(2)}) collective-permute-start(bf16[480,128]{1,0:T(8,128)(2,1)S(1)} %get-tuple-element.30), channel_id=1, source_target_pairs={{0,4},{2,6},{4,0},{6,2},{1,5},{3,7},{5,1},{7,3},{8,12},{10,14},{12... | collective-permute-start | bytes 368648 | tf_op jit(solution)/shard_map/ppermute | solution.py:668
  38.6 8.3 %collective-permute-start.7 = (bf16[480,128]{1,0:T(8,128)(2,1)S(1)}, bf16[480,128]{1,0:T(8,128)(2,1)S(1)}, u32[]{:S(2)}, u32[]{:S(2)}) collective-permute-start(bf16[480,128]{1,0:T(8,128)(2,1)S(1)} %get-tuple-element.31), channel_id=1, source_target_pairs={{0,6},{2,4},{4,2},{6,0},{1,7},{3,5},{5,3},{7,1},{8,14},{10,12},{12... | collective-permute-start | bytes 368648 | tf_op jit(solution)/shard_map/ppermute | solution.py:668
  40.0 18.6 %collective-permute-start.18 = (bf16[768,128]{1,0:T(8,128)(2,1)S(1)}, bf16[768,128]{1,0:T(8,128)(2,1)S(1)}, u32[]{:S(2)}, u32[]{:S(2)}) collective-permute-start(bf16[768,128]{1,0:T(8,128)(2,1)S(1)} %shard_map.98.refs_0_), channel_id=1, source_target_pairs={{0,16},{16,0},{1,17},{17,1},{2,18},{18,2},{3,19},{19,3},{4,20},{20... | collective-permute-start | bytes 589832 | tf_op jit(solution)/shard_map/ppermute | solution.py:671
  48.2 5.5 %collective-permute-start.9 = (bf16[192,128]{1,0:T(8,128)(2,1)S(1)}, bf16[192,128]{1,0:T(8,128)(2,1)S(1)}, u32[]{:S(2)}, u32[]{:S(2)}) collective-permute-start(bf16[192,128]{1,0:T(8,128)(2,1)S(1)} %get-tuple-element.34), channel_id=1, source_target_pairs={{0,4},{2,6},{4,0},{6,2},{1,5},{3,7},{5,1},{7,3},{8,12},{10,14},{12... | collective-permute-start | bytes 147464 | tf_op jit(solution)/shard_map/ppermute | solution.py:668
  51.2 5.9 %collective-permute-start.10 = (bf16[192,128]{1,0:T(8,128)(2,1)S(1)}, bf16[192,128]{1,0:T(8,128)(2,1)S(1)}, u32[]{:S(2)}, u32[]{:S(2)}) collective-permute-start(bf16[192,128]{1,0:T(8,128)(2,1)S(1)} %get-tuple-element.35), channel_id=1, source_target_pairs={{0,6},{2,4},{4,2},{6,0},{1,7},{3,5},{5,3},{7,1},{8,14},{10,12},{12... | collective-permute-start | bytes 147464 | tf_op jit(solution)/shard_map/ppermute | solution.py:668
  53.0 5.7 %collective-permute-start.16 = (bf16[64,640]{1,0:T(8,128)(2,1)S(1)}, bf16[64,640]{1,0:T(8,128)(2,1)S(1)}, u32[]{:S(2)}, u32[]{:S(2)}) collective-permute-start(bf16[64,640]{1,0:T(8,128)(2,1)S(1)} %shard_map.96), channel_id=1, source_target_pairs={{0,1},{1,0},{2,3},{3,2},{4,5},{5,4},{6,7},{7,6},{8,9},{9,8},{10,11... | collective-permute-start | bytes 245768 | tf_op jit(solution)/shard_map/ppermute | solution.py:671
  53.7 4.4 %collective-permute-start.8 = (bf16[192,128]{1,0:T(8,128)(2,1)S(1)}, bf16[192,128]{1,0:T(8,128)(2,1)S(1)}, u32[]{:S(2)}, u32[]{:S(2)}) collective-permute-start(bf16[192,128]{1,0:T(8,128)(2,1)S(1)} %get-tuple-element.32), channel_id=1, source_target_pairs={{0,2},{2,0},{4,6},{6,4},{1,3},{3,1},{5,7},{7,5},{8,10},{10,8},{12,... | collective-permute-start | bytes 147464 | tf_op jit(solution)/shard_map/ppermute | solution.py:668
  57.1 1.6 %copy-start.1 = (bf16[1,1,64,2560]{3,2,1,0:T(8,128)(2,1)S(1)}, bf16[1,1,64,2560]{3,2,1,0:T(8,128)(2,1)}, u32[]{:S(2)}) copy-start(bf16[1,1,64,2560]{3,2,1,0:T(8,128)(2,1)} %param.8) | copy-start | bytes 983044
  57.1 1.7 %copy-start.2 = (f32[1,1,32,128]{3,2,1,0:T(8,128)S(1)}, f32[1,1,32,128]{3,2,1,0:T(8,128)}, u32[]{:S(2)}) copy-start(f32[1,1,32,128]{3,2,1,0:T(8,128)} %param.12) | copy-start | bytes 49156
  60.0 1.2 %collective-permute-start.19 = (f32[32,128]{1,0:T(8,128)S(1)}, f32[32,128]{1,0:T(8,128)S(1)}, u32[]{:S(2)}, u32[]{:S(2)}) collective-permute-start(f32[32,128]{1,0:T(8,128)S(1)} %get-tuple-element.45), channel_id=1, source_target_pairs={{0,8},{8,0},{1,9},{9,1},{2,10},{10,2},{3,11},{11,3},{4,12},{12,4},... | collective-permute-start | bytes 49160 | tf_op jit(solution)/shard_map/ppermute | solution.py:27
